TPU v7x, 32 devices: a whole 2x2x4 slice. The times are simulated.
32 devices in a mesh: seq: 2 (over y), fsdp: 16 (over z, x, core).
Axes of the slice: x: 2, y: 2, z: 4, core: 2. Of those that a mesh axis runs over, the one named last changes fastest.
Arguments:
- tokens: bfloat16 [16, 1024, 768], P('fsdp', 'seq'), may hold values from -6 to 6
- doc_lengths: int32 [16, 16], P('fsdp'), may hold values from 1 to 256, 1024 in all within a row
- feature_ints: int32 [12, 64, 256], replicated, may hold values from -128 to 127
- w_query: bfloat16 [768, 768], P('fsdp'), may hold values from -0.21875 to 0.21875
- b_query: bfloat16 [768], P('fsdp'), may hold values from -1.75 to 1.75
- w_key: bfloat16 [768, 768], P('fsdp'), may hold values from -0.21875 to 0.21875
- b_key: bfloat16 [768], P('fsdp'), may hold values from -1.75 to 1.75
- w_value: bfloat16 [768, 768], P('fsdp'), may hold values from -0.21875 to 0.21875
- b_value: bfloat16 [768], P('fsdp'), may hold values from -3 to 3
- w_out: bfloat16 [768, 768], P('fsdp'), may hold values from -1.25 to 1.25
- b_out: bfloat16 [768], P('fsdp'), may hold values from -3 to 3
- norm1_gain: bfloat16 [768], P('fsdp'), may hold values from 0.25 to 1.75
- norm1_bias: bfloat16 [768], P('fsdp'), may hold values from -3 to 3
- w_in: bfloat16 [768, 3072], P('fsdp'), may hold values from -0.21875 to 0.21875
- b_in: bfloat16 [3072], P('fsdp'), may hold values from -3 to 3
- w_down: bfloat16 [3072, 768], P('fsdp'), may hold values from -0.109375 to 0.109375
- b_down: bfloat16 [768], P('fsdp'), may hold values from -3 to 3
- norm2_gain: bfloat16 [768], P('fsdp'), may hold values from 0.25 to 1.75
- norm2_bias: bfloat16 [768], P('fsdp'), may hold values from -3 to 3
- cotangent: bfloat16 [16, 1024, 768], P('fsdp', 'seq'), may hold values from -6 to 6
Outputs:
- layer_out: bfloat16 [16, 1024, 768], P('fsdp', 'seq')
- grad_tokens: float32 [16, 1024, 768], P('fsdp', 'seq')
- grad_w_query: float32 [768, 768], P('fsdp')
- grad_b_query: float32 [768], P('fsdp')
- grad_w_key: float32 [768, 768], P('fsdp')
- grad_b_key: float32 [768], P('fsdp')
- grad_w_value: float32 [768, 768], P('fsdp')
- grad_b_value: float32 [768], P('fsdp')
- grad_w_out: float32 [768, 768], P('fsdp')
- grad_b_out: float32 [768], P('fsdp')
- grad_norm1_gain: float32 [768], P('fsdp')
- grad_norm1_bias: float32 [768], P('fsdp')
- grad_w_in: float32 [768, 3072], P('fsdp')
- grad_b_in: float32 [3072], P('fsdp')
- grad_w_down: float32 [3072, 768], P('fsdp')
- grad_b_down: float32 [768], P('fsdp')
- grad_norm2_gain: float32 [768], P('fsdp')
- grad_norm2_bias: float32 [768], P('fsdp')
Inputs may be any that keep to these rules, and one draw needn't show every extreme that they name: `doc_lengths`: each row lists the document lengths of one stream in order and sums to 1024; the longest document of every row has exactly 256 tokens.
All inputs are finite; a program needn't handle non-finite values.
Results may differ from a plain program's by a relative error of at most 0.03.
Values may be sent and summed in bfloat16 or wider, within the bound.
A program may use at most 128 MiB of HBM per device.

v0:
```python
from functools import partial

import jax
import jax.numpy as jnp
from jax import lax
from jax.sharding import PartitionSpec as P

unit_spread = 0.013531646934131853
inv_root_two = 0.7071067811865476
inv_root_tau = 0.3989422804014327
far_below = -1e30


def layer_norm(residual, norm_gain, norm_bias):
    centred = residual - jnp.mean(residual, axis=1, keepdims=True)
    inverse = lax.rsqrt(jnp.mean(centred * centred, axis=1, keepdims=True) + 1e-06)
    normed = centred * inverse
    return (normed * norm_gain.astype(jnp.float32) + norm_bias.astype(jnp.float32), normed, inverse)


def norm_back(grad_out, normed, inverse, norm_gain):
    scaled = grad_out * norm_gain.astype(jnp.float32)
    centre_part = jnp.mean(scaled, axis=1, keepdims=True)
    slope_part = jnp.mean(scaled * normed, axis=1, keepdims=True)
    grad_resid = inverse * (scaled - centre_part - normed * slope_part)
    return (grad_resid, jnp.sum(grad_out * normed, axis=0), jnp.sum(grad_out, axis=0))


def gelu_value(pre_act):
    return 0.5 * pre_act * (1.0 + lax.erf(pre_act * inv_root_two))


def gelu_slope(pre_act):
    return (
        0.5 * (1.0 + lax.erf(pre_act * inv_root_two))
        + pre_act * jnp.exp(-0.5 * pre_act * pre_act) * inv_root_tau
    )


def affine(row_block, weight, bias_row):
    return jnp.dot(row_block, weight, preferred_element_type=jnp.float32) + bias_row.astype(
        jnp.float32
    )


def left_product(first_op, second):
    return lax.dot_general(
        first_op, second, (((0,), (0,)), ((), ())), preferred_element_type=jnp.float32
    )


def right_product(first_op, second):
    return lax.dot_general(
        first_op, second, (((1,), (1,)), ((), ())), preferred_element_type=jnp.float32
    )


def column_total(values):
    return jnp.sum(values, axis=0, dtype=jnp.float32)


def head_logits(rows_low, feature_block):
    head_size = rows_low.shape[1]
    raw_part = jnp.dot(rows_low, feature_block, preferred_element_type=jnp.float32) * (
        head_size ** (-0.25) * unit_spread
    )
    rows_wide = rows_low.astype(jnp.float32)
    half_norm = jnp.sum(rows_wide * rows_wide, axis=1, keepdims=True) * (0.5 * head_size ** (-0.5))
    return (raw_part - half_norm, rows_wide)


def logit_back(grad_logit, rows_wide, feature_block):
    head_size = rows_wide.shape[1]
    through = right_product(grad_logit.astype(jnp.bfloat16), feature_block) * (
        head_size ** (-0.25) * unit_spread
    )
    return through - jnp.sum(grad_logit, axis=1, keepdims=True) * rows_wide * head_size ** (-0.5)


def spread_rows(doc_mask, row_values):
    spread = jnp.where(
        doc_mask[:, :, None], row_values[:, None, :], jnp.zeros((), row_values.dtype)
    )
    return spread.reshape(row_values.shape[0], -1)


def pick_rows(doc_mask, wide_values):
    split_parts = wide_values.reshape(wide_values.shape[0], doc_mask.shape[1], -1)
    return jnp.sum(jnp.where(doc_mask[:, :, None], split_parts, 0.0), axis=1)


def head_forward(packed, doc_mask):
    query_h, key_h, value_h, feature_block = packed
    q_logit = head_logits(query_h, feature_block)[0]
    k_logit = head_logits(key_h, feature_block)[0]
    q_shift = jnp.max(q_logit, axis=1, keepdims=True)
    doc_peak = jnp.max(
        jnp.where(doc_mask, jnp.max(k_logit, axis=1, keepdims=True), far_below), axis=0
    )
    k_shift = jnp.max(jnp.where(doc_mask, doc_peak[None, :], far_below), axis=1, keepdims=True)
    phi_query = jnp.exp(q_logit - q_shift).astype(jnp.bfloat16)
    phi_key = jnp.exp(k_logit - k_shift).astype(jnp.bfloat16)
    mask_low = doc_mask.astype(jnp.bfloat16)
    kv_low = left_product(spread_rows(doc_mask, value_h), phi_key).astype(jnp.bfloat16)
    totals_low = left_product(mask_low, phi_key).astype(jnp.bfloat16)
    numerator = pick_rows(doc_mask, right_product(phi_query, kv_low))
    denominator = jnp.sum(jnp.where(doc_mask, right_product(phi_query, totals_low), 0.0), axis=1)
    attended = (numerator / denominator[:, None]).astype(jnp.bfloat16)
    return (attended, kv_low, totals_low, numerator, denominator, q_shift, k_shift)


def head_backward(packed, doc_mask):
    (
        query_h,
        key_h,
        value_h,
        feature_block,
        kv_low,
        totals_low,
        numerator,
        denominator,
        q_shift,
        k_shift,
        grad_att,
    ) = packed
    q_logit, query_wide = head_logits(query_h, feature_block)
    k_logit, key_wide = head_logits(key_h, feature_block)
    q_exp = jnp.exp(q_logit - q_shift)
    k_exp = jnp.exp(k_logit - k_shift)
    phi_query = q_exp.astype(jnp.bfloat16)
    phi_key = k_exp.astype(jnp.bfloat16)
    grad_wide = grad_att.astype(jnp.float32)
    grad_numer = (grad_wide / denominator[:, None]).astype(jnp.bfloat16)
    grad_denom = (-jnp.sum(grad_wide * numerator, axis=1) / (denominator * denominator)).astype(
        jnp.bfloat16
    )
    mask_low = doc_mask.astype(jnp.bfloat16)
    denom_spread = mask_low * grad_denom[:, None]
    numer_spread = spread_rows(doc_mask, grad_numer)
    grad_phi_q = jnp.dot(numer_spread, kv_low, preferred_element_type=jnp.float32) + jnp.dot(
        denom_spread, totals_low, preferred_element_type=jnp.float32
    )
    grad_kv = left_product(numer_spread, phi_query).astype(jnp.bfloat16)
    grad_totals = left_product(denom_spread, phi_query).astype(jnp.bfloat16)
    grad_phi_k = jnp.dot(
        spread_rows(doc_mask, value_h), grad_kv, preferred_element_type=jnp.float32
    ) + jnp.dot(mask_low, grad_totals, preferred_element_type=jnp.float32)
    grad_value = pick_rows(doc_mask, right_product(phi_key, grad_kv))
    grad_query = logit_back(grad_phi_q * q_exp, query_wide, feature_block)
    grad_key = logit_back(grad_phi_k * k_exp, key_wide, feature_block)
    return (
        grad_query.astype(jnp.bfloat16),
        grad_key.astype(jnp.bfloat16),
        grad_value.astype(jnp.bfloat16),
    )


def to_heads(seq_rows, heads_here):
    return seq_rows.reshape(seq_rows.shape[0], heads_here, -1).transpose(1, 0, 2)


def to_rows(head_rows):
    return head_rows.transpose(1, 0, 2).reshape(head_rows.shape[1], -1)


def per_device(
    tokens,
    doc_lengths,
    feature_ints,
    w_query,
    b_query,
    w_key,
    b_key,
    w_value,
    b_value,
    w_out,
    b_out,
    norm1_gain,
    norm1_bias,
    w_in,
    b_in,
    w_down,
    b_down,
    norm2_gain,
    norm2_bias,
    cotangent,
):
    (
        query_weight,
        query_bias,
        key_weight,
        key_bias,
        value_weight,
        value_bias,
        out_weight,
        out_bias,
        gain_one,
        offset_one,
    ) = (
        lax.all_gather(w_query, "fsdp", axis=0, tiled=True),
        lax.all_gather(b_query, "fsdp", axis=0, tiled=True),
        lax.all_gather(w_key, "fsdp", axis=0, tiled=True),
        lax.all_gather(b_key, "fsdp", axis=0, tiled=True),
        lax.all_gather(w_value, "fsdp", axis=0, tiled=True),
        lax.all_gather(b_value, "fsdp", axis=0, tiled=True),
        lax.all_gather(w_out, "fsdp", axis=0, tiled=True),
        lax.all_gather(b_out, "fsdp", axis=0, tiled=True),
        lax.all_gather(norm1_gain, "fsdp", axis=0, tiled=True),
        lax.all_gather(norm1_bias, "fsdp", axis=0, tiled=True),
    )
    row_block = tokens[0]
    seq_count = lax.axis_size("seq")
    heads_here = feature_ints.shape[0] // seq_count
    stream_len = row_block.shape[0] * seq_count
    query_rows = affine(row_block, query_weight, query_bias).astype(jnp.bfloat16)
    key_rows = affine(row_block, key_weight, key_bias).astype(jnp.bfloat16)
    value_rows = affine(row_block, value_weight, value_bias).astype(jnp.bfloat16)
    query_seq, key_seq, value_seq = (
        lax.all_to_all(query_rows, "seq", split_axis=1, concat_axis=0, tiled=True),
        lax.all_to_all(key_rows, "seq", split_axis=1, concat_axis=0, tiled=True),
        lax.all_to_all(value_rows, "seq", split_axis=1, concat_axis=0, tiled=True),
    )
    feature_block = lax.dynamic_slice_in_dim(
        feature_ints, lax.axis_index("seq") * heads_here, heads_here, 0
    ).astype(jnp.bfloat16)
    doc_ends = jnp.cumsum(doc_lengths[0])
    doc_starts = doc_ends - doc_lengths[0]
    position = lax.broadcasted_iota(jnp.int32, (stream_len, 1), 0)
    doc_mask = jnp.logical_and(position >= doc_starts[None, :], position < doc_ends[None, :])
    query_heads = to_heads(query_seq, heads_here)
    key_heads = to_heads(key_seq, heads_here)
    value_heads = to_heads(value_seq, heads_here)
    attended, kv_low, totals_low, numerator, denominator, q_shift, k_shift = lax.map(
        partial(head_forward, doc_mask=doc_mask),
        (query_heads, key_heads, value_heads, feature_block),
    )
    att_rows = lax.all_to_all(to_rows(attended), "seq", split_axis=0, concat_axis=1, tiled=True)
    residual_one = row_block.astype(jnp.float32) + affine(att_rows, out_weight, out_bias)
    hidden_wide, normed_one, inverse_one = layer_norm(residual_one, gain_one, offset_one)
    hidden_low = hidden_wide.astype(jnp.bfloat16)
    in_weight, in_bias, down_weight, down_bias, gain_two, offset_two = (
        lax.all_gather(w_in, "fsdp", axis=0, tiled=True),
        lax.all_gather(b_in, "fsdp", axis=0, tiled=True),
        lax.all_gather(w_down, "fsdp", axis=0, tiled=True),
        lax.all_gather(b_down, "fsdp", axis=0, tiled=True),
        lax.all_gather(norm2_gain, "fsdp", axis=0, tiled=True),
        lax.all_gather(norm2_bias, "fsdp", axis=0, tiled=True),
    )
    pre_act = affine(hidden_low, in_weight, in_bias)
    gelu_low = gelu_value(pre_act).astype(jnp.bfloat16)
    residual_two = hidden_low.astype(jnp.float32) + affine(gelu_low, down_weight, down_bias)
    layer_wide, normed_two, inverse_two = layer_norm(residual_two, gain_two, offset_two)
    in_weight, in_bias, down_weight, down_bias, gain_two, offset_two = (
        lax.all_gather(w_in, "fsdp", axis=0, tiled=True),
        lax.all_gather(b_in, "fsdp", axis=0, tiled=True),
        lax.all_gather(w_down, "fsdp", axis=0, tiled=True),
        lax.all_gather(b_down, "fsdp", axis=0, tiled=True),
        lax.all_gather(norm2_gain, "fsdp", axis=0, tiled=True),
        lax.all_gather(norm2_bias, "fsdp", axis=0, tiled=True),
    )
    grad_out = cotangent[0].astype(jnp.float32)
    grad_resid_two, grad_gain_two, grad_offset_two = norm_back(
        grad_out, normed_two, inverse_two, gain_two
    )
    grad_down_low = grad_resid_two.astype(jnp.bfloat16)
    grad_down_weight = left_product(gelu_low, grad_down_low)
    grad_down_bias = column_total(grad_down_low)
    grad_pre_low = (right_product(grad_down_low, down_weight) * gelu_slope(pre_act)).astype(
        jnp.bfloat16
    )
    grad_in_weight = left_product(hidden_low, grad_pre_low)
    grad_in_bias = column_total(grad_pre_low)
    grad_hidden = right_product(grad_pre_low, in_weight) + grad_resid_two
    (
        query_weight,
        query_bias,
        key_weight,
        key_bias,
        value_weight,
        value_bias,
        out_weight,
        out_bias,
        gain_one,
        offset_one,
    ) = (
        lax.all_gather(w_query, "fsdp", axis=0, tiled=True),
        lax.all_gather(b_query, "fsdp", axis=0, tiled=True),
        lax.all_gather(w_key, "fsdp", axis=0, tiled=True),
        lax.all_gather(b_key, "fsdp", axis=0, tiled=True),
        lax.all_gather(w_value, "fsdp", axis=0, tiled=True),
        lax.all_gather(b_value, "fsdp", axis=0, tiled=True),
        lax.all_gather(w_out, "fsdp", axis=0, tiled=True),
        lax.all_gather(b_out, "fsdp", axis=0, tiled=True),
        lax.all_gather(norm1_gain, "fsdp", axis=0, tiled=True),
        lax.all_gather(norm1_bias, "fsdp", axis=0, tiled=True),
    )
    grad_resid_one, grad_gain_one, grad_offset_one = norm_back(
        grad_hidden, normed_one, inverse_one, gain_one
    )
    ffn_shards = (
        lax.psum_scatter(grad_in_weight, "fsdp", scatter_dimension=0, tiled=True),
        lax.psum_scatter(grad_in_bias, "fsdp", scatter_dimension=0, tiled=True),
        lax.psum_scatter(grad_down_weight, "fsdp", scatter_dimension=0, tiled=True),
        lax.psum_scatter(grad_down_bias, "fsdp", scatter_dimension=0, tiled=True),
        lax.psum_scatter(grad_gain_two, "fsdp", scatter_dimension=0, tiled=True),
        lax.psum_scatter(grad_offset_two, "fsdp", scatter_dimension=0, tiled=True),
        lax.psum_scatter(grad_gain_one, "fsdp", scatter_dimension=0, tiled=True),
        lax.psum_scatter(grad_offset_one, "fsdp", scatter_dimension=0, tiled=True),
    )
    ffn_owned = (
        lax.psum(ffn_shards[0].astype(jnp.bfloat16), "seq").astype(jnp.float32),
        lax.psum(ffn_shards[1].astype(jnp.bfloat16), "seq").astype(jnp.float32),
        lax.psum(ffn_shards[2].astype(jnp.bfloat16), "seq").astype(jnp.float32),
        lax.psum(ffn_shards[3].astype(jnp.bfloat16), "seq").astype(jnp.float32),
        lax.psum(ffn_shards[4].astype(jnp.bfloat16), "seq").astype(jnp.float32),
        lax.psum(ffn_shards[5].astype(jnp.bfloat16), "seq").astype(jnp.float32),
        lax.psum(ffn_shards[6].astype(jnp.bfloat16), "seq").astype(jnp.float32),
        lax.psum(ffn_shards[7].astype(jnp.bfloat16), "seq").astype(jnp.float32),
    )
    grad_proj_low = grad_resid_one.astype(jnp.bfloat16)
    grad_out_weight = left_product(att_rows, grad_proj_low)
    grad_out_bias = column_total(grad_proj_low)
    grad_att_rows = right_product(grad_proj_low, out_weight).astype(jnp.bfloat16)
    grad_att_seq = lax.all_to_all(grad_att_rows, "seq", split_axis=1, concat_axis=0, tiled=True)
    head_grads = lax.map(
        partial(head_backward, doc_mask=doc_mask),
        (
            query_heads,
            key_heads,
            value_heads,
            feature_block,
            kv_low,
            totals_low,
            numerator,
            denominator,
            q_shift,
            k_shift,
            to_heads(grad_att_seq, heads_here),
        ),
    )
    grad_query_rows, grad_key_rows, grad_value_rows = (
        lax.all_to_all(to_rows(head_grads[0]), "seq", split_axis=0, concat_axis=1, tiled=True),
        lax.all_to_all(to_rows(head_grads[1]), "seq", split_axis=0, concat_axis=1, tiled=True),
        lax.all_to_all(to_rows(head_grads[2]), "seq", split_axis=0, concat_axis=1, tiled=True),
    )
    grad_query_weight = left_product(row_block, grad_query_rows)
    grad_key_weight = left_product(row_block, grad_key_rows)
    grad_value_weight = left_product(row_block, grad_value_rows)
    grad_input = (
        right_product(grad_query_rows, query_weight)
        + right_product(grad_key_rows, key_weight)
        + right_product(grad_value_rows, value_weight)
        + grad_resid_one
    )
    attn_shards = (
        lax.psum_scatter(grad_query_weight, "fsdp", scatter_dimension=0, tiled=True),
        lax.psum_scatter(column_total(grad_query_rows), "fsdp", scatter_dimension=0, tiled=True),
        lax.psum_scatter(grad_key_weight, "fsdp", scatter_dimension=0, tiled=True),
        lax.psum_scatter(column_total(grad_key_rows), "fsdp", scatter_dimension=0, tiled=True),
        lax.psum_scatter(grad_value_weight, "fsdp", scatter_dimension=0, tiled=True),
        lax.psum_scatter(column_total(grad_value_rows), "fsdp", scatter_dimension=0, tiled=True),
        lax.psum_scatter(grad_out_weight, "fsdp", scatter_dimension=0, tiled=True),
        lax.psum_scatter(grad_out_bias, "fsdp", scatter_dimension=0, tiled=True),
    )
    attn_owned = (
        lax.psum(attn_shards[0].astype(jnp.bfloat16), "seq").astype(jnp.float32),
        lax.psum(attn_shards[1].astype(jnp.bfloat16), "seq").astype(jnp.float32),
        lax.psum(attn_shards[2].astype(jnp.bfloat16), "seq").astype(jnp.float32),
        lax.psum(attn_shards[3].astype(jnp.bfloat16), "seq").astype(jnp.float32),
        lax.psum(attn_shards[4].astype(jnp.bfloat16), "seq").astype(jnp.float32),
        lax.psum(attn_shards[5].astype(jnp.bfloat16), "seq").astype(jnp.float32),
        lax.psum(attn_shards[6].astype(jnp.bfloat16), "seq").astype(jnp.float32),
        lax.psum(attn_shards[7].astype(jnp.bfloat16), "seq").astype(jnp.float32),
    )
    return (
        layer_wide.astype(jnp.bfloat16)[None],
        grad_input[None],
        attn_owned[0],
        attn_owned[1],
        attn_owned[2],
        attn_owned[3],
        attn_owned[4],
        attn_owned[5],
        attn_owned[6],
        attn_owned[7],
        ffn_owned[6],
        ffn_owned[7],
        ffn_owned[0],
        ffn_owned[1],
        ffn_owned[2],
        ffn_owned[3],
        ffn_owned[4],
        ffn_owned[5],
    )


def solution(mesh):
    placed = (
        P("fsdp", "seq", None),
        P("fsdp", None),
        P(),
        P("fsdp", None),
        P("fsdp"),
        P("fsdp", None),
        P("fsdp"),
        P("fsdp", None),
        P("fsdp"),
        P("fsdp", None),
        P("fsdp"),
        P("fsdp"),
        P("fsdp"),
        P("fsdp", None),
        P("fsdp"),
        P("fsdp", None),
        P("fsdp"),
        P("fsdp"),
        P("fsdp"),
        P("fsdp", "seq", None),
    )
    return jax.shard_map(
        per_device,
        mesh=mesh,
        in_specs=placed,
        out_specs=(
            P("fsdp", "seq", None),
            P("fsdp", "seq", None),
            P("fsdp", None),
            P("fsdp"),
            P("fsdp", None),
            P("fsdp"),
            P("fsdp", None),
            P("fsdp"),
            P("fsdp", None),
            P("fsdp"),
            P("fsdp"),
            P("fsdp"),
            P("fsdp", None),
            P("fsdp"),
            P("fsdp", None),
            P("fsdp"),
            P("fsdp"),
            P("fsdp"),
        ),
        check_vma=False,
    )
```

profile of v0, /device:TPU:0, one launch (start us, length us, event | category | flops | bytes accessed | tf_op | source)
XLA Modules:
  0.0 982.8 jit_solution(11895613560107328245)
XLA Ops:
  21.6 63.1 %all-reduce.21 = (bf16[768]{0:T(1024)(128)(2,1)S(1)}, bf16[768]{0:T(1024)(128)(2,1)S(1)}, bf16[768]{0:T(1024)(128)(2,1)S(1)}, bf16[768]{0:T(1024)(128)(2,1)}, bf...) all-reduce(bf16[768]{0:T(1024)(128)(2,1)S(1)} %dynamic-update-slice, ...), channel_id=1, replica_groups=mesh['seq'=2,'fsdp'=16] {'fsdp'}, use_global_device_ids=true, to_apply=%add | all-reduce | flops 9984 | bytes 39936
  94.6 4.9 all-to-all-done
  103.1 27.2 %all-gather.11.cloned.1.call-done = bf16[768,768]{1,0:T(8,128)(2,1)} async-done(((bf16[48,768]{1,0:T(8,128)(2,1)}), bf16[768,768]{1,0:T(8,128)(2,1)}) %all-gather.11.cloned.1.call-update) | async-done | bytes 1179664 | tf_op jit(solution)/shard_map/all_gather | solution.py:202
  154.3 72.2 %while.38 = (s32[]{:T(128)}, bf16[6,1024,64]{1,2,0:T(8,128)(2,1)}, bf16[6,1024,256]{2,1,0:T(8,128)(2,1)}, bf16[6,16,256]{2,1,0:T(8,128)(2,1)}, f32[6,1024,64]{1,...) while((s32[]{:T(128)}, bf16[6,1024,64]{1,2,0:T(8,128)(2,1)}, ...), condition=%wide.region_10.11_spmd.clone, body=%wide.region_1.10_spmd.clone.sunk | while | flops 1165508608 | bytes 23870028 | solution.py:233
  232.0 4.5 all-to-all-start.3
  236.7 11.4 %all-to-all-done.3 = bf16[2,512,384]{1,2,0:T(8,128)(2,1)} async-done(((bf16[2,512,384]{1,2,0:T(8,128)(2,1)}), bf16[2,512,384]{1,2,0:T(8,128)(2,1)}, u32[]{:S(2)}, u32[]{:S(2)}) %all-to-all-start.3) | async-done | bytes 786464 | tf_op jit(solution)/shard_map/all_to_all | solution.py:237
  252.0 8.5 multiply_convert_fusion
  260.5 17.3 %all-gather.17.cloned.1.call-done = bf16[3072,768]{1,0:T(8,128)(2,1)} async-done(((bf16[192,768]{1,0:T(8,128)(2,1)}), bf16[3072,768]{1,0:T(8,128)(2,1)}) %all-gather.17.cloned.1.call-update) | async-done | bytes 4718608 | tf_op jit(solution)/shard_map/all_gather | solution.py:244
  277.8 6.6 fusion.129
  288.0 4.7 convert_reduce_fusion
  302.9 3.9 fusion.112
  306.8 7.2 all-to-all-done.4
  322.2 127.6 %while.39 = (s32[]{:T(128)}, bf16[6,1024,64]{1,2,0:T(8,128)(2,1)}, bf16[6,1024,64]{1,2,0:T(8,128)(2,1)}, bf16[6,1024,64]{1,2,0:T(8,128)(2,1)}, bf16[6,1024,64]{1...) while((s32[]{:T(128)}, bf16[6,1024,64]{1,2,0:T(8,128)(2,1)}, ...), condition=%wide.region_26.27_spmd.clone, body=%wide.region_19.26_spmd.clone.sunk | while | flops 2317456384 | bytes 54171828 | solution.py:325
  452.4 12.9 %all_to_all.140 = bf16[2,512,384]{1,2,0:T(8,128)(2,1)S(1)} all-to-all(bf16[2,512,384]{1,2,0:T(8,128)(2,1)S(1)} %copy.120), channel_id=1, replica_groups=mesh['seq'=2,'fsdp'=16] {'seq'}, dimensions={0} | all-to-all | bytes 1572864 | tf_op jit(solution)/shard_map/all_to_all | solution.py:342
  470.8 12.1 %all_to_all.141 = bf16[2,512,384]{1,2,0:T(8,128)(2,1)S(1)} all-to-all(bf16[2,512,384]{1,2,0:T(8,128)(2,1)S(1)} %copy.121), channel_id=1, replica_groups=mesh['seq'=2,'fsdp'=16] {'seq'}, dimensions={0} | all-to-all | bytes 1572864 | tf_op jit(solution)/shard_map/all_to_all | solution.py:343
  488.4 11.2 %all_to_all.142 = bf16[2,512,384]{1,2,0:T(8,128)(2,1)S(1)} all-to-all(bf16[2,512,384]{1,2,0:T(8,128)(2,1)S(1)} %copy.122), channel_id=1, replica_groups=mesh['seq'=2,'fsdp'=16] {'seq'}, dimensions={0} | all-to-all | bytes 1572864 | tf_op jit(solution)/shard_map/all_to_all | solution.py:344
  503.7 7.2 fusion.130
  512.4 8.2 fusion.115
  531.9 64.3 %reduce-scatter.21.cloned.1.call-done = f32[48,768]{1,0:T(8,128)} async-done(((f32[768,768]{1,0:T(8,128)}), f32[48,768]{1,0:T(8,128)}) %reduce-scatter.21.cloned.1.call-update) | async-done | bytes 147472
  597.9 64.3 %reduce-scatter.23.cloned.1.call-done = f32[48,768]{1,0:T(8,128)} async-done(((f32[768,768]{1,0:T(8,128)}), f32[48,768]{1,0:T(8,128)}) %reduce-scatter.23.cloned.1.call-update) | async-done | bytes 147472
  663.9 112.6 %reduce-scatter.15.cloned.1.call-done = f32[48,3072]{1,0:T(8,128)} async-done(((f32[768,3072]{1,0:T(8,128)}), f32[48,3072]{1,0:T(8,128)}) %reduce-scatter.15.cloned.1.call-update) | async-done | bytes 589840 | tf_op jit(solution)/shard_map/reduce_scatter | solution.py:301
  778.4 113.0 %reduce-scatter.17.cloned.1.call-done = f32[192,768]{1,0:T(8,128)} async-done(((f32[3072,768]{1,0:T(8,128)}), f32[192,768]{1,0:T(8,128)}) %reduce-scatter.17.cloned.1.call-update) | async-done | bytes 589840 | tf_op jit(solution)/shard_map/reduce_scatter | solution.py:303
  893.4 60.4 %all-reduce.20 = (bf16[768]{0:T(1024)(128)(2,1)S(1)}, bf16[768]{0:T(1024)(128)(2,1)S(1)}, bf16[768]{0:T(1024)(128)(2,1)S(1)}, bf16[768]{0:T(1024)(128)(2,1)S(1)}...) all-reduce(f32[768]{0:T(1024)S(1)} %reduce_sum.269, ...), channel_id=3, replica_groups=mesh['seq'=2,'fsdp'=16] {'fsdp'}, use_global_device_ids=true, to_apply=%region_30.31.clone | all-reduce | flops 9984 | bytes 59904
  954.6 5.0 all-reduce.22
  (706 shorter events, 332.0 us)
Async XLA Ops:
  7.2 77.6 %all-gather.7.cloned.1.call-start = ((), (), s32[]{:S(2)}) async-start(), calls=%async_computation.14 | async-start | bytes 1253376 | tf_op jit(solution)/shard_map/all_gather | solution.py:200
  7.9 83.7 %all-gather.9.cloned.1.call-start = ((), (), s32[]{:S(2)}) async-start(), calls=%async_computation.15 | async-start | bytes 1253376 | tf_op jit(solution)/shard_map/all_gather | solution.py:204
  8.7 121.6 %all-gather.11.cloned.1.call-start = ((), (), s32[]{:S(2)}) async-start(), calls=%async_computation.16 | async-start | bytes 1253376 | tf_op jit(solution)/shard_map/all_gather | solution.py:202
  9.4 227.3 %all-gather.13.cloned.1.call-start = ((), (), s32[]{:S(2)}) async-start(), calls=%async_computation.17 | async-start | bytes 1253376 | tf_op jit(solution)/shard_map/all_gather | solution.py:206
  10.0 242.0 %all-gather.15.cloned.1.call-start = ((), (), s32[]{:S(2)}) async-start(), calls=%async_computation.18 | async-start | bytes 5013504 | tf_op jit(solution)/shard_map/all_gather | solution.py:242
  88.0 11.5 %all-to-all-start = ((bf16[512,2,384]{2,0,1:T(8,128)(2,1)}), bf16[512,2,384]{2,0,1:T(8,128)(2,1)S(1)}, u32[]{:S(2)}, u32[]{:S(2)}) async-start(bf16[512,2,384]{2,0,1:T(8,128)(2,1)} %bitcast.250), calls=%async_computation | async-start | bytes 1572864 | tf_op jit(solution)/shard_map/all_to_all | solution.py:219
  99.5 33.8 %all-to-all-start.1 = ((bf16[512,2,384]{2,0,1:T(8,128)(2,1)}), bf16[512,2,384]{2,0,1:T(8,128)(2,1)S(1)}, u32[]{:S(2)}, u32[]{:S(2)}) async-start(bf16[512,2,384]{2,0,1:T(8,128)(2,1)} %bitcast.368), calls=%async_computation.1 | async-start | bytes 1572864 | tf_op jit(solution)/shard_map/all_to_all | solution.py:221
  133.3 15.6 %all-to-all-start.2 = ((bf16[512,2,384]{2,0,1:T(8,128)(2,1)}), bf16[512,2,384]{2,0,1:T(8,128)(2,1)S(1)}, u32[]{:S(2)}, u32[]{:S(2)}) async-start(bf16[512,2,384]{2,0,1:T(8,128)(2,1)} %bitcast.248), calls=%async_computation.2 | async-start | bytes 1572864 | tf_op jit(solution)/shard_map/all_to_all | solution.py:220
  136.9 140.9 %all-gather.17.cloned.1.call-start = ((), (), s32[]{:S(2)}) async-start(), calls=%async_computation.19 | async-start | bytes 5013504 | tf_op jit(solution)/shard_map/all_gather | solution.py:244
  229.8 6.8 copy-start.41
  229.8 18.2 %copy-start.14 = (bf16[1,512,768]{2,1,0:T(8,128)(2,1)S(1)}, bf16[1,512,768]{2,1,0:T(8,128)(2,1)}, u32[]{:S(2)}) copy-start(bf16[1,512,768]{2,1,0:T(8,128)(2,1)} %param.24) | copy-start | bytes 2359300
  232.0 16.1 %all-to-all-start.3 = ((bf16[2,512,384]{1,2,0:T(8,128)(2,1)}), bf16[2,512,384]{1,2,0:T(8,128)(2,1)}, u32[]{:S(2)}, u32[]{:S(2)}) async-start(bf16[2,512,384]{1,2,0:T(8,128)(2,1)} %copy.117), calls=%async_computation.3 | async-start | bytes 1572864 | tf_op jit(solution)/shard_map/all_to_all | solution.py:237
  277.8 10.2 %copy-start.51 = (f32[512,3072]{1,0:T(8,128)S(1)}, f32[512,3072]{1,0:T(8,128)}, u32[]{:S(2)}) copy-start(f32[512,3072]{1,0:T(8,128)} %get-tuple-element.603) | copy-start | bytes 18874372
  299.0 15.0 %all-to-all-start.4 = ((bf16[512,2,384]{2,0,1:T(8,128)(2,1)}), bf16[512,2,384]{2,0,1:T(8,128)(2,1)S(1)}, u32[]{:S(2)}, u32[]{:S(2)}) async-start(bf16[512,2,384]{2,0,1:T(8,128)(2,1)} %bitcast.369), calls=%async_computation.4 | async-start | bytes 1572864 | tf_op jit(solution)/shard_map/all_to_all | solution.py:324
  302.6 223.4 %reduce-scatter.13.cloned.1.call-start = ((), (), s32[]{:S(2)}) async-start(), calls=%async_computation.20 | async-start | bytes 2506752 | tf_op jit(solution)/shard_map/reduce_scatter | solution.py:362
  306.8 223.4 %reduce-scatter.19.cloned.1.call-start = ((), (), s32[]{:S(2)}) async-start(), calls=%async_computation.23 | async-start | bytes 2506752
  452.3 13.9 %copy-start.15 = (bf16[1,512,768]{2,1,0:T(8,128)(2,1)S(1)}, bf16[1,512,768]{2,1,0:T(8,128)(2,1)}, u32[]{:S(2)}) copy-start(bf16[1,512,768]{2,1,0:T(8,128)(2,1)} %param.24) | copy-start | bytes 2359300
  469.0 127.1 %reduce-scatter.21.cloned.1.call-start = ((), (), s32[]{:S(2)}) async-start(), calls=%async_computation.24 | async-start | bytes 2506752
  486.6 175.6 %reduce-scatter.23.cloned.1.call-start = ((), (), s32[]{:S(2)}) async-start(), calls=%async_computation.25 | async-start | bytes 2506752
  488.3 11.3 %copy-start.16 = (bf16[1,512,768]{2,1,0:T(8,128)(2,1)S(1)}, bf16[1,512,768]{2,1,0:T(8,128)(2,1)}, u32[]{:S(2)}) copy-start(bf16[1,512,768]{2,1,0:T(8,128)(2,1)} %param.24) | copy-start | bytes 2359300
  502.4 274.2 %reduce-scatter.15.cloned.1.call-start = ((), (), s32[]{:S(2)}) async-start(), calls=%async_computation.21 | async-start | bytes 10027008 | tf_op jit(solution)/shard_map/reduce_scatter | solution.py:301
  511.0 380.4 %reduce-scatter.17.cloned.1.call-start = ((), (), s32[]{:S(2)}) async-start(), calls=%async_computation.22 | async-start | bytes 10027008 | tf_op jit(solution)/shard_map/reduce_scatter | solution.py:303
  520.7 448.4 %all-reduce.26.cloned.1.call-start = ((), (), s32[]{:S(2)}) async-start(), calls=%async_computation.26 | async-start | bytes 2506752 | tf_op jit(solution)/shard_map/psum | solution.py:366
  893.2 73.8 %copy-start.25 = (bf16[768,768]{1,0:T(8,128)(2,1)S(1)}, bf16[768,768]{1,0:T(8,128)(2,1)}, u32[]{:S(2)}) copy-start(bf16[768,768]{1,0:T(8,128)(2,1)} %all-gather.9.cloned.1.call-done) | copy-start | bytes 3538948
  (123 other events, 374.3 us)
Sparse Core Ops, SparseCore 0:
  10.3 41.1 all-gather.6
  53.8 37.0 all-gather.8
  93.2 37.0 all-gather.10
  132.4 37.0 all-gather.12
  171.7 52.1 all-gather.14
  226.0 51.8 all-gather.16
  307.2 62.2 reduce-scatter.12
  469.1 60.9 reduce-scatter.18
  533.9 62.1 reduce-scatter.20
  599.8 62.3 reduce-scatter.22
  666.3 110.2 reduce-scatter.14
  780.5 110.8 reduce-scatter.16
  894.6 44.2 all-reduce.25
where the time goes:
time: 993 us; the launch traced here: 983 us
  waiting for transfers between devices  428 us (43%)
  matrix products  189 us (19%)
  blocking collectives  165 us (17%)
  local copies, waits for them, and re-layouts  114 us (11%)
  other arithmetic  46.3 us (5%)
  starting transfers between devices  19.8 us (2%)
  between operations  17.9 us (2%)
    unnamed x16, waiting for transfers between devices  134 us
    unnamed x2, blocking collectives  124 us
    reduce_scatter x1, waiting for transfers between devices, per_device(): lax.psum_scatter(grad_down_weight, 'fsdp', scatter_dimension=0, tiled=True)  113 us
    reduce_scatter x1, waiting for transfers between devices, per_device(): lax.psum_scatter(grad_in_weight, 'fsdp', scatter_dimension=0, tiled=True)  113 us
    dot_general x36, matrix products, right_product(): lax.dot_general(first_op, second, (((1,), (1,)), ((), ())), preferred_ele...  48.1 us
    dot_general x24, matrix products, left_product(): lax.dot_general(first_op, second, (((0,), (0,)), ((), ())), preferred_ele...  40.8 us
    unnamed x118, local copies, waits for them, and re-layouts  33.4 us
    dot_general x24, matrix products, head_logits(): jnp.dot(rows_low, feature_block, preferred_element_type=jnp.float32)  27.9 us
  transfers between devices with their start and end apart: 18, of which 10 were waited for; matrix products, arithmetic and copies ran while one was open for 31% of the time, Pallas kernels for 0%

commit v1 on v0

v1 whole, which is shorter than its diff:
```python
from functools import partial

import jax
import jax.numpy as jnp
from jax import lax
from jax.experimental import pallas as pl
from jax.experimental.pallas import tpu as pltpu
from jax.sharding import PartitionSpec as P

unit_spread = 0.013531646934131853
inv_root_two = 0.7071067811865476
inv_root_tau = 0.3989422804014327
far_below = -1e30
log2_e = 1.4426950408889634
MESH = pl.DeviceIdType.MESH
f32 = jnp.float32
bf16 = jnp.bfloat16
TAIL = 16


def layer_norm(residual, norm_gain, norm_bias):
    centred = residual - jnp.mean(residual, axis=1, keepdims=True)
    inverse = lax.rsqrt(jnp.mean(centred * centred, axis=1, keepdims=True) + 1e-06)
    normed = centred * inverse
    return (normed * norm_gain.astype(f32) + norm_bias.astype(f32), normed, inverse)


def norm_back(grad_out, normed, inverse, norm_gain):
    scaled = grad_out * norm_gain.astype(f32)
    centre_part = jnp.mean(scaled, axis=1, keepdims=True)
    slope_part = jnp.mean(scaled * normed, axis=1, keepdims=True)
    grad_resid = inverse * (scaled - centre_part - normed * slope_part)
    return (grad_resid, jnp.sum(grad_out * normed, axis=0), jnp.sum(grad_out, axis=0))


def gelu_value(pre_act):
    return 0.5 * pre_act * (1.0 + lax.erf(pre_act * inv_root_two))


def gelu_slope(pre_act):
    return (
        0.5 * (1.0 + lax.erf(pre_act * inv_root_two))
        + pre_act * jnp.exp(-0.5 * pre_act * pre_act) * inv_root_tau
    )


def mul(a, b):
    return lax.dot_general(a, b, (((1,), (0,)), ((), ())), preferred_element_type=f32)


def mul_tb(a, b):
    return lax.dot_general(a, b, (((1,), (1,)), ((), ())), preferred_element_type=f32)


def mul_ta(a, b):
    return lax.dot_general(a, b, (((0,), (0,)), ((), ())), preferred_element_type=f32)


def affine(row_block, weight, bias_row):
    return mul(row_block, weight) + bias_row.astype(f32)


def column_total(values):
    return jnp.sum(values, axis=0, dtype=f32)


def lane_ids(shape):
    return lax.broadcasted_iota(jnp.int32, shape, len(shape) - 1)


def doc_setup(lengths, place, mask_ref, onehot_ref, strad_ref, stradrow_ref):
    rows = mask_ref.shape[0]
    docs = lengths.shape[1]
    total = jnp.int32(0)
    ends = []
    for d in range(docs):
        total = total + lengths[0, d]
        ends.append(total)
    pos = lax.broadcasted_iota(jnp.int32, (rows, 128), 0) + place * rows
    pos_row = lax.broadcasted_iota(jnp.int32, (8, rows), 1) + place * rows
    did = jnp.zeros((rows, 128), jnp.int32)
    did_row = jnp.zeros((8, rows), jnp.int32)
    edge = jnp.int32(0)
    for end in ends[:-1]:
        did = did + (pos >= end).astype(jnp.int32)
        did_row = did_row + (pos_row >= end).astype(jnp.int32)
        edge = edge + (end <= rows).astype(jnp.int32)
    for j in range(rows // 128):
        cols = did_row[0:1, j * 128 : (j + 1) * 128]
        mask_ref[:, j * 128 : (j + 1) * 128] = (did == cols).astype(f32).astype(bf16)
    onehot_ref[...] = (did == lane_ids((rows, 128))).astype(f32)
    strad_ref[...] = (did == edge).astype(f32)
    one_row = (did_row[0:1] == edge).astype(f32)
    stradrow_ref[...] = jnp.broadcast_to(one_row, stradrow_ref.shape).astype(bf16)


def features_setup(ints_ref, omx_ref):
    heads, size, feats = ints_ref.shape

    @pl.loop(0, heads)
    def _(h):
        mat = ints_ref[h].astype(f32).astype(bf16)
        zero = jnp.zeros((size, feats), bf16)
        odd = lax.rem(h, 2) == 1
        omx_ref[h, 0:size] = jnp.where(odd, zero, mat)
        omx_ref[h, size : 2 * size] = jnp.where(odd, mat, zero)
        omx_ref[h, 2 * size :] = jnp.ones((2 * size, feats), bf16)


def three_terms(value):
    first = value.astype(bf16).astype(f32)
    second = (value - first).astype(bf16).astype(f32)
    return first, second, value - first - second


def forward_states(p, scale, q_ref, k_ref, v_ref, omx_ref, onehot_ref, strad_ref, stradrow_ref, pq_ref, pk_ref, peak_ref, out_ref):
    rows = q_ref.shape[1]
    lanes = lane_ids((1, 128))
    qp, kp, vp = q_ref[p], k_ref[p], v_ref[p]
    kf = kp.astype(f32)
    ksq = kf * kf
    vt = jnp.concatenate([vp.T * stradrow_ref[0:1], stradrow_ref[...]], axis=0)
    tail = jnp.zeros((TAIL, pq_ref.shape[-1]), f32)
    tail_row = lax.broadcasted_iota(jnp.int32, tail.shape, 0)
    for j in range(2):
        om = omx_ref[2 * p + j, 0:128]
        raw_q = mul(qp, om)
        raw_q = raw_q - jnp.max(raw_q, axis=1, keepdims=True)
        pq_ref[p, j] = jnp.exp2(raw_q * (scale * log2_e)).astype(bf16)
        here = (lanes >= 64) if j else (lanes < 64)
        half = jnp.sum(jnp.where(here, ksq, 0.0), axis=1, keepdims=True) * (0.0625 / scale)
        raw_k = mul(kp, om) - half
        row_peak = jnp.max(raw_k, axis=1, keepdims=True)
        doc_peak = jnp.max(jnp.where(onehot_ref[...] > 0.5, row_peak, far_below), axis=0, keepdims=True)
        back = jnp.max(jnp.where(onehot_ref[...] > 0.5, doc_peak, far_below), axis=1, keepdims=True)
        edge_peak = jnp.max(jnp.where(strad_ref[...] > 0.5, row_peak, far_below), axis=0, keepdims=True)
        phi_k = jnp.exp2((raw_k - back) * (scale * log2_e)).astype(bf16)
        pk_ref[p, j] = phi_k
        part = mul(vt, phi_k)
        out_ref[p, 64 * j : 64 * j + 64] = part[64 * j : 64 * j + 64].astype(bf16)
        edge_wide = jnp.concatenate([edge_peak, edge_peak], axis=1)
        peak_ref[p, j] = edge_wide
        tail = jnp.where(tail_row == j, part[128 : 128 + TAIL], tail)
        for t, term in enumerate(three_terms(edge_wide)):
            tail = jnp.where(tail_row == 2 + 3 * j + t, term, tail)
    out_ref[p, 128:] = tail.astype(bf16)


def edge_parts(state_ref, p, j):
    tail = state_ref[p, 128:].astype(f32)
    feats = tail.shape[1]
    totals = jnp.broadcast_to(tail[j : j + 1], (128, feats)).astype(bf16)
    peak = tail[2 + 3 * j : 3 + 3 * j] + tail[3 + 3 * j : 4 + 3 * j] + tail[4 + 3 * j : 5 + 3 * j]
    return jnp.concatenate([state_ref[p, 0:128], totals], axis=0), peak


def edge_weights(scale, own, other, strad):
    top = jnp.maximum(own, other)
    own_w = jnp.exp2((own - top) * (scale * log2_e))
    other_w = jnp.exp2((other - top) * (scale * log2_e))
    return 1.0 + strad * (own_w[:, 0:128] - 1.0), strad * other_w[:, 0:128]


def forward_finish(p, scale, v_ref, pq_ref, pk_ref, mask_ref, strad_ref, peak_ref, in_ref, att_ref, den_ref):
    rows = v_ref.shape[1]
    first_half = lane_ids((rows, 128)) < 64
    vx = jnp.concatenate([v_ref[p], jnp.ones((rows, 128), bf16)], axis=1)
    got = []
    for j in range(2):
        phi_q = pq_ref[p, j]
        pair = mul_tb(phi_q, pk_ref[p, j]).astype(bf16) * mask_ref[...]
        near = mul(pair, vx)
        state, other = edge_parts(in_ref, p, j)
        far = mul_tb(phi_q, state)
        wn, wf = edge_weights(scale, peak_ref[p, j], other, strad_ref[...])
        den = near[:, 128:] * wn + far[:, 128:] * wf
        got.append(((near[:, :128] * wn + far[:, :128] * wf) / den, den))
    att_ref[p] = jnp.where(first_half, got[0][0], got[1][0]).astype(bf16)
    den_ref[p] = jnp.where(first_half, got[0][1], got[1][1])


def numer_grads(p, att_ref, den_ref, gatt_ref):
    rows = att_ref.shape[1]
    lanes = lane_ids((rows, 128))
    gn = gatt_ref[p].astype(f32) / den_ref[p]
    prod = gn * att_ref[p].astype(f32)
    d0 = -jnp.sum(jnp.where(lanes < 64, prod, 0.0), axis=1, keepdims=True)
    d1 = -jnp.sum(jnp.where(lanes < 64, 0.0, prod), axis=1, keepdims=True)
    return gn, d0, d1, lanes


def backward_states(p, scale, att_ref, den_ref, gatt_ref, pq_ref, strad_ref, peak_ref, in_ref, out_ref):
    gn, d0, d1, lanes = numer_grads(p, att_ref, den_ref, gatt_ref)
    far = [edge_weights(scale, peak_ref[p, j], edge_parts(in_ref, p, j)[1], strad_ref[...])[1] for j in range(2)]
    left = (gn * jnp.where(lanes < 64, far[0], far[1])).astype(bf16)
    right = (jnp.where(lanes == 0, d0 * far[0], 0.0) + jnp.where(lanes == 1, d1 * far[1], 0.0)).astype(bf16)
    turned = jnp.concatenate([left.T, right.T[0:TAIL]], axis=0)
    tails = []
    for j in range(2):
        part = mul(turned, pq_ref[p, j])
        out_ref[p, 64 * j : 64 * j + 64] = part[64 * j : 64 * j + 64].astype(bf16)
        tails.append(part[128:])
    rowid = lax.broadcasted_iota(jnp.int32, tails[0].shape, 0)
    out_ref[p, 128:] = jnp.where(rowid == 0, tails[0], tails[1]).astype(bf16)


def backward_finish(
    p, scale, q_ref, k_ref, v_ref, omx_ref, pq_ref, pk_ref, mask_ref, strad_ref, peak_ref, in_ref, gin_ref,
    att_ref, den_ref, gatt_ref, gq_ref, gk_ref, gv_ref,
):
    rows = q_ref.shape[1]
    gn, d0, d1, lanes = numer_grads(p, att_ref, den_ref, gatt_ref)
    first_half = lanes < 64
    vp = v_ref[p]
    ones = jnp.ones((rows, 128), bf16)
    vx = jnp.concatenate([vp, ones], axis=1)
    strad = strad_ref[...]
    gq = jnp.zeros((rows, 128), f32)
    gk = jnp.zeros((rows, 128), f32)
    gv = jnp.zeros((rows, 128), f32)
    q_sums, k_sums = [], []
    for j in range(2):
        here = (lanes >= 64) if j else (lanes < 64)
        gd = d1 if j else d0
        state, other = edge_parts(in_ref, p, j)
        wn, wf = edge_weights(scale, peak_ref[p, j], other, strad)
        base_l = jnp.where(here, gn, 0.0)
        base_r = jnp.where(lanes == 0, gd, 0.0)
        near = jnp.concatenate([(base_l * wn).astype(bf16), (base_r * wn).astype(bf16)], axis=1)
        far = jnp.concatenate([(base_l * wf).astype(bf16), (base_r * wf).astype(bf16)], axis=1)
        phi_q, phi_k = pq_ref[p, j], pk_ref[p, j]
        turned = mul_tb(phi_k, phi_q).astype(bf16) * mask_ref[...]
        gv = gv + mul(turned, near[:, 0:128])
        gpair = mul_tb(near, vx).astype(bf16) * mask_ref[...]
        gphi_q = mul(gpair, phi_k) + mul(far, state)
        gturned = mul_tb(vx, near).astype(bf16) * mask_ref[...]
        gstate, _ = edge_parts(gin_ref, p, j)
        vs = jnp.concatenate(
            [(jnp.where(here, vp.astype(f32), 0.0) * strad).astype(bf16), jnp.where(lanes == 0, strad, 0.0).astype(bf16)],
            axis=1,
        )
        gphi_k = mul(gturned, phi_q) + mul(vs, gstate)
        gv = gv + jnp.where(here, mul_tb(phi_k, gstate[0:128]) * strad, 0.0)
        omx = omx_ref[2 * p + j]
        back_q = mul_tb((gphi_q * phi_q.astype(f32)).astype(bf16), omx)
        back_k = mul_tb((gphi_k * phi_k.astype(f32)).astype(bf16), omx)
        gq = gq + back_q[:, 0:128]
        gk = gk + back_k[:, 0:128]
        q_sums.append(back_q[:, 128:])
        k_sums.append(back_k[:, 128:])
    gq = gq * scale - jnp.where(first_half, q_sums[0], q_sums[1]) * q_ref[p].astype(f32) * 0.125
    gk = gk * scale - jnp.where(first_half, k_sums[0], k_sums[1]) * k_ref[p].astype(f32) * 0.125
    gq_ref[p] = gq.astype(bf16)
    gk_ref[p] = gk.astype(bf16)
    gv_ref[p] = gv.astype(bf16)


def peer_barrier(peers):
    barrier = pltpu.get_barrier_semaphore()
    for peer in peers:
        pl.semaphore_signal(barrier, inc=1, device_id=peer, device_id_type=MESH)
    pl.semaphore_wait(barrier, len(peers))


def forward_kernel(
    scale, x_ref, wq_ref, wk_ref, wv_ref, bias_ref, ints_ref, len_ref,
    q_ref, k_ref, v_ref, pq_ref, pk_ref, att_ref, den_ref, peak_ref, state_ref,
    omx_ref, mask_ref, onehot_ref, strad_ref, stradrow_ref, send_ref, ssem, rsem,
):
    place = lax.axis_index("seq")
    peer = {"seq": 1 - place}
    peer_barrier([peer])
    pairs = q_ref.shape[0]
    doc_setup(len_ref, place, mask_ref, onehot_ref, strad_ref, stradrow_ref)
    features_setup(ints_ref, omx_ref)
    for n, (w_ref, o_ref) in enumerate(((wq_ref, q_ref), (wk_ref, k_ref), (wv_ref, v_ref))):
        for j in range(pairs // 2):
            cols = slice(256 * j, 256 * j + 256)
            got = (mul(x_ref[...], w_ref[:, cols]) + bias_ref[n : n + 1, cols].astype(f32)).astype(bf16)
            o_ref[2 * j] = got[:, 0:128]
            o_ref[2 * j + 1] = got[:, 128:256]

    def copy(p):
        return pltpu.make_async_remote_copy(
            src_ref=send_ref.at[p], dst_ref=state_ref.at[p], send_sem=ssem.at[p], recv_sem=rsem.at[p],
            device_id=peer, device_id_type=MESH,
        )

    @pl.loop(0, pairs)
    def _(p):
        forward_states(p, scale, q_ref, k_ref, v_ref, omx_ref, onehot_ref, strad_ref, stradrow_ref, pq_ref, pk_ref, peak_ref, send_ref)
        copy(p).start()

    @pl.loop(0, pairs)
    def _(p):
        copy(p).wait()
        forward_finish(p, scale, v_ref, pq_ref, pk_ref, mask_ref, strad_ref, peak_ref, state_ref, att_ref, den_ref)


def backward_kernel(
    scale, q_ref, k_ref, v_ref, pq_ref, pk_ref, att_ref, den_ref, peak_ref, state_ref, gatt_ref, ints_ref, len_ref,
    gq_ref, gk_ref, gv_ref,
    gstate_ref, omx_ref, mask_ref, onehot_ref, strad_ref, stradrow_ref, send_ref, ssem, rsem,
):
    place = lax.axis_index("seq")
    peer = {"seq": 1 - place}
    peer_barrier([peer])
    pairs = q_ref.shape[0]
    doc_setup(len_ref, place, mask_ref, onehot_ref, strad_ref, stradrow_ref)
    features_setup(ints_ref, omx_ref)

    def copy(p):
        return pltpu.make_async_remote_copy(
            src_ref=send_ref.at[p], dst_ref=gstate_ref.at[p], send_sem=ssem.at[p], recv_sem=rsem.at[p],
            device_id=peer, device_id_type=MESH,
        )

    @pl.loop(0, pairs)
    def _(p):
        backward_states(p, scale, att_ref, den_ref, gatt_ref, pq_ref, strad_ref, peak_ref, state_ref, send_ref)
        copy(p).start()

    @pl.loop(0, pairs)
    def _(p):
        copy(p).wait()
        backward_finish(
            p, scale, q_ref, k_ref, v_ref, omx_ref, pq_ref, pk_ref, mask_ref, strad_ref, peak_ref, state_ref, gstate_ref,
            att_ref, den_ref, gatt_ref, gq_ref, gk_ref, gv_ref,
        )


def scratch_masks(rows, heads, feats):
    return [
        pltpu.VMEM((heads, 256, feats), bf16),
        pltpu.VMEM((rows, rows), bf16),
        pltpu.VMEM((rows, 128), f32),
        pltpu.VMEM((rows, 128), f32),
        pltpu.VMEM((TAIL, rows), bf16),
    ]


def vmem():
    return pl.BlockSpec(memory_space=pltpu.VMEM)


def attention_forward(x, wq, wk, wv, biases, ints, lengths):
    rows = x.shape[0]
    heads, size, feats = ints.shape
    pairs = heads // 2
    scale = size ** (-0.25) * unit_spread
    shape = jax.ShapeDtypeStruct
    return pl.pallas_call(
        partial(forward_kernel, scale),
        out_shape=[
            shape((pairs, rows, 128), bf16), shape((pairs, rows, 128), bf16), shape((pairs, rows, 128), bf16),
            shape((pairs, 2, rows, feats), bf16), shape((pairs, 2, rows, feats), bf16),
            shape((pairs, rows, 128), bf16), shape((pairs, rows, 128), f32),
            shape((pairs, 2, 1, feats), f32), shape((pairs, 128 + TAIL, feats), bf16),
        ],
        in_specs=[vmem()] * 6 + [pl.BlockSpec(memory_space=pltpu.SMEM)],
        out_specs=[vmem()] * 9,
        scratch_shapes=scratch_masks(rows, heads, feats) + [
            pltpu.VMEM((pairs, 128 + TAIL, feats), bf16),
            pltpu.SemaphoreType.DMA((pairs,)),
            pltpu.SemaphoreType.DMA((pairs,)),
        ],
        compiler_params=pltpu.CompilerParams(collective_id=0, has_side_effects=True, vmem_limit_bytes=60 << 20),
        name="attention_forward",
    )(x, wq, wk, wv, biases, ints, lengths)


def attention_backward(saved, gatt, ints, lengths):
    pairs, rows, _ = gatt.shape
    heads, size, feats = ints.shape
    scale = size ** (-0.25) * unit_spread
    shape = jax.ShapeDtypeStruct
    return pl.pallas_call(
        partial(backward_kernel, scale),
        out_shape=[shape((pairs, rows, 128), bf16)] * 3,
        in_specs=[vmem()] * 11 + [pl.BlockSpec(memory_space=pltpu.SMEM)],
        out_specs=[vmem()] * 3,
        scratch_shapes=[pltpu.VMEM((pairs, 128 + TAIL, feats), bf16)] + scratch_masks(rows, heads, feats) + [
            pltpu.VMEM((pairs, 128 + TAIL, feats), bf16),
            pltpu.SemaphoreType.DMA((pairs,)),
            pltpu.SemaphoreType.DMA((pairs,)),
        ],
        compiler_params=pltpu.CompilerParams(collective_id=1, has_side_effects=True, vmem_limit_bytes=60 << 20),
        name="attention_backward",
    )(*saved, gatt, ints, lengths)


def to_pairs(rows):
    return rows.reshape(rows.shape[0], -1, 128).transpose(1, 0, 2)


def from_pairs(pairs):
    return pairs.transpose(1, 0, 2).reshape(pairs.shape[1], -1)


def gathered(piece):
    return lax.all_gather(piece, "fsdp", axis=0, tiled=True)


def per_device(
    tokens, doc_lengths, feature_ints, w_query, b_query, w_key, b_key, w_value, b_value, w_out, b_out,
    norm1_gain, norm1_bias, w_in, b_in, w_down, b_down, norm2_gain, norm2_bias, cotangent,
):
    row_block = tokens[0]
    width = row_block.shape[1]
    fsdp = lax.axis_size("fsdp")
    me = lax.axis_index("fsdp")
    attn_stack = gathered(jnp.stack([w_query, w_key, w_value, w_out], axis=1))
    query_weight, key_weight, value_weight, out_weight = (attn_stack[:, i] for i in range(4))
    small = jnp.concatenate(
        [b_query, b_key, b_value, b_out, norm1_gain, norm1_bias, b_down, norm2_gain, norm2_bias, b_in]
    )
    small = lax.all_gather(small[None], "fsdp", axis=0, tiled=True)
    part = width // fsdp
    vectors = [small[:, part * i : part * (i + 1)].reshape(-1) for i in range(9)] + [small[:, 9 * part :].reshape(-1)]
    query_bias, key_bias, value_bias, out_bias, gain_one, offset_one, down_bias, gain_two, offset_two, in_bias = vectors
    saved = attention_forward(
        row_block, query_weight, key_weight, value_weight, jnp.stack([query_bias, key_bias, value_bias]),
        feature_ints, doc_lengths,
    )
    att_rows = from_pairs(saved[5])
    residual_one = row_block.astype(f32) + affine(att_rows, out_weight, out_bias)
    hidden_wide, normed_one, inverse_one = layer_norm(residual_one, gain_one, offset_one)
    hidden_low = hidden_wide.astype(bf16)
    in_weight = gathered(w_in)
    down_weight = gathered(w_down)
    pre_act = affine(hidden_low, in_weight, in_bias)
    gelu_low = gelu_value(pre_act).astype(bf16)
    residual_two = hidden_low.astype(f32) + affine(gelu_low, down_weight, down_bias)
    layer_wide, normed_two, inverse_two = layer_norm(residual_two, gain_two, offset_two)
    grad_out = cotangent[0].astype(f32)
    grad_resid_two, grad_gain_two, grad_offset_two = norm_back(grad_out, normed_two, inverse_two, gain_two)
    grad_down_low = grad_resid_two.astype(bf16)
    grad_down_weight = mul_ta(gelu_low, grad_down_low)
    grad_down_bias = column_total(grad_down_low)
    grad_pre_low = (mul_tb(grad_down_low, down_weight) * gelu_slope(pre_act)).astype(bf16)
    grad_in_weight = mul_ta(hidden_low, grad_pre_low)
    grad_in_bias = column_total(grad_pre_low)
    grad_hidden = mul_tb(grad_pre_low, in_weight) + grad_resid_two
    grad_resid_one, grad_gain_one, grad_offset_one = norm_back(grad_hidden, normed_one, inverse_one, gain_one)
    grad_proj_low = grad_resid_one.astype(bf16)
    grad_out_weight = mul_ta(att_rows, grad_proj_low)
    grad_out_bias = column_total(grad_proj_low)
    grad_att_rows = mul_tb(grad_proj_low, out_weight).astype(bf16)
    grads = attention_backward(saved, to_pairs(grad_att_rows), feature_ints, doc_lengths)
    grad_query_rows, grad_key_rows, grad_value_rows = (from_pairs(g) for g in grads)
    grad_query_weight = mul_ta(row_block, grad_query_rows)
    grad_key_weight = mul_ta(row_block, grad_key_rows)
    grad_value_weight = mul_ta(row_block, grad_value_rows)
    grad_input = (
        mul_tb(grad_query_rows, query_weight)
        + mul_tb(grad_key_rows, key_weight)
        + mul_tb(grad_value_rows, value_weight)
        + grad_resid_one
    )

    def owned(grad):
        shard = lax.psum_scatter(grad.astype(bf16), "fsdp", scatter_dimension=0, tiled=True)
        return lax.psum(shard, "seq").astype(f32)

    sums = jnp.stack(
        [
            column_total(grad_query_rows), column_total(grad_key_rows), column_total(grad_value_rows), grad_out_bias,
            grad_gain_one, grad_offset_one, grad_down_bias, grad_gain_two, grad_offset_two,
            *grad_in_bias.reshape(-1, width),
        ]
    )
    sums = lax.psum(sums, ("fsdp", "seq"))
    mine = [lax.dynamic_slice(sums[i], (me * part,), (part,)) for i in range(9)]
    wide = in_bias.shape[0] // fsdp
    mine_in = lax.dynamic_slice(sums[9:].reshape(-1), (me * wide,), (wide,))
    return (
        layer_wide.astype(bf16)[None],
        grad_input[None],
        owned(grad_query_weight), mine[0],
        owned(grad_key_weight), mine[1],
        owned(grad_value_weight), mine[2],
        owned(grad_out_weight), mine[3],
        mine[4], mine[5],
        owned(grad_in_weight), mine_in,
        owned(grad_down_weight), mine[6],
        mine[7], mine[8],
    )


def solution(mesh):
    rows, matrix, vector = P("fsdp", "seq", None), P("fsdp", None), P("fsdp")
    weights = (matrix, vector) * 4 + (vector, vector) + (matrix, vector) * 2 + (vector, vector)
    return jax.shard_map(
        per_device,
        mesh=mesh,
        in_specs=(rows, matrix, P(), *weights, rows),
        out_specs=(rows, rows, *weights),
        check_vma=False,
    )
```

time: 993 us -> 703 us (0.71)
  matrix products: 189 us -> 61.8 us
  local copies, waits for them, and re-layouts: 114 us -> 46.3 us
  blocking collectives: 165 us -> 104 us
  Pallas kernels: 0 us -> 51.6 us
  other arithmetic: 46.3 us -> 13 us
  waiting for transfers between devices: 428 us -> 402 us
  starting transfers between devices: 19.8 us -> 0.66 us
    dot_general x114 -> x15, matrix products: 189 us -> 61.8 us  [the longest x6 25.9 us: mul_ta(): lax.dot_general(a, b, (((0,), (0,)), ((), ())), preferred_element_type=f32)]
    unnamed x2 -> x1, blocking collectives: 124 us -> 64.8 us
    pallas_call x0 -> x2, Pallas kernels: none -> 51.6 us  [the longest x1 28.4 us: attention_backward(): pl.pallas_call(partial(backward_kernel, scale), out_shape=[shape((pairs,...]
    psum x1, waiting for transfers between devices: 0.01 us -> 39.4 us  [owned(): return lax.psum(shard, 'seq').astype(f32)]
    unnamed x16 -> x13, waiting for transfers between devices: 134 us -> 96.3 us
    all_to_all x3 -> x0, blocking collectives: 36.2 us -> none  [the longest x1 12.9 us: per_device(): lax.all_to_all(to_rows(head_grads[0]), 'seq', split_axis=0, concat_axis=1...]
    psum x1, blocking collectives: 4.97 us -> 39.7 us  [per_device(): sums = lax.psum(sums, ('fsdp', 'seq'))]
    all_to_all x5 -> x0, waiting for transfers between devices: 23.5 us -> none  [the longest x1 11.4 us: per_device(): lax.all_to_all(to_rows(attended), 'seq', split_axis=0, concat_axis=1, til...]
  transfers between devices with their start and end apart: 18 -> 10, of which waited for: 10 -> 8; matrix products, arithmetic and copies ran while one was open for 31% -> 11% of each run, Pallas kernels for 0% -> 3%
where the time goes in v1:
time: 703 us; the launch traced here: 695 us
  waiting for transfers between devices  402 us (57%)
  blocking collectives  104 us (15%)
  matrix products  61.8 us (9%)
  Pallas kernels  51.6 us (7%)
  local copies, waits for them, and re-layouts  46.3 us (7%)
  between operations  15.8 us (2%)
  other arithmetic  13 us (2%)
    reduce_scatter x3, waiting for transfers between devices, owned(): lax.psum_scatter(grad.astype(bf16), 'fsdp', scatter_dimension=0, tiled=True)  216 us
    unnamed x13, waiting for transfers between devices  96.3 us
    unnamed x1, blocking collectives  64.8 us
    all_gather x3, waiting for transfers between devices, gathered(): return lax.all_gather(piece, 'fsdp', axis=0, tiled=True)  49.8 us
    psum x1, blocking collectives, per_device(): sums = lax.psum(sums, ('fsdp', 'seq'))  39.7 us
    psum x1, waiting for transfers between devices, owned(): return lax.psum(shard, 'seq').astype(f32)  39.4 us
    pallas_call x1, Pallas kernels, attention_backward(): pl.pallas_call(partial(backward_kernel, scale), out_shape=[shape((pairs,...  28.4 us
    dot_general x6, matrix products, mul_ta(): lax.dot_general(a, b, (((0,), (0,)), ((), ())), preferred_element_type=f32)  25.9 us
  transfers between devices with their start and end apart: 10, of which 8 were waited for; matrix products, arithmetic and copies ran while one was open for 11% of the time, Pallas kernels for 3%

profile of v1, /device:TPU:0, one launch (start us, length us, event | category | flops | bytes accessed | tf_op | source)
XLA Modules:
  0.0 695.4 jit_solution(12480834476443174097)
XLA Ops:
  12.4 6.8 concatenate.3
  19.5 64.8 %all-reduce = bf16[9984]{0:T(1024)(128)(2,1)S(1)} all-reduce(bf16[9984]{0:T(1024)(128)(2,1)S(1)} %dynamic-update-slice), channel_id=2, replica_groups=mesh['seq'=2,'fsdp'=16] {'fsdp'}, use_global_device_ids=true, to_apply=%add | all-reduce | flops 9984 | bytes 39936
  85.9 3.9 slice_bitcast_fusion.1
  89.8 23.1 %attention_forward.1 = (bf16[6,512,128]{2,1,0:T(8,128)(2,1)}, bf16[6,512,128]{2,1,0:T(8,128)(2,1)}, bf16[6,512,128]{2,1,0:T(8,128)(2,1)}, bf16[6,2,512,256]{3,2,...) custom-call(bf16[512,768]{1,0:T(8,128)(2,1)} %bitcast.138, ...), custom_call_target="tpu_custom_call" | custom-call | tf_op jit(solution)/shard_map/attention_forward/pallas_call | solution.py:352
  117.2 4.1 all-gather.7.cloned.1.call-done
  121.3 8.3 %multiply_convert_fusion = (bf16[512,3072]{1,0:T(8,128)(2,1)}, f32[512,3072]{1,0:T(8,128)}) fusion(f32[3072]{0:T(1024)S(1)} %reshape.180, bf16[768,3072]{1,0:T(8,128)(2,1)} %all-gather.7.cloned.1.call-done, f32[512,768]{1,0:T(8,128)S(1)} %get-tuple-element.140, f32[768]{0:T(1024)S(1)} %reshape.179, f32[768]{0:T(1024)S(1)} %reshape.178, ...), kind=kOutput, calls=%fused_computation.8 | convolution fusion | flops 2427322368 | bytes 15751168 | tf_op jit(solution)/shard_map/dot_general | solution.py:48
  129.6 45.7 %all-gather.9.cloned.1.call-done = bf16[3072,768]{1,0:T(8,128)(2,1)} async-done(((bf16[192,768]{1,0:T(8,128)(2,1)}), bf16[3072,768]{1,0:T(8,128)(2,1)}) %all-gather.9.cloned.1.call-update) | async-done | bytes 4718608 | tf_op jit(solution)/shard_map/all_gather | solution.py:401
  175.3 6.2 fusion.41
  185.0 4.7 convert_reduce_fusion
  189.8 3.1 multiply_reduce_fusion
  193.5 3.0 convolution_convert_fusion.6
  199.1 28.4 %attention_backward.1 = (bf16[6,512,128]{2,1,0:T(8,128)(2,1)}, bf16[6,512,128]{2,1,0:T(8,128)(2,1)}, bf16[6,512,128]{2,1,0:T(8,128)(2,1)}) custom-call(bf16[6,512,128]{2,1,0:T(8,128)(2,1)} %get-tuple-element.31.q_ref, bf16[6,512,128]{2,1,0:T(8,128)(2,1)} %get-tuple-element.32.k_ref, bf16[6,512,128]{2,1,0:T(8,128)(2,1)} %get-tuple-element.33.v_ref, ...), custom_call_target="tpu_custom_call" | custom-call | tf_op jit(solution)/shard_map/attention_backward/pallas_call | solution.py:377
  236.5 3.2 fusion.16
  243.4 3.2 fusion.17
  251.0 7.5 %convolution_convert_fusion.1 = bf16[768,3072]{1,0:T(8,128)(2,1)} fusion(bf16[512,3072]{1,0:T(8,128)(2,1)} %copy-done.15, f32[512,768]{1,0:T(8,128)} %copy-done.1, f32[768]{0:T(1024)S(1)} %reshape.179, f32[768]{0:T(1024)S(1)} %reshape.178, f32[512]{0:T(512)S(1)} %add_rsqrt_fusion.1, f32[512]{0:T(512)S(1)} %broadcast_multiply_fusion.5), kind=kOutput, calls=%fused_computation.11 | convolution fusion | flops 2420244480 | bytes 9447424 | tf_op jit(solution)/shard_map/dot_general | solution.py:56
  258.9 7.3 %convolution_convert_fusion = bf16[3072,768]{1,0:T(8,128)(2,1)} fusion(bf16[512,3072]{1,0:T(8,128)(2,1)} %get-tuple-element.141, f32[512,768]{1,0:T(8,128)} %copy-done.9), kind=kOutput, calls=%fused_computation.10 | convolution fusion | flops 2418671616 | bytes 9437184 | tf_op jit(solution)/shard_map/dot_general | solution.py:56
  269.3 39.7 %psum.50 = f32[13,768]{1,0:T(8,128)S(1)} all-reduce(f32[13,768]{1,0:T(8,128)S(1)} %stack.63), channel_id=1, replica_groups=mesh['seq'=2,'fsdp'=16] {'fsdp','seq'}, use_global_device_ids=true, to_apply=%region_20.0 | all-reduce | flops 9984 | bytes 79872 | tf_op jit(solution)/shard_map/psum | solution.py:472
  317.2 35.7 %reduce-scatter.21.cloned.1.call-done = bf16[48,768]{1,0:T(8,128)(2,1)} async-done(((bf16[768,768]{1,0:T(8,128)(2,1)}), bf16[48,768]{1,0:T(8,128)(2,1)}) %reduce-scatter.21.cloned.1.call-update) | async-done | bytes 73744
  354.6 59.0 %reduce-scatter.23.cloned.1.call-done = bf16[48,768]{1,0:T(8,128)(2,1)} async-done(((bf16[768,768]{1,0:T(8,128)(2,1)}), bf16[48,768]{1,0:T(8,128)(2,1)}) %reduce-scatter.23.cloned.1.call-update) | async-done | bytes 73744
  415.3 59.1 %reduce-scatter.13.cloned.1.call-done = bf16[48,768]{1,0:T(8,128)(2,1)} async-done(((bf16[768,768]{1,0:T(8,128)(2,1)}), bf16[48,768]{1,0:T(8,128)(2,1)}) %reduce-scatter.13.cloned.1.call-update) | async-done | bytes 73744 | tf_op jit(solution)/shard_map/reduce_scatter | solution.py:462
  474.5 78.5 %reduce-scatter.15.cloned.1.call-done = bf16[48,3072]{1,0:T(8,128)(2,1)} async-done(((bf16[768,3072]{1,0:T(8,128)(2,1)}), bf16[48,3072]{1,0:T(8,128)(2,1)}) %reduce-scatter.15.cloned.1.call-update) | async-done | bytes 294928 | tf_op jit(solution)/shard_map/reduce_scatter | solution.py:462
  552.9 78.7 %reduce-scatter.17.cloned.1.call-done = bf16[192,768]{1,0:T(8,128)(2,1)} async-done(((bf16[3072,768]{1,0:T(8,128)(2,1)}), bf16[192,768]{1,0:T(8,128)(2,1)}) %reduce-scatter.17.cloned.1.call-update) | async-done | bytes 294928 | tf_op jit(solution)/shard_map/reduce_scatter | solution.py:462
  635.9 3.3 add_bitcast_fusion
  639.3 39.4 %all-reduce.4.cloned.1.call-done = (bf16[48,768]{0,1:T(8,128)(2,1)}, bf16[48,768]{0,1:T(8,128)(2,1)}, bf16[48,768]{0,1:T(8,128)(2,1)}, bf16[48,768]{1,0:T(8,128)...) async-done(((bf16[48,768]{0,1:T(8,128)(2,1)}, bf16[48,768]{0,1:T(8,128)(2,1)}, bf16[48,768]{0,1:T(8,128)(2,1)}, bf16[48,768]{1,0:T(8,128)(2,1)}, ...) | async-done | bytes 884752 | tf_op jit(solution)/shard_map/psum | solution.py:463
  (144 shorter events, 62.8 us)
Async XLA Ops:
  7.2 78.7 %all-gather.5.cloned.1.call-start = ((), (), s32[]{:S(2)}) async-start(), calls=%async_computation.6 | async-start | bytes 5013504 | tf_op jit(solution)/shard_map/all_gather | solution.py:401
  9.0 112.3 %all-gather.7.cloned.1.call-start = ((), (), s32[]{:S(2)}) async-start(), calls=%async_computation.7 | async-start | bytes 5013504 | tf_op jit(solution)/shard_map/all_gather | solution.py:401
  9.8 165.6 %all-gather.9.cloned.1.call-start = ((), (), s32[]{:S(2)}) async-start(), calls=%async_computation.8 | async-start | bytes 5013504 | tf_op jit(solution)/shard_map/all_gather | solution.py:401
  10.5 305.0 %reduce-scatter.19.cloned.1.call-start = ((), (), s32[]{:S(2)}) async-start(), calls=%async_computation.12 | async-start | bytes 1253376
  114.4 2.5 copy-start.3
  116.9 58.4 %copy-start.1 = (f32[512,768]{1,0:T(8,128)}, f32[512,768]{1,0:T(8,128)S(1)}, u32[]{:S(2)}) copy-start(f32[512,768]{1,0:T(8,128)S(1)} %get-tuple-element.140) | copy-start | bytes 4718596
  175.3 9.7 %copy-start.14 = (f32[512,3072]{1,0:T(8,128)S(1)}, f32[512,3072]{1,0:T(8,128)}, u32[]{:S(2)}) copy-start(f32[512,3072]{1,0:T(8,128)} %get-tuple-element.142) | copy-start | bytes 18874372
  183.4 6.3 slice-start
  185.0 4.8 copy-start.9
  185.0 4.8 copy-start.2
  185.0 4.8 slice-start.1
  189.8 3.2 copy-start.15
  232.8 2.5 copy-start.7
  235.3 117.7 %reduce-scatter.21.cloned.1.call-start = ((), (), s32[]{:S(2)}) async-start(), calls=%async_computation.13 | async-start | bytes 1253376
  239.7 2.5 copy-start.5
  242.1 171.5 %reduce-scatter.23.cloned.1.call-start = ((), (), s32[]{:S(2)}) async-start(), calls=%async_computation.14 | async-start | bytes 1253376
  246.6 2.5 copy-start.4
  249.1 225.4 %reduce-scatter.13.cloned.1.call-start = ((), (), s32[]{:S(2)}) async-start(), calls=%async_computation.9 | async-start | bytes 1253376 | tf_op jit(solution)/shard_map/reduce_scatter | solution.py:462
  251.0 301.9 %reduce-scatter.15.cloned.1.call-start = ((), (), s32[]{:S(2)}) async-start(), calls=%async_computation.10 | async-start | bytes 5013504 | tf_op jit(solution)/shard_map/reduce_scatter | solution.py:462
  258.6 373.1 %reduce-scatter.17.cloned.1.call-start = ((), (), s32[]{:S(2)}) async-start(), calls=%async_computation.11 | async-start | bytes 5013504 | tf_op jit(solution)/shard_map/reduce_scatter | solution.py:462
  266.2 2.8 copy-start.6
  266.2 412.5 %all-reduce.4.cloned.1.call-start = ((), (), s32[]{:S(2)}) async-start(), calls=%async_computation.15 | async-start | bytes 2506752 | tf_op jit(solution)/shard_map/psum | solution.py:463
  633.5 2.4 copy-start.8
  678.7 8.5 %copy-start.12 = (bf16[192,768]{1,0:T(8,128)(2,1)S(1)}, bf16[192,768]{1,0:T(8,128)(2,1)}, u32[]{:S(2)}) copy-start(bf16[192,768]{1,0:T(8,128)(2,1)} %get-tuple-element.108) | copy-start | bytes 884740
  (4 other events, 5.9 us)
Sparse Core Ops, SparseCore 0:
  10.9 56.4 all-gather.4
  69.6 51.6 all-gather.6
  123.6 51.6 all-gather.8
  235.4 56.6 reduce-scatter.18
  295.5 57.3 reduce-scatter.20
  356.4 57.1 reduce-scatter.22
  417.3 57.1 reduce-scatter.12
  478.3 74.5 reduce-scatter.14
  556.8 74.8 reduce-scatter.16
  634.8 43.8 all-reduce.3

commit v2 on v1

--- a/solution.py
+++ b/solution.py
@@ -16,6 +16,7 @@
 f32 = jnp.float32
 bf16 = jnp.bfloat16
 TAIL = 16
+DEPTH = 4
 
 
 def layer_norm(residual, norm_gain, norm_bias):
@@ -262,7 +263,663 @@
     pl.semaphore_wait(barrier, len(peers))
 
 
+class Place:
+    def __init__(self):
+        me = lax.axis_index("fsdp")
+        self.y = lax.axis_index("seq")
+        self.c = lax.rem(me, 2)
+        self.x = lax.rem(lax.div(me, 2), 2)
+        self.z = lax.div(me, 4)
+        self.across = {"seq": 1 - self.y}
+        self.twin = {"fsdp": self.z * 4 + self.x * 2 + 1 - self.c}
+        self.beside = {"fsdp": self.z * 4 + (1 - self.x) * 2 + self.c}
+
+    def along(self, d):
+        return {"fsdp": self.other(d) * 4 + self.x * 2 + self.c}
+
+    def other(self, d):
+        return lax.rem(self.z + (d + DEPTH), DEPTH)
+
+    def peers(self):
+        return [self.twin, self.beside, self.across] + [self.along(d) for d in range(1, DEPTH)]
+
+
+def cols_at(start, size):
+    return pl.ds(pl.multiple_of(start, 128), size)
+
+
+def remote(src, dst, ssem, rsem, peer):
+    return pltpu.make_async_remote_copy(
+        src_ref=src, dst_ref=dst, send_sem=ssem, recv_sem=rsem, device_id=peer, device_id_type=MESH
+    )
+
+
+class Gather:
+    def __init__(self, at, own, full, base, width, ssem, rsem, lsem):
+        self.at, self.own, self.full = at, own, full
+        self.third, self.base, self.width = width // 3, base, width
+        self.ssem, self.rsem, self.lsem = ssem, rsem, lsem
+        self.sent = []
+
+    def spread(self):
+        return cols_at(self.base + self.third * self.at.y, 2 * self.third)
+
+    def extra(self, y):
+        return cols_at(self.base + 2 * self.third * y, self.third)
+
+    def whole(self):
+        return pl.ds(self.base, self.width)
+
+    def go(self, n, ends):
+        src, dst, peer = ends()
+        remote(src, dst, self.ssem.at[n], self.rsem.at[n], peer).start()
+        self.sent.append((n, ends))
+
+    def came(self, n, ref):
+        remote(ref, ref, self.ssem.at[n], self.rsem.at[n], self.at.twin).wait_recv()
+
+    def local(self):
+        at = self.at
+        return pltpu.make_async_copy(
+            self.own.at[:, self.whole()], self.full.at[at.z, at.x, at.c, :, self.whole()], self.lsem
+        )
+
+    def begin(self):
+        at = self.at
+        self.local().start()
+        for d in range(1, DEPTH):
+            self.go(d - 1, lambda d=d: (*self.first(), at.along(d)))
+
+    def first(self):
+        at = self.at
+        return self.own.at[:, self.spread()], self.full.at[at.z, at.x, at.c, :, self.spread()]
+
+    def piece(self, d, x, cols):
+        return self.full.at[self.at.other(-d), x, self.at.c, :, cols]
+
+    def stage_x(self):
+        at = self.at
+        self.go(DEPTH - 1, lambda: (*self.first(), at.beside))
+        for d in range(1, DEPTH):
+            self.came(d - 1, self.piece(d, at.x, self.spread()))
+            self.go(DEPTH - 1 + d, lambda d=d: (*[self.piece(d, at.x, self.spread())] * 2, at.beside))
+            self.go(2 * DEPTH - 2 + d, lambda d=d: (*[self.piece(d, at.x, self.extra(at.y))] * 2, at.across))
+
+    def stage_y(self):
+        at = self.at
+        for d in range(DEPTH):
+            self.came(DEPTH - 1 + d, self.piece(d, 1 - at.x, self.spread()))
+            self.go(3 * DEPTH - 2 + d, lambda d=d: (*[self.piece(d, 1 - at.x, self.extra(at.y))] * 2, at.across))
+
+    def stage_c(self):
+        at = self.at
+        for d in range(1, DEPTH):
+            self.came(2 * DEPTH - 2 + d, self.piece(d, at.x, self.extra(1 - at.y)))
+        for d in range(DEPTH):
+            self.came(3 * DEPTH - 2 + d, self.piece(d, 1 - at.x, self.extra(1 - at.y)))
+        self.local().wait()
+        self.go(4 * DEPTH - 2, lambda: (*[self.full.at[:, :, at.c, :, self.whole()]] * 2, at.twin))
+
+    def ready(self):
+        self.came(4 * DEPTH - 2, self.full.at[:, :, 1 - self.at.c, :, self.whole()])
+
+    def drain(self):
+        for n, ends in self.sent:
+            src, dst, peer = ends()
+            remote(src, dst, self.ssem.at[n], self.rsem.at[n], peer).wait_send()
+
+
+GATHER_COPIES = 4 * DEPTH - 1
+
+
+class SmallSum:
+    def __init__(self, at, total, land, ssem, rsem, over_seq):
+        self.at, self.total, self.land, self.ssem, self.rsem, self.over_seq = at, total, land, ssem, rsem, over_seq
+        self.sent = []
+
+    def go(self, src, n, peer):
+        copy = remote(self.total.at[src], self.land.at[n], self.ssem.at[n], self.rsem.at[n], peer)
+        copy.start()
+        self.sent.append(copy)
+
+    def came(self, n):
+        remote(self.land.at[n], self.land.at[n], self.ssem.at[n], self.rsem.at[n], self.at.twin).wait_recv()
+
+    def begin(self):
+        for d in range(1, DEPTH):
+            self.go(0, d - 1, self.at.along(d))
+
+    def step(self, k):
+        if k == 0:
+            got = self.total[0]
+            for d in range(1, DEPTH):
+                self.came(d - 1)
+            order = [self.at.z] + [self.at.other(-d) for d in range(1, DEPTH)]
+            parts = [got] + [self.land[d - 1] for d in range(1, DEPTH)]
+            value = jnp.zeros_like(got)
+            for z in range(DEPTH):
+                one = jnp.zeros_like(got)
+                for place, part in zip(order, parts):
+                    one = jnp.where(place == z, part, one)
+                value = value + one
+        else:
+            self.came(DEPTH - 2 + k)
+            value = self.total[k] + self.land[DEPTH - 2 + k]
+        self.total[k + 1] = value
+        hops = [self.at.beside, self.at.twin] + ([self.at.across] if self.over_seq else [])
+        if k < len(hops):
+            self.go(k + 1, DEPTH - 1 + k, hops[k])
+
+    def steps(self):
+        return 4 if self.over_seq else 3
+
+    def result(self):
+        return self.total[self.steps()]
+
+    def drain(self):
+        for copy in self.sent:
+            copy.wait_send()
+
+
+def spread_vectors(at, pieces, wide):
+    width = 768
+    part = pieces[0].shape[-1]
+    rows = [p[...].astype(f32).reshape(1, part) for p in pieces]
+    rows = jnp.concatenate(rows + [jnp.zeros((16 - len(rows), part), f32)], axis=0)
+    rows = jnp.concatenate([rows, jnp.zeros((16, width - part), f32)], axis=1)
+    rows = pltpu.roll(rows, (at.z * 4 + at.x * 2 + at.c) * part, 1)
+    span = wide.shape[-1]
+    row = jnp.concatenate([wide[...].astype(f32).reshape(1, span), jnp.zeros((1, width - span), f32)], axis=1)
+    row = pltpu.roll(jnp.broadcast_to(row, (16, width)), (at.x * 2 + at.c) * span, 1)
+    here = lax.broadcasted_iota(jnp.int32, (16, width), 0)
+    return jnp.where(here == len(pieces) + at.z, row, rows)
+
+
 def forward_kernel(
+    scale, x_ref, wq_ref, wk_ref, wv_ref, wo_ref, win_ref, wdn_ref, bq_ref, bk_ref, bv_ref, bo_ref, g1_ref, o1_ref, bd_ref,
+    g2_ref, o2_ref, bin_ref, ints_ref, len_ref,
+    q_ref, k_ref, v_ref, pq_ref, pk_ref, att_ref, den_ref, peak_ref, state_ref, sq_ref, fin_ref, fdn_ref, vec_ref,
+    omx_ref, mask_ref, onehot_ref, strad_ref, stradrow_ref, send_ref, total_ref, land_ref,
+    ssem, rsem, gs_sem, gr_sem, gl_sem, vs_sem, vr_sem,
+):
+    at = Place()
+    pairs = q_ref.shape[0]
+    blocks = []
+    specs = [(w, sq_ref.at[n], 0, 768) for n, w in enumerate((wq_ref, wk_ref, wv_ref, wo_ref))]
+    specs += [(win_ref, fin_ref, 1536 * h, 1536) for h in range(2)]
+    half = wdn_ref.shape[0] // 2
+    specs += [(wdn_ref.at[pl.ds(half * h, half)], fdn_ref.at[:, :, :, pl.ds(half * h, half)], 0, 768) for h in range(2)]
+    for n, (own, full, base, width) in enumerate(specs):
+        blocks.append(Gather(at, own, full, base, width, gs_sem.at[n], gr_sem.at[n], gl_sem.at[n]))
+    bq, bk, bv, bo, bi0, bi1, bd0, bd1 = blocks
+    peer_barrier(at.peers())
+    vec = SmallSum(at, total_ref, land_ref, vs_sem, vr_sem, False)
+    total_ref[0] = spread_vectors(
+        at, (bq_ref, bk_ref, bv_ref, bo_ref, g1_ref, o1_ref, bd_ref, g2_ref, o2_ref), bin_ref
+    ).astype(bf16)
+    bq.begin()
+    vec.begin()
+    for b in blocks[1:]:
+        b.begin()
+    doc_setup(len_ref, at.y, mask_ref, onehot_ref, strad_ref, stradrow_ref)
+    features_setup(ints_ref, omx_ref)
+
+    def project(n, o_ref):
+        for j in range(pairs // 2):
+            cols = slice(256 * j, 256 * j + 256)
+            got = mul(x_ref[...], sq_ref[n, :, :, :, :, cols].reshape(768, 256))
+            got = (got + vec_ref[n : n + 1, cols].astype(f32)).astype(bf16)
+            o_ref[2 * j] = got[:, 0:128]
+            o_ref[2 * j + 1] = got[:, 128:256]
+
+    bq.stage_x()
+    vec.step(0)
+    bk.stage_x()
+    bq.stage_y()
+    vec.step(1)
+    bv.stage_x()
+    bk.stage_y()
+    bq.stage_c()
+    vec.step(2)
+    vec_ref[...] = vec.result()
+    bo.stage_x()
+    bv.stage_y()
+    bk.stage_c()
+    bq.ready()
+    project(0, q_ref)
+    bv.stage_c()
+    bk.ready()
+    project(1, k_ref)
+    bo.stage_y()
+    bv.ready()
+    project(2, v_ref)
+
+    def copy(p):
+        return remote(send_ref.at[p], state_ref.at[p], ssem.at[p], rsem.at[p], at.across)
+
+    early = {0: [bi0.stage_x], 2: [bo.stage_c, bi0.stage_y], 4: [bi1.stage_x], 5: [bi0.stage_c]}
+    late = {0: [bi1.stage_y], 1: [bo.ready], 2: [bd0.stage_x, bi0.ready], 3: [bi1.stage_c], 4: [bd0.stage_y], 5: [bd1.stage_x]}
+
+    @pl.loop(0, pairs)
+    def _(p):
+        forward_states(p, scale, q_ref, k_ref, v_ref, omx_ref, onehot_ref, strad_ref, stradrow_ref, pq_ref, pk_ref, peak_ref, send_ref)
+        copy(p).start()
+        for n, todo in early.items():
+            @pl.when(p == n)
+            def _(todo=todo):
+                for one in todo:
+                    one()
+
+    @pl.loop(0, pairs)
+    def _(p):
+        copy(p).wait()
+        forward_finish(p, scale, v_ref, pq_ref, pk_ref, mask_ref, strad_ref, peak_ref, state_ref, att_ref, den_ref)
+        for n, todo in late.items():
+            @pl.when(p == n)
+            def _(todo=todo):
+                for one in todo:
+                    one()
+
+    bd0.stage_c()
+    bd1.stage_y()
+    bi1.ready()
+    bd1.stage_c()
+    bd0.ready()
+    bd1.ready()
+    for b in blocks:
+        b.drain()
+    vec.drain()
+
+
+class Scatter:
+    def __init__(self, at, n, flip, source, acc, twin_in, wide_in, half_in, deep_in, done, done_in, put, ssem, rsem, lsem):
+        self.at, self.n, self.flip, self.source, self.acc = at, n, flip, source, acc
+        self.twin_in, self.wide_in, self.half_in, self.deep_in = twin_in, wide_in, half_in, deep_in
+        self.done, self.done_in, self.put = done, done_in, put
+        self.ssem, self.rsem, self.lsem = ssem, rsem, lsem
+        self.half = acc.shape[-1] // 2
+        self.sent = []
+
+    def side(self, y):
+        return cols_at(self.half * y, self.half)
+
+    def go(self, n, ends):
+        src, dst, peer = ends()
+        remote(src, dst, self.ssem.at[n], self.rsem.at[n], peer).start()
+        self.sent.append((n, ends))
+
+    def came(self, n, ref):
+        remote(ref, ref, self.ssem.at[n], self.rsem.at[n], self.at.twin).wait_recv()
+
+    def local(self):
+        return pltpu.make_async_copy(self.source(self.at.c), self.acc, self.lsem)
+
+    def begin(self):
+        self.go(0, lambda: (self.source(1 - self.at.c), self.twin_in, self.at.twin))
+        self.local().start()
+
+    def stage_1(self):
+        at = self.at
+        self.local().wait()
+        self.came(0, self.twin_in)
+
+        @pl.loop(0, DEPTH)
+        def _(z):
+            for x in range(2):
+                self.acc[z, x] = (self.acc[z, x].astype(f32) + self.twin_in[z, x].astype(f32)).astype(bf16)
+
+        if self.flip:
+            self.go(1, lambda: (self.acc.at[:, :, :, self.side(1 - at.y)], self.wide_in, at.across))
+        else:
+            self.go(1, lambda: (self.acc.at[:, 1 - at.x], self.wide_in, at.beside))
+
+    def stage_2(self):
+        at = self.at
+        self.came(1, self.wide_in)
+
+        @pl.loop(0, DEPTH)
+        def _(z):
+            if self.flip:
+                for x in range(2):
+                    spot = (z, x, slice(None), self.side(at.y))
+                    self.acc[spot] = (self.acc[spot].astype(f32) + self.wide_in[z, x].astype(f32)).astype(bf16)
+            else:
+                self.acc[z, at.x] = (self.acc[z, at.x].astype(f32) + self.wide_in[z].astype(f32)).astype(bf16)
+
+        if self.flip:
+            self.go(2, lambda: (self.acc.at[:, 1 - at.x, :, self.side(at.y)], self.half_in, at.beside))
+        else:
+            self.go(2, lambda: (self.acc.at[:, at.x, :, self.side(1 - at.y)], self.half_in, at.across))
+
+    def stage_3(self):
+        at = self.at
+        self.came(2, self.half_in)
+
+        @pl.loop(0, DEPTH)
+        def _(z):
+            spot = (z, at.x, slice(None), self.side(at.y))
+            self.acc[spot] = (self.acc[spot].astype(f32) + self.half_in[z].astype(f32)).astype(bf16)
+
+        for d in range(1, DEPTH):
+            self.go(2 + d, lambda d=d: (self.acc.at[at.other(d), at.x, :, self.side(at.y)], self.deep_in.at[d - 1], at.along(d)))
+
+    def stage_4(self):
+        at = self.at
+        value = self.acc[at.z, at.x, :, self.side(at.y)].astype(f32)
+        for d in range(1, DEPTH):
+            self.came(2 + d, self.deep_in.at[d - 1])
+            value = value + self.deep_in[d - 1].astype(f32)
+        low = value.astype(bf16)
+        self.done[...] = low
+        self.put(at.y, low.astype(f32))
+        self.go(2 + DEPTH, lambda: (self.done, self.done_in, at.across))
+
+    def stage_5(self):
+        self.came(2 + DEPTH, self.done_in)
+        self.put(1 - self.at.y, self.done_in[...].astype(f32))
+
+    def drain(self):
+        for n, ends in self.sent:
+            src, dst, peer = ends()
+            remote(src, dst, self.ssem.at[n], self.rsem.at[n], peer).wait_send()
+
+
+SCATTER_COPIES = DEPTH + 3
+FLIPS = (False, True, False, True, False, True, False, True, False, True, False, True)
+
+
+def backward_kernel(
+    scale, x_ref, q_ref, k_ref, v_ref, pq_ref, pk_ref, att_ref, den_ref, peak_ref, state_ref, sq_ref, gatt_ref, gres_ref,
+    vecin_ref, ints_ref, len_ref, gdn_ref, gin_ref, go_ref,
+    gx_ref, oq_ref, ok_ref, ov_ref, oo_ref, oin_ref, odn_ref, vec_ref,
+    gstate_ref, omx_ref, mask_ref, onehot_ref, strad_ref, stradrow_ref, send_ref,
+    xt_ref, gq_ref, gk_ref, gv_ref, gw_ref, total_ref, land_ref,
+    acc_ref, twin_ref, wide0_ref, wide1_ref, half_ref, deep_ref, done_ref, donein_ref,
+    ssem, rsem, ws_sem, wr_sem, wl_sem, vs_sem, vr_sem,
+):
+    at = Place()
+    pairs = q_ref.shape[0]
+    sources = [lambda c, b=b: gdn_ref.at[:, :, c, pl.ds(48 * b, 48)] for b in range(4)]
+    sources += [lambda c, b=b: gin_ref.at[:, :, c, :, pl.ds(768 * b, 768)] for b in range(4)]
+    sources += [lambda c: go_ref.at[:, :, c]]
+    sources += [lambda c, n=n: gw_ref.at[n, :, :, c] for n in (2, 1, 0)]
+
+    def putter(ref, row, col):
+        def put(y, value):
+            ref[pl.ds(row, 48), cols_at(col + 384 * y, 384)] = value
+
+        return put
+
+    puts = [putter(odn_ref, 48 * b, 0) for b in range(4)] + [putter(oin_ref, 0, 768 * b) for b in range(4)]
+    puts += [putter(r, 0, 0) for r in (oo_ref, ov_ref, ok_ref, oq_ref)]
+    units = []
+    for n, (source, put) in enumerate(zip(sources, puts)):
+        wide = wide1_ref.at[n // 2] if FLIPS[n] else wide0_ref.at[n // 2]
+        units.append(
+            Scatter(
+                at, n, FLIPS[n], source, acc_ref.at[n], twin_ref.at[n], wide, half_ref.at[n], deep_ref.at[n],
+                done_ref.at[n], donein_ref.at[n], put, ws_sem.at[n], wr_sem.at[n], wl_sem.at[n],
+            )
+        )
+    early = len(units) - 3
+
+    def step(s):
+        for k in range(5):
+            u = s - k
+            if 0 <= u < len(units):
+                getattr(units[u], "stage_" + str(k + 1))()
+
+    peer_barrier(at.peers())
+    for u in units[:early]:
+        u.begin()
+    doc_setup(len_ref, at.y, mask_ref, onehot_ref, strad_ref, stradrow_ref)
+    features_setup(ints_ref, omx_ref)
+
+    def copy(p):
+        return remote(send_ref.at[p], gstate_ref.at[p], ssem.at[p], rsem.at[p], at.across)
+
+    @pl.loop(0, pairs)
+    def _(p):
+        backward_states(p, scale, att_ref, den_ref, gatt_ref, pq_ref, strad_ref, peak_ref, state_ref, send_ref)
+        copy(p).start()
+        for n, s in ((2, 0), (5, 1)):
+            @pl.when(p == n)
+            def _(s=s):
+                step(s)
+
+    for j in range(pairs):
+        xt_ref[128 * j : 128 * j + 128] = x_ref[:, 128 * j : 128 * j + 128].T
+    total_ref[0] = vecin_ref[...]
+
+    @pl.loop(0, pairs)
+    def _(p):
+        copy(p).wait()
+        backward_finish(
+            p, scale, q_ref, k_ref, v_ref, omx_ref, pq_ref, pk_ref, mask_ref, strad_ref, peak_ref, state_ref, gstate_ref,
+            att_ref, den_ref, gatt_ref, gq_ref, gk_ref, gv_ref,
+        )
+        cols = cols_at(128 * p, 128)
+        both = mul(xt_ref[...], jnp.concatenate([gq_ref[p], gk_ref[p]], axis=1)).astype(bf16)
+        gw_ref[0, :, :, :, :, cols] = both[:, 0:128].reshape(DEPTH, 2, 2, 48, 128)
+        gw_ref[1, :, :, :, :, cols] = both[:, 128:256].reshape(DEPTH, 2, 2, 48, 128)
+        gw_ref[2, :, :, :, :, cols] = mul(xt_ref[...], gv_ref[p]).astype(bf16).reshape(DEPTH, 2, 2, 48, 128)
+        for n, ref in enumerate((gq_ref, gk_ref, gv_ref)):
+            total_ref[0, n : n + 1, cols] = jnp.sum(ref[p].astype(f32), axis=0, keepdims=True)
+        for n in range(6):
+            @pl.when(p == n)
+            def _(n=n):
+                step(n + 2)
+
+    vec = SmallSum(at, total_ref, land_ref, vs_sem, vr_sem, True)
+    vec.begin()
+    for u in units[early:]:
+        u.begin()
+    step(8)
+
+    def grad_input(j):
+        cols = slice(256 * j, 256 * j + 256)
+        value = gres_ref[:, cols]
+        for n, ref in enumerate((gq_ref, gk_ref, gv_ref)):
+            for i in range(pairs // 2):
+                left = jnp.concatenate([ref[2 * i], ref[2 * i + 1]], axis=1)
+                right = sq_ref[n, 256 * j : 256 * j + 256, 256 * i : 256 * i + 256]
+                value = value + mul_tb(left, right)
+        gx_ref[:, cols] = value
+
+    step(9)
+    vec.step(0)
+    grad_input(0)
+    step(10)
+    vec.step(1)
+    grad_input(1)
+    step(11)
+    vec.step(2)
+    grad_input(2)
+    step(12)
+    vec.step(3)
+    vec_ref[...] = vec.result()
+    for s in range(13, 16):
+        step(s)
+    for u in units:
+        u.drain()
+    vec.drain()
+
+
+def scratch_masks(rows, heads, feats):
+    return [
+        pltpu.VMEM((heads, 256, feats), bf16),
+        pltpu.VMEM((rows, rows), bf16),
+        pltpu.VMEM((rows, 128), f32),
+        pltpu.VMEM((rows, 128), f32),
+        pltpu.VMEM((TAIL, rows), bf16),
+    ]
+
+
+def vmem():
+    return pl.BlockSpec(memory_space=pltpu.VMEM)
+
+
+def anywhere():
+    return pl.BlockSpec(memory_space=pl.ANY)
+
+
+def smem():
+    return pl.BlockSpec(memory_space=pltpu.SMEM)
+
+
+def attention_forward(x, weights, vectors, ints, lengths):
+    rows, width = x.shape
+    heads, size, feats = ints.shape
+    pairs = heads // 2
+    hidden = weights[4].shape[1]
+    part = weights[0].shape[0]
+    scale = size ** (-0.25) * unit_spread
+    shape = jax.ShapeDtypeStruct
+    grid = (DEPTH, 2, 2)
+    dma = pltpu.SemaphoreType.DMA
+    return pl.pallas_call(
+        partial(forward_kernel, scale),
+        out_shape=[
+            shape((pairs, rows, 128), bf16), shape((pairs, rows, 128), bf16), shape((pairs, rows, 128), bf16),
+            shape((pairs, 2, rows, feats), bf16), shape((pairs, 2, rows, feats), bf16),
+            shape((pairs, rows, 128), bf16), shape((pairs, rows, 128), f32),
+            shape((pairs, 2, 1, feats), f32), shape((pairs, 128 + TAIL, feats), bf16),
+            shape((4, *grid, part, width), bf16),
+            shape((*grid, part, hidden), bf16), shape((*grid, weights[5].shape[0], width), bf16),
+            shape((16, width), bf16),
+        ],
+        in_specs=[vmem()] * 18 + [smem()],
+        out_specs=[vmem()] * 10 + [anywhere()] * 2 + [vmem()],
+        scratch_shapes=scratch_masks(rows, heads, feats) + [
+            pltpu.VMEM((pairs, 128 + TAIL, feats), bf16),
+            pltpu.VMEM((4, 16, width), bf16),
+            pltpu.VMEM((DEPTH + 1, 16, width), bf16),
+            dma((pairs,)), dma((pairs,)),
+            dma((8, GATHER_COPIES)), dma((8, GATHER_COPIES)), dma((8,)),
+            dma((DEPTH + 1,)), dma((DEPTH + 1,)),
+        ],
+        compiler_params=pltpu.CompilerParams(collective_id=0, has_side_effects=True, vmem_limit_bytes=60 << 20),
+        name="attention_forward",
+    )(x, *weights, *vectors, ints, lengths)
+
+
+def attention_backward(x, saved, gatt, gres, vec, ints, lengths, gdn, gin, go):
+    rows, width = x.shape
+    heads, size, feats = ints.shape
+    pairs = heads // 2
+    scale = size ** (-0.25) * unit_spread
+    shape = jax.ShapeDtypeStruct
+    dma = pltpu.SemaphoreType.DMA
+    grid = (DEPTH, 2, 2)
+    part = width // 16
+    hidden = gin.shape[1]
+    units = 12
+    gdn = gdn.reshape(*grid, -1, width)
+    gin = gin.reshape(*grid, part, hidden)
+    go = go.reshape(*grid, part, width)
+    return pl.pallas_call(
+        partial(backward_kernel, scale),
+        out_shape=[shape((rows, width), f32)]
+        + [shape((part, width), f32)] * 4
+        + [shape((part, hidden), f32), shape((hidden // 16, width), f32), shape((16, width), f32)],
+        in_specs=[vmem()] * 15 + [smem()] + [anywhere()] * 3,
+        out_specs=[vmem()] * 8,
+        scratch_shapes=[pltpu.VMEM((pairs, 128 + TAIL, feats), bf16)] + scratch_masks(rows, heads, feats) + [
+            pltpu.VMEM((pairs, 128 + TAIL, feats), bf16),
+            pltpu.VMEM((width, rows), bf16),
+            pltpu.VMEM((pairs, rows, 128), bf16), pltpu.VMEM((pairs, rows, 128), bf16), pltpu.VMEM((pairs, rows, 128), bf16),
+            pltpu.VMEM((3, *grid, part, width), bf16),
+            pltpu.VMEM((5, 16, width), f32),
+            pltpu.VMEM((DEPTH + 2, 16, width), f32),
+            pltpu.VMEM((units, DEPTH, 2, part, width), bf16),
+            pltpu.VMEM((units, DEPTH, 2, part, width), bf16),
+            pltpu.VMEM((units // 2, DEPTH, part, width), bf16),
+            pltpu.VMEM((units // 2, DEPTH, 2, part, width // 2), bf16),
+            pltpu.VMEM((units, DEPTH, part, width // 2), bf16),
+            pltpu.VMEM((units, DEPTH - 1, part, width // 2), bf16),
+            pltpu.VMEM((units, part, width // 2), bf16),
+            pltpu.VMEM((units, part, width // 2), bf16),
+            dma((pairs,)), dma((pairs,)),
+            dma((units, SCATTER_COPIES)), dma((units, SCATTER_COPIES)), dma((units,)),
+            dma((DEPTH + 2,)), dma((DEPTH + 2,)),
+        ],
+        compiler_params=pltpu.CompilerParams(collective_id=1, has_side_effects=True, vmem_limit_bytes=63 << 20),
+        name="attention_backward",
+    )(x, *saved, gatt, gres, vec, ints, lengths, gdn, gin, go)
+
+
+def to_pairs(rows):
+    return rows.reshape(rows.shape[0], -1, 128).transpose(1, 0, 2)
+
+
+def from_pairs(pairs):
+    return pairs.transpose(1, 0, 2).reshape(pairs.shape[1], -1)
+
+
+def per_device(
+    tokens, doc_lengths, feature_ints, w_query, b_query, w_key, b_key, w_value, b_value, w_out, b_out,
+    norm1_gain, norm1_bias, w_in, b_in, w_down, b_down, norm2_gain, norm2_bias, cotangent,
+):
+    row_block = tokens[0]
+    width = row_block.shape[1]
+    me = lax.axis_index("fsdp")
+    *saved, square, in_weight, down_weight, vec = attention_forward(
+        row_block,
+        (w_query, w_key, w_value, w_out, w_in, w_down),
+        (b_query, b_key, b_value, b_out, norm1_gain, norm1_bias, b_down, norm2_gain, norm2_bias, b_in),
+        feature_ints, doc_lengths,
+    )
+    in_weight = in_weight.reshape(width, -1)
+    down_weight = down_weight.reshape(-1, width)
+    square = square.reshape(4, width, width)
+    out_weight = square[3]
+    _, _, _, out_bias, gain_one, offset_one, down_bias, gain_two, offset_two = (vec[i] for i in range(9))
+    in_bias = vec[9:13].reshape(-1)
+    att_rows = from_pairs(saved[5])
+    residual_one = row_block.astype(f32) + affine(att_rows, out_weight, out_bias)
+    hidden_wide, normed_one, inverse_one = layer_norm(residual_one, gain_one, offset_one)
+    hidden_low = hidden_wide.astype(bf16)
+    pre_act = affine(hidden_low, in_weight, in_bias)
+    gelu_low = gelu_value(pre_act).astype(bf16)
+    residual_two = hidden_low.astype(f32) + affine(gelu_low, down_weight, down_bias)
+    layer_wide, normed_two, inverse_two = layer_norm(residual_two, gain_two, offset_two)
+    grad_out = cotangent[0].astype(f32)
+    grad_resid_two, grad_gain_two, grad_offset_two = norm_back(grad_out, normed_two, inverse_two, gain_two)
+    grad_down_low = grad_resid_two.astype(bf16)
+    grad_down_weight = mul_ta(gelu_low, grad_down_low).astype(bf16)
+    grad_down_bias = column_total(grad_down_low)
+    grad_pre_low = (mul_tb(grad_down_low, down_weight) * gelu_slope(pre_act)).astype(bf16)
+    grad_in_weight = mul_ta(hidden_low, grad_pre_low).astype(bf16)
+    grad_in_bias = column_total(grad_pre_low)
+    grad_hidden = mul_tb(grad_pre_low, in_weight) + grad_resid_two
+    grad_resid_one, grad_gain_one, grad_offset_one = norm_back(grad_hidden, normed_one, inverse_one, gain_one)
+    grad_proj_low = grad_resid_one.astype(bf16)
+    grad_out_weight = mul_ta(att_rows, grad_proj_low).astype(bf16)
+    grad_out_bias = column_total(grad_proj_low)
+    grad_att_rows = mul_tb(grad_proj_low, out_weight).astype(bf16)
+    nothing = jnp.zeros((width,), f32)
+    sums = jnp.stack(
+        [
+            nothing, nothing, nothing, grad_out_bias, grad_gain_one, grad_offset_one, grad_down_bias, grad_gain_two,
+            grad_offset_two, *grad_in_bias.reshape(-1, width), nothing, nothing, nothing,
+        ]
+    )
+    grad_input, gq, gk, gv, go, gin, gdn, sums = attention_backward(
+        row_block, (*saved, square), to_pairs(grad_att_rows), grad_resid_one, sums, feature_ints, doc_lengths,
+        grad_down_weight, grad_in_weight, grad_out_weight,
+    )
+    part = b_query.shape[0]
+    wide = b_in.shape[0]
+    mine = lax.dynamic_slice(sums, (0, me * part), (9, part))
+    mine_in = lax.dynamic_slice(sums[9:13].reshape(-1), (me * wide,), (wide,))
+    return (
+        layer_wide.astype(bf16)[None],
+        grad_input[None],
+        gq, mine[0], gk, mine[1], gv, mine[2], go, mine[3], mine[4], mine[5], gin, mine_in, gdn, mine[6], mine[7], mine[8],
+    )
+
+
+def forward_kernel_wide(
     scale, x_ref, wq_ref, wk_ref, wv_ref, bias_ref, ints_ref, len_ref,
     q_ref, k_ref, v_ref, pq_ref, pk_ref, att_ref, den_ref, peak_ref, state_ref,
     omx_ref, mask_ref, onehot_ref, strad_ref, stradrow_ref, send_ref, ssem, rsem,
@@ -297,7 +954,7 @@
         forward_finish(p, scale, v_ref, pq_ref, pk_ref, mask_ref, strad_ref, peak_ref, state_ref, att_ref, den_ref)
 
 
-def backward_kernel(
+def backward_kernel_wide(
     scale, q_ref, k_ref, v_ref, pq_ref, pk_ref, att_ref, den_ref, peak_ref, state_ref, gatt_ref, ints_ref, len_ref,
     gq_ref, gk_ref, gv_ref,
     gstate_ref, omx_ref, mask_ref, onehot_ref, strad_ref, stradrow_ref, send_ref, ssem, rsem,
@@ -329,28 +986,14 @@
         )
 
 
-def scratch_masks(rows, heads, feats):
-    return [
-        pltpu.VMEM((heads, 256, feats), bf16),
-        pltpu.VMEM((rows, rows), bf16),
-        pltpu.VMEM((rows, 128), f32),
-        pltpu.VMEM((rows, 128), f32),
-        pltpu.VMEM((TAIL, rows), bf16),
-    ]
-
-
-def vmem():
-    return pl.BlockSpec(memory_space=pltpu.VMEM)
-
-
-def attention_forward(x, wq, wk, wv, biases, ints, lengths):
+def attention_forward_wide(x, wq, wk, wv, biases, ints, lengths):
     rows = x.shape[0]
     heads, size, feats = ints.shape
     pairs = heads // 2
     scale = size ** (-0.25) * unit_spread
     shape = jax.ShapeDtypeStruct
     return pl.pallas_call(
-        partial(forward_kernel, scale),
+        partial(forward_kernel_wide, scale),
         out_shape=[
             shape((pairs, rows, 128), bf16), shape((pairs, rows, 128), bf16), shape((pairs, rows, 128), bf16),
             shape((pairs, 2, rows, feats), bf16), shape((pairs, 2, rows, feats), bf16),
@@ -369,13 +1012,13 @@
     )(x, wq, wk, wv, biases, ints, lengths)
 
 
-def attention_backward(saved, gatt, ints, lengths):
+def attention_backward_wide(saved, gatt, ints, lengths):
     pairs, rows, _ = gatt.shape
     heads, size, feats = ints.shape
     scale = size ** (-0.25) * unit_spread
     shape = jax.ShapeDtypeStruct
     return pl.pallas_call(
-        partial(backward_kernel, scale),
+        partial(backward_kernel_wide, scale),
         out_shape=[shape((pairs, rows, 128), bf16)] * 3,
         in_specs=[vmem()] * 11 + [pl.BlockSpec(memory_space=pltpu.SMEM)],
         out_specs=[vmem()] * 3,
@@ -389,19 +1032,11 @@
     )(*saved, gatt, ints, lengths)
 
 
-def to_pairs(rows):
-    return rows.reshape(rows.shape[0], -1, 128).transpose(1, 0, 2)
-
-
-def from_pairs(pairs):
-    return pairs.transpose(1, 0, 2).reshape(pairs.shape[1], -1)
-
-
 def gathered(piece):
     return lax.all_gather(piece, "fsdp", axis=0, tiled=True)
 
 
-def per_device(
+def per_device_wide(
     tokens, doc_lengths, feature_ints, w_query, b_query, w_key, b_key, w_value, b_value, w_out, b_out,
     norm1_gain, norm1_bias, w_in, b_in, w_down, b_down, norm2_gain, norm2_bias, cotangent,
 ):
@@ -418,7 +1053,7 @@
     part = width // fsdp
     vectors = [small[:, part * i : part * (i + 1)].reshape(-1) for i in range(9)] + [small[:, 9 * part :].reshape(-1)]
     query_bias, key_bias, value_bias, out_bias, gain_one, offset_one, down_bias, gain_two, offset_two, in_bias = vectors
-    saved = attention_forward(
+    saved = attention_forward_wide(
         row_block, query_weight, key_weight, value_weight, jnp.stack([query_bias, key_bias, value_bias]),
         feature_ints, doc_lengths,
     )
@@ -446,7 +1081,7 @@
     grad_out_weight = mul_ta(att_rows, grad_proj_low)
     grad_out_bias = column_total(grad_proj_low)
     grad_att_rows = mul_tb(grad_proj_low, out_weight).astype(bf16)
-    grads = attention_backward(saved, to_pairs(grad_att_rows), feature_ints, doc_lengths)
+    grads = attention_backward_wide(saved, to_pairs(grad_att_rows), feature_ints, doc_lengths)
     grad_query_rows, grad_key_rows, grad_value_rows = (from_pairs(g) for g in grads)
     grad_query_weight = mul_ta(row_block, grad_query_rows)
     grad_key_weight = mul_ta(row_block, grad_key_rows)
@@ -490,8 +1125,9 @@
 def solution(mesh):
     rows, matrix, vector = P("fsdp", "seq", None), P("fsdp", None), P("fsdp")
     weights = (matrix, vector) * 4 + (vector, vector) + (matrix, vector) * 2 + (vector, vector)
+    near = mesh.shape["fsdp"] == 4 * DEPTH and mesh.shape["seq"] == 2
     return jax.shard_map(
-        per_device,
+        per_device if near else per_device_wide,
         mesh=mesh,
         in_specs=(rows, matrix, P(), *weights, rows),
         out_specs=(rows, rows, *weights),

time: 703 us -> 279 us (0.40)
  waiting for transfers between devices: 402 us -> 0 us
  Pallas kernels: 51.6 us -> 220 us
  blocking collectives: 104 us -> 0 us
  matrix products: 61.8 us -> 31 us
  local copies, waits for them, and re-layouts: 46.3 us -> 21.4 us
  between operations: 15.8 us -> 0.98 us
  other arithmetic: 13 us -> 5.31 us
    reduce_scatter x3 -> x0, waiting for transfers between devices: 216 us -> none  [owned(): lax.psum_scatter(grad.astype(bf16), 'fsdp', scatter_dimension=0, tiled=True)]
    unnamed x13 -> x0, waiting for transfers between devices: 96.3 us -> none
    pallas_call x1, Pallas kernels: 28.4 us -> 115 us  [attention_backward(): pl.pallas_call(partial(backward_kernel, scale), out_shape=[shape((rows, w...]
    pallas_call x1, Pallas kernels: 23.1 us -> 105 us  [attention_forward(): pl.pallas_call(partial(forward_kernel, scale), out_shape=[shape((pairs, r...]
    unnamed x1 -> x0, blocking collectives: 64.8 us -> none
    all_gather x3 -> x0, waiting for transfers between devices: 49.8 us -> none  [gathered(): return lax.all_gather(piece, 'fsdp', axis=0, tiled=True)]
    psum x1 -> x0, blocking collectives: 39.7 us -> none  [per_device(): sums = lax.psum(sums, ('fsdp', 'seq'))]
    psum x1 -> x0, waiting for transfers between devices: 39.4 us -> none  [owned(): return lax.psum(shard, 'seq').astype(f32)]
  transfers between devices with their start and end apart: 10 -> 0, of which waited for: 8 -> 0; matrix products, arithmetic and copies ran while one was open for 11% -> 0% of each run, Pallas kernels for 3% -> 0%
where the time goes in v2:
time: 279 us; the launch traced here: 278 us
  Pallas kernels  220 us (79%)
  matrix products  31 us (11%)
  local copies, waits for them, and re-layouts  21.4 us (8%)
  other arithmetic  5.31 us (2%)
    pallas_call x1, Pallas kernels, attention_backward(): pl.pallas_call(partial(backward_kernel, scale), out_shape=[shape((rows, w...  115 us
    pallas_call x1, Pallas kernels, attention_forward(): pl.pallas_call(partial(forward_kernel, scale), out_shape=[shape((pairs, r...  105 us
    dot_general x3, matrix products, mul_ta(): lax.dot_general(a, b, (((0,), (0,)), ((), ())), preferred_element_type=f32)  14 us
    dot_general x3, matrix products, mul_tb(): lax.dot_general(a, b, (((1,), (1,)), ((), ())), preferred_element_type=f32)  9.87 us
    unnamed x43, local copies, waits for them, and re-layouts  9.56 us
    dot_general x3, matrix products, mul(): lax.dot_general(a, b, (((1,), (0,)), ((), ())), preferred_element_type=f32)  7.1 us

profile of v2, /device:TPU:0, one launch (start us, length us, event | category | flops | bytes accessed | tf_op | source)
XLA Modules:
  0.0 278.3 jit_solution(3767838709771054)
XLA Ops:
  0.7 104.9 %attention_forward.1 = (bf16[6,512,128]{2,1,0:T(8,128)(2,1)}, bf16[6,512,128]{2,1,0:T(8,128)(2,1)}, bf16[6,512,128]{2,1,0:T(8,128)(2,1)}, bf16[6,2,512,256]{3,2,...) custom-call(bf16[512,768]{1,0:T(8,128)(2,1)} %bitcast.74, ...), custom_call_target="tpu_custom_call" | custom-call | tf_op jit(solution)/shard_map/attention_forward/pallas_call | solution.py:780
  105.6 1.0 convert_reduce_fusion.5
  107.3 1.4 copy.38
  108.7 1.4 slice.59
  110.2 0.9 fusion.22
  111.5 1.6 copy-done.12
  113.1 3.3 %multiply_convert_fusion = (bf16[512,3072]{1,0:T(8,128)(2,1)S(1)}, f32[512,3072]{1,0:T(8,128)S(1)}) fusion(f32[3072]{0:T(1024)S(1)} %reshape.131, bf16[768,3072]{1,0:T(8,128)(2,1)S(1)} %bitcast.81, f32[512,768]{1,0:T(8,128)S(1)} %get-tuple-element.92, f32[768]{0:T(1024)S(1)} %get-tuple-element.70, f32[768]{0:T(1024)S(1)} %get-tuple-element.71, ...), kind=kOutput, calls=%fused_computation.8 | convolution fusion | flops 2427322368 | bytes 15751168 | tf_op jit(solution)/shard_map/dot_general | solution.py:49
  116.5 2.8 %fusion.23 = (f32[512]{0:T(512)S(1)}, f32[512,768]{1,0:T(8,128)S(1)}) fusion(f32[768]{0:T(1024)S(1)} %get-tuple-element.69, bf16[512,3072]{1,0:T(8,128)(2,1)S(1)} %get-tuple-element.93, bf16[3072,768]{1,0:T(8,128)(2,1)S(1)} %bitcast.85, f32[768]{0:T(1024)S(1)} %get-tuple-element.70, f32[768]{0:T(1024)S(1)} %get-tuple-element.71, ...), kind=kOutput, calls=%fused_computation.71 | convolution fusion | flops 2419457536 | bytes 11025408 | tf_op jit(solution)/shard_map/dot_general | solution.py:49
  120.4 0.8 fusion.14
  121.3 1.5 convert_reduce_fusion.2
  122.8 4.9 %convert_reduce_fusion = (f32[3072]{0:T(1024)S(1)}, bf16[512,3072]{1,0:T(8,128)(2,1)S(1)}) fusion(f32[512,3072]{1,0:T(8,128)S(1)} %get-tuple-element.94, f32[3072]{0:T(1024)S(1)} %reshape.131, bf16[3072,768]{1,0:T(8,128)(2,1)S(1)} %bitcast.86, f32[512,768]{1,0:T(8,128)S(1)} %get-tuple-element.74), kind=kOutput, calls=%fused_computation.7 | convolution fusion | flops 2436756480 | bytes 15753216 | tf_op jit(solution)/shard_map/dot_general | solution.py:53
  127.8 3.1 %multiply_reduce_fusion = (f32[768]{0:T(1024)S(1)}, f32[512]{0:T(512)S(1)}, f32[512]{0:T(512)S(1)}, f32[768]{0:T(1024)S(1)}, f32[512,768]{1,0:T(8,128)S(1)}) fusion(f32[512,768]{1,0:T(8,128)S(1)} %get-tuple-element.92, f32[512]{0:T(512)S(1)} %add_rsqrt_fusion.1, f32[512]{0:T(512)S(1)} %broadcast_multiply_fusion.5, f32[768]{0:T(1024)S(1)} %get-tuple-element.71, ...), kind=kOutput, calls=%fused_computation.24 | convolution fusion | flops 2419848704 | bytes 12600320 | tf_op jit(solution)/shard_map/dot_general | solution.py:53
  131.5 1.8 convolution_convert_fusion.3
  133.3 2.3 copy.39
  135.6 2.3 copy.40
  138.2 1.3 stack.27.vecin_ref
  139.5 7.3 %convolution_convert_fusion.1 = bf16[3072,768]{1,0:T(8,128)(2,1)} fusion(bf16[512,3072]{1,0:T(8,128)(2,1)} %copy-done.13, f32[512,768]{1,0:T(8,128)} %copy-done.5), kind=kOutput, calls=%fused_computation.11 | convolution fusion | flops 2418671616 | bytes 9437184 | tf_op jit(solution)/shard_map/dot_general | solution.py:57
  146.9 4.9 %convolution_convert_fusion = bf16[768,3072]{1,0:T(8,128)(2,1)} fusion(bf16[512,3072]{1,0:T(8,128)(2,1)S(1)} %copy-done.15, f32[512,768]{1,0:T(8,128)S(1)} %copy-done.3, f32[768]{0:T(1024)S(1)} %get-tuple-element.70, f32[768]{0:T(1024)S(1)} %get-tuple-element.71, f32[512]{0:T(512)S(1)} %add_rsqrt_fusion.1, f32[512]{0:T(512)S(1)} %broadcast_multiply_fusion.5), kind=kOutput, calls=%fused_computation.10 | convolution fusion | flops 2420244480 | bytes 9447424 | tf_op jit(solution)/shard_map/dot_general | solution.py:57
  151.7 1.8 convolution_convert_fusion.2
  153.5 114.7 %attention_backward.1 = (f32[512,768]{1,0:T(8,128)}, f32[48,768]{1,0:T(8,128)}, f32[48,768]{1,0:T(8,128)}, f32[48,768]{1,0:T(8,128)}, f32[48,768]{1,0:T(8,128)},...) custom-call(bf16[512,768]{1,0:T(8,128)(2,1)} %bitcast.75, ...), custom_call_target="tpu_custom_call" | custom-call | tf_op jit(solution)/shard_map/attention_backward/pallas_call | solution.py:820
  268.2 1.6 dynamic-slice_bitcast_fusion
  271.3 2.7 copy.48
  276.7 0.8 copy.53
  277.5 0.8 copy.54
  (69 shorter events, 7.0 us)
Async XLA Ops:
  108.7 1.5 copy-start.4
  110.2 2.9 %copy-start.12 = (bf16[4,2,2,48,3072]{4,3,2,1,0:T(8,128)(2,1)S(1)}, bf16[4,2,2,48,3072]{4,3,2,1,0:T(8,128)(2,1)}, u32[]{:S(2)}) copy-start(bf16[4,2,2,48,3072]{4,3,2,1,0:T(8,128)(2,1)} %get-tuple-element.42) | copy-start | bytes 14155780
  111.2 19.8 %copy-start.2 = (f32[512,768]{1,0:T(8,128)}, f32[512,768]{1,0:T(8,128)S(1)}, u32[]{:S(2)}) copy-start(f32[512,768]{1,0:T(8,128)S(1)} %get-tuple-element.92) | copy-start | bytes 4718596
  111.2 5.3 %slice-start = ((s8[4718592]{0:T(1024)(128)(4,1)}), s8[4194304]{0:T(1024)(128)(4,1)S(1)}, s32[]{:S(2)}) async-start(s8[4718592]{0:T(1024)(128)(4,1)} %bitcast.83), calls=%async_computation | async-start | bytes 8388608
  113.1 3.4 %slice-start.1 = ((s8[4718592]{0:T(1024)(128)(4,1)}), s8[524288]{0:T(1024)(128)(4,1)S(1)}, s32[]{:S(2)}) async-start(s8[4718592]{0:T(1024)(128)(4,1)} %bitcast.83), calls=%async_computation.1 | async-start | bytes 1048576
  116.5 2.9 %copy-start.13 = (bf16[512,3072]{1,0:T(8,128)(2,1)}, bf16[512,3072]{1,0:T(8,128)(2,1)S(1)}, u32[]{:S(2)}) copy-start(bf16[512,3072]{1,0:T(8,128)(2,1)S(1)} %get-tuple-element.93) | copy-start | bytes 9437188
  119.3 1.1 copy-start.1
  122.8 5.0 %copy-start.5 = (f32[512,768]{1,0:T(8,128)}, f32[512,768]{1,0:T(8,128)S(1)}, u32[]{:S(2)}) copy-start(f32[512,768]{1,0:T(8,128)S(1)} %get-tuple-element.74) | copy-start | bytes 4718596
  127.8 3.2 %copy-start.14 = (bf16[512,3072]{1,0:T(8,128)(2,1)}, bf16[512,3072]{1,0:T(8,128)(2,1)S(1)}, u32[]{:S(2)}) copy-start(bf16[512,3072]{1,0:T(8,128)(2,1)S(1)} %get-tuple-element.99) | copy-start | bytes 9437188
  131.5 20.2 %copy-start = (f32[512,768]{1,0:T(8,128)}, f32[512,768]{1,0:T(8,128)S(1)}, u32[]{:S(2)}) copy-start(f32[512,768]{1,0:T(8,128)S(1)} %get-tuple-element.76.gres_ref) | copy-start | bytes 4718596
  139.5 7.3 %copy-start.3 = (f32[512,768]{1,0:T(8,128)S(1)}, f32[512,768]{1,0:T(8,128)}, u32[]{:S(2)}) copy-start(f32[512,768]{1,0:T(8,128)} %copy-done.2) | copy-start | bytes 4718596
  139.5 7.3 %copy-start.15 = (bf16[512,3072]{1,0:T(8,128)(2,1)S(1)}, bf16[512,3072]{1,0:T(8,128)(2,1)}, u32[]{:S(2)}) copy-start(bf16[512,3072]{1,0:T(8,128)(2,1)} %copy-done.14) | copy-start | bytes 9437188
  271.2 2.8 copy-start.11
  271.2 3.4 %copy-start.10 = (f32[48,768]{1,0:T(8,128)S(1)}, f32[48,768]{1,0:T(8,128)}, u32[]{:S(2)}) copy-start(f32[48,768]{1,0:T(8,128)} %get-tuple-element.124) | copy-start | bytes 442372
  271.2 4.1 %copy-start.9 = (f32[48,768]{1,0:T(8,128)S(1)}, f32[48,768]{1,0:T(8,128)}, u32[]{:S(2)}) copy-start(f32[48,768]{1,0:T(8,128)} %get-tuple-element.126) | copy-start | bytes 442372
  271.2 4.8 %copy-start.8 = (f32[48,768]{1,0:T(8,128)S(1)}, f32[48,768]{1,0:T(8,128)}, u32[]{:S(2)}) copy-start(f32[48,768]{1,0:T(8,128)} %get-tuple-element.128) | copy-start | bytes 442372
  271.2 5.4 %copy-start.7 = (f32[48,3072]{1,0:T(8,128)S(1)}, f32[48,3072]{1,0:T(8,128)}, u32[]{:S(2)}) copy-start(f32[48,3072]{1,0:T(8,128)} %get-tuple-element.132) | copy-start | bytes 1769476
  274.0 3.5 %copy-start.6 = (f32[192,768]{1,0:T(8,128)S(1)}, f32[192,768]{1,0:T(8,128)}, u32[]{:S(2)}) copy-start(f32[192,768]{1,0:T(8,128)} %get-tuple-element.134) | copy-start | bytes 1769476

commit v3 on v2

--- a/solution.py
+++ b/solution.py
@@ -17,6 +17,7 @@
 bf16 = jnp.bfloat16
 TAIL = 16
 DEPTH = 4
+AHEAD = 1
 
 
 def layer_norm(residual, norm_gain, norm_bias):
@@ -438,28 +439,26 @@
 def forward_kernel(
     scale, x_ref, wq_ref, wk_ref, wv_ref, wo_ref, win_ref, wdn_ref, bq_ref, bk_ref, bv_ref, bo_ref, g1_ref, o1_ref, bd_ref,
     g2_ref, o2_ref, bin_ref, ints_ref, len_ref,
-    q_ref, k_ref, v_ref, pq_ref, pk_ref, att_ref, den_ref, peak_ref, state_ref, sq_ref, fin_ref, fdn_ref, vec_ref,
-    omx_ref, mask_ref, onehot_ref, strad_ref, stradrow_ref, send_ref, total_ref, land_ref,
+    q_ref, k_ref, v_ref, pq_ref, pk_ref, att_ref, den_ref, peak_ref, state_ref, omx_ref, sq_ref, fin_ref, fdn_ref, vec_ref,
+    mask_ref, onehot_ref, strad_ref, stradrow_ref, send_ref, total_ref, land_ref,
     ssem, rsem, gs_sem, gr_sem, gl_sem, vs_sem, vr_sem,
 ):
     at = Place()
     pairs = q_ref.shape[0]
     blocks = []
     specs = [(w, sq_ref.at[n], 0, 768) for n, w in enumerate((wq_ref, wk_ref, wv_ref, wo_ref))]
-    specs += [(win_ref, fin_ref, 1536 * h, 1536) for h in range(2)]
-    half = wdn_ref.shape[0] // 2
-    specs += [(wdn_ref.at[pl.ds(half * h, half)], fdn_ref.at[:, :, :, pl.ds(half * h, half)], 0, 768) for h in range(2)]
+    specs += [(win_ref, fin_ref, 768 * h, 768) for h in range(4)]
+    specs += [(wdn_ref.at[pl.ds(48 * h, 48)], fdn_ref.at[:, :, :, pl.ds(48 * h, 48)], 0, 768) for h in range(4)]
     for n, (own, full, base, width) in enumerate(specs):
         blocks.append(Gather(at, own, full, base, width, gs_sem.at[n], gr_sem.at[n], gl_sem.at[n]))
-    bq, bk, bv, bo, bi0, bi1, bd0, bd1 = blocks
     peer_barrier(at.peers())
     vec = SmallSum(at, total_ref, land_ref, vs_sem, vr_sem, False)
     total_ref[0] = spread_vectors(
         at, (bq_ref, bk_ref, bv_ref, bo_ref, g1_ref, o1_ref, bd_ref, g2_ref, o2_ref), bin_ref
     ).astype(bf16)
-    bq.begin()
+    blocks[0].begin()
     vec.begin()
-    for b in blocks[1:]:
+    for b in blocks[1:AHEAD]:
         b.begin()
     doc_setup(len_ref, at.y, mask_ref, onehot_ref, strad_ref, stradrow_ref)
     features_setup(ints_ref, omx_ref)
@@ -472,76 +471,58 @@
             o_ref[2 * j] = got[:, 0:128]
             o_ref[2 * j + 1] = got[:, 128:256]
 
-    bq.stage_x()
-    vec.step(0)
-    bk.stage_x()
-    bq.stage_y()
-    vec.step(1)
-    bv.stage_x()
-    bk.stage_y()
-    bq.stage_c()
-    vec.step(2)
+    def tick(t):
+        if t + AHEAD < len(blocks):
+            blocks[t + AHEAD].begin()
+        for k, name in enumerate(("stage_x", "stage_y", "stage_c", "ready")):
+            if 0 <= t - k < len(blocks):
+                getattr(blocks[t - k], name)()
+
+    for t in range(3):
+        tick(t)
+        vec.step(t)
     vec_ref[...] = vec.result()
-    bo.stage_x()
-    bv.stage_y()
-    bk.stage_c()
-    bq.ready()
-    project(0, q_ref)
-    bv.stage_c()
-    bk.ready()
-    project(1, k_ref)
-    bo.stage_y()
-    bv.ready()
-    project(2, v_ref)
+    for n, ref in enumerate((q_ref, k_ref, v_ref)):
+        tick(3 + n)
+        project(n, ref)
 
     def copy(p):
         return remote(send_ref.at[p], state_ref.at[p], ssem.at[p], rsem.at[p], at.across)
 
-    early = {0: [bi0.stage_x], 2: [bo.stage_c, bi0.stage_y], 4: [bi1.stage_x], 5: [bi0.stage_c]}
-    late = {0: [bi1.stage_y], 1: [bo.ready], 2: [bd0.stage_x, bi0.ready], 3: [bi1.stage_c], 4: [bd0.stage_y], 5: [bd1.stage_x]}
+    early = {0: 6, 2: 7, 4: 8}
+    late = {0: 9, 1: 10, 2: 11, 3: 12, 4: 13, 5: 14}
 
     @pl.loop(0, pairs)
     def _(p):
         forward_states(p, scale, q_ref, k_ref, v_ref, omx_ref, onehot_ref, strad_ref, stradrow_ref, pq_ref, pk_ref, peak_ref, send_ref)
         copy(p).start()
-        for n, todo in early.items():
+        for n, t in early.items():
             @pl.when(p == n)
-            def _(todo=todo):
-                for one in todo:
-                    one()
+            def _(t=t):
+                tick(t)
 
     @pl.loop(0, pairs)
     def _(p):
         copy(p).wait()
         forward_finish(p, scale, v_ref, pq_ref, pk_ref, mask_ref, strad_ref, peak_ref, state_ref, att_ref, den_ref)
-        for n, todo in late.items():
+        for n, t in late.items():
             @pl.when(p == n)
-            def _(todo=todo):
-                for one in todo:
-                    one()
-
-    bd0.stage_c()
-    bd1.stage_y()
-    bi1.ready()
-    bd1.stage_c()
-    bd0.ready()
-    bd1.ready()
+            def _(t=t):
+                tick(t)
+
     for b in blocks:
         b.drain()
     vec.drain()
 
 
 class Scatter:
-    def __init__(self, at, n, flip, source, acc, twin_in, wide_in, half_in, deep_in, done, done_in, put, ssem, rsem, lsem):
-        self.at, self.n, self.flip, self.source, self.acc = at, n, flip, source, acc
-        self.twin_in, self.wide_in, self.half_in, self.deep_in = twin_in, wide_in, half_in, deep_in
+    def __init__(self, at, order, source, twin_in, lands, done, done_in, put, ssem, rsem):
+        self.at, self.order, self.source, self.acc = at, order, source, source(at.c)
+        self.twin_in, self.lands = twin_in, lands
         self.done, self.done_in, self.put = done, done_in, put
-        self.ssem, self.rsem, self.lsem = ssem, rsem, lsem
-        self.half = acc.shape[-1] // 2
+        self.ssem, self.rsem = ssem, rsem
+        self.half = twin_in.shape[-1] // 2
         self.sent = []
-
-    def side(self, y):
-        return cols_at(self.half * y, self.half)
 
     def go(self, n, ends):
         src, dst, peer = ends()
@@ -551,68 +532,88 @@
     def came(self, n, ref):
         remote(ref, ref, self.ssem.at[n], self.rsem.at[n], self.at.twin).wait_recv()
 
-    def local(self):
-        return pltpu.make_async_copy(self.source(self.at.c), self.acc, self.lsem)
+    def side(self, y):
+        return cols_at(self.half * y, self.half)
+
+    def spot(self, fixed, **other):
+        at = self.at
+        z = other.get("z", at.z if "z" in fixed else slice(None))
+        x = other.get("x", at.x if "x" in fixed else slice(None))
+        cols = self.side(other.get("y", at.y)) if "y" in fixed or "y" in other else slice(None)
+        return z, x, slice(None), cols
+
+    def first(self, i):
+        return 1 + sum(DEPTH - 1 if kind == "z" else 1 for kind in self.order[:i])
+
+    def send(self, i):
+        at, kind, fixed = self.at, self.order[i], self.order[:i]
+        if kind == "z":
+            for d in range(1, DEPTH):
+                self.go(
+                    self.first(i) + d - 1,
+                    lambda d=d: (self.acc.at[self.spot(fixed, z=at.other(d))], self.lands[i].at[d - 1], at.along(d)),
+                )
+        elif kind == "x":
+            self.go(self.first(i), lambda: (self.acc.at[self.spot(fixed, x=1 - at.x)], self.lands[i], at.beside))
+        else:
+            self.go(self.first(i), lambda: (self.acc.at[self.spot(fixed, y=1 - at.y)], self.lands[i], at.across))
+
+    def add(self, parts, fixed, store):
+        def at_z(z):
+            for x in [None] if "x" in fixed else range(2):
+                spot = list(self.spot(fixed))
+                inner = ()
+                if z is not None:
+                    spot[0] = z
+                    inner += (z,)
+                if x is not None:
+                    spot[1] = x
+                    inner += (x,)
+                value = self.acc[tuple(spot)].astype(f32)
+                for part in parts:
+                    value = value + part[inner + (slice(None), slice(None))].astype(f32)
+                store(tuple(spot), value)
+
+        if "z" in fixed:
+            at_z(None)
+        else:
+            pl.loop(0, DEPTH)(at_z)
+
+    def keep(self, spot, value):
+        self.acc[spot] = value.astype(bf16)
+
+    def finish(self, spot, value):
+        low = value.astype(bf16)
+        self.done[...] = low
+        self.put(self.at.y, low.astype(f32))
+
+    def arrived(self, i):
+        if self.order[i] != "z":
+            self.came(self.first(i), self.lands[i])
+            return [self.lands[i]]
+        for d in range(1, DEPTH):
+            self.came(self.first(i) + d - 1, self.lands[i].at[d - 1])
+        return [self.lands[i].at[d - 1] for d in range(1, DEPTH)]
 
     def begin(self):
         self.go(0, lambda: (self.source(1 - self.at.c), self.twin_in, self.at.twin))
-        self.local().start()
 
     def stage_1(self):
-        at = self.at
-        self.local().wait()
         self.came(0, self.twin_in)
-
-        @pl.loop(0, DEPTH)
-        def _(z):
-            for x in range(2):
-                self.acc[z, x] = (self.acc[z, x].astype(f32) + self.twin_in[z, x].astype(f32)).astype(bf16)
-
-        if self.flip:
-            self.go(1, lambda: (self.acc.at[:, :, :, self.side(1 - at.y)], self.wide_in, at.across))
-        else:
-            self.go(1, lambda: (self.acc.at[:, 1 - at.x], self.wide_in, at.beside))
+        self.add([self.twin_in], "", self.keep)
+        self.send(0)
 
     def stage_2(self):
-        at = self.at
-        self.came(1, self.wide_in)
-
-        @pl.loop(0, DEPTH)
-        def _(z):
-            if self.flip:
-                for x in range(2):
-                    spot = (z, x, slice(None), self.side(at.y))
-                    self.acc[spot] = (self.acc[spot].astype(f32) + self.wide_in[z, x].astype(f32)).astype(bf16)
-            else:
-                self.acc[z, at.x] = (self.acc[z, at.x].astype(f32) + self.wide_in[z].astype(f32)).astype(bf16)
-
-        if self.flip:
-            self.go(2, lambda: (self.acc.at[:, 1 - at.x, :, self.side(at.y)], self.half_in, at.beside))
-        else:
-            self.go(2, lambda: (self.acc.at[:, at.x, :, self.side(1 - at.y)], self.half_in, at.across))
+        self.add(self.arrived(0), self.order[:1], self.keep)
+        self.send(1)
 
     def stage_3(self):
-        at = self.at
-        self.came(2, self.half_in)
-
-        @pl.loop(0, DEPTH)
-        def _(z):
-            spot = (z, at.x, slice(None), self.side(at.y))
-            self.acc[spot] = (self.acc[spot].astype(f32) + self.half_in[z].astype(f32)).astype(bf16)
-
-        for d in range(1, DEPTH):
-            self.go(2 + d, lambda d=d: (self.acc.at[at.other(d), at.x, :, self.side(at.y)], self.deep_in.at[d - 1], at.along(d)))
+        self.add(self.arrived(1), self.order[:2], self.keep)
+        self.send(2)
 
     def stage_4(self):
-        at = self.at
-        value = self.acc[at.z, at.x, :, self.side(at.y)].astype(f32)
-        for d in range(1, DEPTH):
-            self.came(2 + d, self.deep_in.at[d - 1])
-            value = value + self.deep_in[d - 1].astype(f32)
-        low = value.astype(bf16)
-        self.done[...] = low
-        self.put(at.y, low.astype(f32))
-        self.go(2 + DEPTH, lambda: (self.done, self.done_in, at.across))
+        self.add(self.arrived(2), self.order, self.finish)
+        self.go(2 + DEPTH, lambda: (self.done, self.done_in, self.at.across))
 
     def stage_5(self):
         self.came(2 + DEPTH, self.done_in)
@@ -624,21 +625,39 @@
             remote(src, dst, self.ssem.at[n], self.rsem.at[n], peer).wait_send()
 
 
+def landing(order, part, width):
+    shapes = []
+    for i, kind in enumerate(order):
+        kept = order[: i + 1]
+        shape = [] if "z" in kept else [DEPTH]
+        shape += [] if "x" in kept else [2]
+        shape += [part, width // 2 if "y" in kept else width]
+        shapes.append(pltpu.VMEM(tuple([DEPTH - 1] + shape if kind == "z" else shape), bf16))
+    return shapes
+
+
 SCATTER_COPIES = DEPTH + 3
-FLIPS = (False, True, False, True, False, True, False, True, False, True, False, True)
+FEED_STEPS = (3, 7)
+HEAD_STEPS = (0, 1, 2, 3, 4, 5)
+PACE = ((0, 2, 4, 6, 8),) * 6 + ((0, 2, 3, 4, 5),) * 3 + ((0, 1, 2, 3, 4),) * 3
+ORDERS = ("xyz", "yxz") * 6
 
 
 def backward_kernel(
-    scale, x_ref, q_ref, k_ref, v_ref, pq_ref, pk_ref, att_ref, den_ref, peak_ref, state_ref, sq_ref, gatt_ref, gres_ref,
-    vecin_ref, ints_ref, len_ref, gdn_ref, gin_ref, go_ref,
+    scale, x_ref, q_ref, k_ref, v_ref, pq_ref, pk_ref, att_ref, den_ref, peak_ref, state_ref, omx_ref, hid_ref, norm_ref,
+    inv_ref, res_ref, gain_ref, vecin_ref, len_ref, gel_ref, slope_ref, win_ref, wdn_ref, sq_ref,
     gx_ref, oq_ref, ok_ref, ov_ref, oo_ref, oin_ref, odn_ref, vec_ref,
-    gstate_ref, omx_ref, mask_ref, onehot_ref, strad_ref, stradrow_ref, send_ref,
-    xt_ref, gq_ref, gk_ref, gv_ref, gw_ref, total_ref, land_ref,
-    acc_ref, twin_ref, wide0_ref, wide1_ref, half_ref, deep_ref, done_ref, donein_ref,
-    ssem, rsem, ws_sem, wr_sem, wl_sem, vs_sem, vr_sem,
+    gstate_ref, mask_ref, onehot_ref, strad_ref, stradrow_ref, send_ref,
+    xt_ref, gq_ref, gk_ref, gv_ref, gatt_ref, low_ref, wide_ref, gelbuf_ref, slopebuf_ref,
+    gdn_ref, gin_ref, go_ref, gw_ref, total_ref, land_ref,
+    twin_ref, done_ref, donein_ref,
+    ssem, rsem, load_sem, late_sem, ws_sem, wr_sem, vs_sem, vr_sem, *land_refs,
 ):
     at = Place()
     pairs = q_ref.shape[0]
+    rows, width = x_ref.shape
+    span = width // 2
+    chunks = win_ref.shape[1] // span
     sources = [lambda c, b=b: gdn_ref.at[:, :, c, pl.ds(48 * b, 48)] for b in range(4)]
     sources += [lambda c, b=b: gin_ref.at[:, :, c, :, pl.ds(768 * b, 768)] for b in range(4)]
     sources += [lambda c: go_ref.at[:, :, c]]
@@ -654,26 +673,139 @@
     puts += [putter(r, 0, 0) for r in (oo_ref, ov_ref, ok_ref, oq_ref)]
     units = []
     for n, (source, put) in enumerate(zip(sources, puts)):
-        wide = wide1_ref.at[n // 2] if FLIPS[n] else wide0_ref.at[n // 2]
+        lands = land_refs[3 * n : 3 * n + 3]
         units.append(
             Scatter(
-                at, n, FLIPS[n], source, acc_ref.at[n], twin_ref.at[n], wide, half_ref.at[n], deep_ref.at[n],
-                done_ref.at[n], donein_ref.at[n], put, ws_sem.at[n], wr_sem.at[n], wl_sem.at[n],
+                at, ORDERS[n], source, twin_ref.at[n], lands, done_ref.at[n], donein_ref.at[n], put, ws_sem.at[n], wr_sem.at[n]
             )
         )
     early = len(units) - 3
 
     def step(s):
         for k in range(5):
-            u = s - k
-            if 0 <= u < len(units):
-                getattr(units[u], "stage_" + str(k + 1))()
+            for u, unit in enumerate(units):
+                if u + PACE[u][k] == s:
+                    getattr(unit, "stage_" + str(k + 1))()
+
+
+    def load(src, dst, sem):
+        return pltpu.make_async_copy(src, dst, sem)
+
+    def slot(m):
+        return lax.rem(m, 2)
+
+    def load_gelu(m):
+        return load(gel_ref.at[:, cols_at(span * m, span)], gelbuf_ref.at[slot(m)], load_sem.at[0, slot(m)])
+
+    def load_chunk(m):
+        start = pl.multiple_of(span * slot(m), 128)
+        return [
+            load(slope_ref.at[:, cols_at(span * m, span)], slopebuf_ref.at[slot(m)], load_sem.at[1, slot(m)]),
+            load(wdn_ref.at[pl.ds(pl.multiple_of(span * m, 128), span)], wide_ref.at[0, pl.ds(start, span)], load_sem.at[2, slot(m)]),
+            load(win_ref.at[:, cols_at(span * m, span)], wide_ref.at[1, :, pl.ds(start, span)], load_sem.at[3, slot(m)]),
+        ]
+
+    def load_square(n, to):
+        return load(sq_ref.at[n], wide_ref.at[to], late_sem.at[to])
 
     peer_barrier(at.peers())
-    for u in units[:early]:
-        u.begin()
+    load_gelu(jnp.int32(0)).start()
+    for one in load_chunk(jnp.int32(0)):
+        one.start()
+    load_square(3, 2).start()
+    total_ref[0] = vecin_ref[...]
+
+    @pl.loop(0, rows // 128)
+    def _(r):
+        here = pl.ds(pl.multiple_of(128 * r, 128), 128)
+        low_ref[here] = res_ref[here].astype(bf16)
+        gx_ref[here] = res_ref[here]
+
+
+    @pl.loop(0, chunks)
+    def _(m):
+        load_gelu(m).wait()
+
+        @pl.when(m < chunks - 1)
+        def _():
+            load_gelu(m + 1).start()
+
+        turned = gelbuf_ref[slot(m)].T
+        for n in range(3):
+            cols = slice(256 * n, 256 * n + 256)
+            got = mul(turned, low_ref[:, cols]).astype(bf16)
+            gdn_ref[lax.div(m, 2), slot(m), :, :, cols] = got.reshape(2, span // 2, 256)
+
+    units[0].begin()
+    units[1].begin()
+    for j in range(pairs):
+        xt_ref[128 * j : 128 * j + 128] = hid_ref[:, 128 * j : 128 * j + 128].T
+
+    @pl.loop(0, chunks)
+    def _(m):
+        for one in load_chunk(m):
+            one.wait()
+
+        @pl.when(m < chunks - 1)
+        def _():
+            for one in load_chunk(m + 1):
+                one.start()
+
+        start = pl.multiple_of(span * slot(m), 128)
+        gpre = mul_tb(low_ref[...], wide_ref[0, pl.ds(start, span)]) * slopebuf_ref[slot(m)].astype(f32)
+        gpre = gpre.astype(bf16)
+        total_ref[0, pl.ds(9 + lax.div(m, 2), 1), cols_at(start, span)] = jnp.sum(gpre.astype(f32), axis=0, keepdims=True)
+        got = mul(xt_ref[...], gpre).astype(bf16)
+        gin_ref[:, :, :, :, cols_at(span * m, span)] = got.reshape(DEPTH, 2, 2, 48, span)
+        for n in range(3):
+            cols = slice(256 * n, 256 * n + 256)
+            gx_ref[:, cols] = gx_ref[:, cols] + mul_tb(gpre, wide_ref[1, cols, pl.ds(start, span)])
+        for n in range(8):
+            @pl.when(m == n)
+            def _(n=n):
+                if n < 2:
+                    units[2 + n].begin()
+                if n % 2:
+                    units[4 + n // 2].begin()
+                if n in FEED_STEPS:
+                    step(FEED_STEPS.index(n))
+
+    done_steps = len(FEED_STEPS)
+
+    @pl.loop(0, rows // 128)
+    def _(r):
+        here = pl.ds(pl.multiple_of(128 * r, 128), 128)
+        grad = gx_ref[here]
+        normed = norm_ref[here].astype(f32)
+        scaled = grad * gain_ref[...]
+        centre = jnp.mean(scaled, axis=1, keepdims=True)
+        slope = jnp.mean(scaled * normed, axis=1, keepdims=True)
+        resid = inv_ref[here] * (scaled - centre - normed * slope)
+        gx_ref[here] = resid
+        low = resid.astype(bf16)
+        low_ref[here] = low
+        total_ref[0, 3:4] = total_ref[0, 3:4] + jnp.sum(low.astype(f32), axis=0, keepdims=True)
+        total_ref[0, 4:5] = total_ref[0, 4:5] + jnp.sum(grad * normed, axis=0, keepdims=True)
+        total_ref[0, 5:6] = total_ref[0, 5:6] + jnp.sum(grad, axis=0, keepdims=True)
+
+    load_square(3, 2).wait()
+    for h in range(2):
+        turned = jnp.concatenate([att_ref[3 * h + i].T for i in range(3)], axis=0)
+        for n in range(3):
+            cols = slice(256 * n, 256 * n + 256)
+            go_ref[2 * h : 2 * h + 2, :, :, :, cols] = mul(turned, low_ref[:, cols]).astype(bf16).reshape(2, 2, 2, 48, 256)
+    units[8].begin()
+    for j in range(pairs // 2):
+        got = mul_tb(low_ref[...], wide_ref[2, 256 * j : 256 * j + 256]).astype(bf16)
+        gatt_ref[2 * j] = got[:, 0:128]
+        gatt_ref[2 * j + 1] = got[:, 128:256]
+    for n in range(3):
+        load_square(n, n).start()
+    step(done_steps)
+    done_steps += 1
+
+
     doc_setup(len_ref, at.y, mask_ref, onehot_ref, strad_ref, stradrow_ref)
-    features_setup(ints_ref, omx_ref)
 
     def copy(p):
         return remote(send_ref.at[p], gstate_ref.at[p], ssem.at[p], rsem.at[p], at.across)
@@ -682,14 +814,9 @@
     def _(p):
         backward_states(p, scale, att_ref, den_ref, gatt_ref, pq_ref, strad_ref, peak_ref, state_ref, send_ref)
         copy(p).start()
-        for n, s in ((2, 0), (5, 1)):
-            @pl.when(p == n)
-            def _(s=s):
-                step(s)
 
     for j in range(pairs):
         xt_ref[128 * j : 128 * j + 128] = x_ref[:, 128 * j : 128 * j + 128].T
-    total_ref[0] = vecin_ref[...]
 
     @pl.loop(0, pairs)
     def _(p):
@@ -705,41 +832,36 @@
         gw_ref[2, :, :, :, :, cols] = mul(xt_ref[...], gv_ref[p]).astype(bf16).reshape(DEPTH, 2, 2, 48, 128)
         for n, ref in enumerate((gq_ref, gk_ref, gv_ref)):
             total_ref[0, n : n + 1, cols] = jnp.sum(ref[p].astype(f32), axis=0, keepdims=True)
-        for n in range(6):
-            @pl.when(p == n)
+        for n, at_pair in enumerate(HEAD_STEPS):
+            @pl.when(p == at_pair)
             def _(n=n):
-                step(n + 2)
+                step(n + done_steps)
 
     vec = SmallSum(at, total_ref, land_ref, vs_sem, vr_sem, True)
     vec.begin()
     for u in units[early:]:
         u.begin()
-    step(8)
+    for n in range(3):
+        load_square(n, n).wait()
 
     def grad_input(j):
         cols = slice(256 * j, 256 * j + 256)
-        value = gres_ref[:, cols]
+        value = gx_ref[:, cols]
         for n, ref in enumerate((gq_ref, gk_ref, gv_ref)):
             for i in range(pairs // 2):
                 left = jnp.concatenate([ref[2 * i], ref[2 * i + 1]], axis=1)
-                right = sq_ref[n, 256 * j : 256 * j + 256, 256 * i : 256 * i + 256]
+                right = wide_ref[n, 256 * j : 256 * j + 256, 256 * i : 256 * i + 256]
                 value = value + mul_tb(left, right)
         gx_ref[:, cols] = value
 
-    step(9)
-    vec.step(0)
-    grad_input(0)
-    step(10)
-    vec.step(1)
-    grad_input(1)
-    step(11)
-    vec.step(2)
-    grad_input(2)
-    step(12)
-    vec.step(3)
+    done_steps += len(HEAD_STEPS)
+    for n, s in enumerate(range(done_steps, len(units) + PACE[-1][-1])):
+        step(s)
+        if n < 4:
+            vec.step(n)
+        if n < 3:
+            grad_input(n)
     vec_ref[...] = vec.result()
-    for s in range(13, 16):
-        step(s)
     for u in units:
         u.drain()
     vec.drain()
@@ -783,19 +905,19 @@
             shape((pairs, rows, 128), bf16), shape((pairs, rows, 128), bf16), shape((pairs, rows, 128), bf16),
             shape((pairs, 2, rows, feats), bf16), shape((pairs, 2, rows, feats), bf16),
             shape((pairs, rows, 128), bf16), shape((pairs, rows, 128), f32),
-            shape((pairs, 2, 1, feats), f32), shape((pairs, 128 + TAIL, feats), bf16),
+            shape((pairs, 2, 1, feats), f32), shape((pairs, 128 + TAIL, feats), bf16), shape((heads, 256, feats), bf16),
             shape((4, *grid, part, width), bf16),
             shape((*grid, part, hidden), bf16), shape((*grid, weights[5].shape[0], width), bf16),
             shape((16, width), bf16),
         ],
         in_specs=[vmem()] * 18 + [smem()],
-        out_specs=[vmem()] * 10 + [anywhere()] * 2 + [vmem()],
-        scratch_shapes=scratch_masks(rows, heads, feats) + [
+        out_specs=[vmem()] * 11 + [anywhere()] * 2 + [vmem()],
+        scratch_shapes=scratch_masks(rows, heads, feats)[1:] + [
             pltpu.VMEM((pairs, 128 + TAIL, feats), bf16),
             pltpu.VMEM((4, 16, width), bf16),
             pltpu.VMEM((DEPTH + 1, 16, width), bf16),
             dma((pairs,)), dma((pairs,)),
-            dma((8, GATHER_COPIES)), dma((8, GATHER_COPIES)), dma((8,)),
+            dma((12, GATHER_COPIES)), dma((12, GATHER_COPIES)), dma((12,)),
             dma((DEPTH + 1,)), dma((DEPTH + 1,)),
         ],
         compiler_params=pltpu.CompilerParams(collective_id=0, has_side_effects=True, vmem_limit_bytes=60 << 20),
@@ -803,49 +925,49 @@
     )(x, *weights, *vectors, ints, lengths)
 
 
-def attention_backward(x, saved, gatt, gres, vec, ints, lengths, gdn, gin, go):
+def attention_backward(x, saved, hidden_low, normed, inverse, grad_resid, gain, vec, lengths, gelu_low, slope, win, wdn, square):
     rows, width = x.shape
-    heads, size, feats = ints.shape
-    pairs = heads // 2
-    scale = size ** (-0.25) * unit_spread
+    pairs, _, _, feats = saved[3].shape
+    heads, hidden = 2 * pairs, win.shape[1]
+    scale = (width // heads) ** (-0.25) * unit_spread
     shape = jax.ShapeDtypeStruct
     dma = pltpu.SemaphoreType.DMA
     grid = (DEPTH, 2, 2)
     part = width // 16
-    hidden = gin.shape[1]
     units = 12
-    gdn = gdn.reshape(*grid, -1, width)
-    gin = gin.reshape(*grid, part, hidden)
-    go = go.reshape(*grid, part, width)
     return pl.pallas_call(
         partial(backward_kernel, scale),
         out_shape=[shape((rows, width), f32)]
         + [shape((part, width), f32)] * 4
         + [shape((part, hidden), f32), shape((hidden // 16, width), f32), shape((16, width), f32)],
-        in_specs=[vmem()] * 15 + [smem()] + [anywhere()] * 3,
+        in_specs=[vmem()] * 17 + [smem()] + [anywhere()] * 5,
         out_specs=[vmem()] * 8,
-        scratch_shapes=[pltpu.VMEM((pairs, 128 + TAIL, feats), bf16)] + scratch_masks(rows, heads, feats) + [
+        scratch_shapes=[pltpu.VMEM((pairs, 128 + TAIL, feats), bf16)] + scratch_masks(rows, heads, feats)[1:] + [
             pltpu.VMEM((pairs, 128 + TAIL, feats), bf16),
             pltpu.VMEM((width, rows), bf16),
             pltpu.VMEM((pairs, rows, 128), bf16), pltpu.VMEM((pairs, rows, 128), bf16), pltpu.VMEM((pairs, rows, 128), bf16),
+            pltpu.VMEM((pairs, rows, 128), bf16),
+            pltpu.VMEM((rows, width), bf16),
+            pltpu.VMEM((3, width, width), bf16),
+            pltpu.VMEM((2, rows, width // 2), bf16), pltpu.VMEM((2, rows, width // 2), bf16),
+            pltpu.VMEM((*grid, hidden // 16, width), bf16),
+            pltpu.VMEM((*grid, part, hidden), bf16),
+            pltpu.VMEM((*grid, part, width), bf16),
             pltpu.VMEM((3, *grid, part, width), bf16),
             pltpu.VMEM((5, 16, width), f32),
             pltpu.VMEM((DEPTH + 2, 16, width), f32),
             pltpu.VMEM((units, DEPTH, 2, part, width), bf16),
-            pltpu.VMEM((units, DEPTH, 2, part, width), bf16),
-            pltpu.VMEM((units // 2, DEPTH, part, width), bf16),
-            pltpu.VMEM((units // 2, DEPTH, 2, part, width // 2), bf16),
-            pltpu.VMEM((units, DEPTH, part, width // 2), bf16),
-            pltpu.VMEM((units, DEPTH - 1, part, width // 2), bf16),
             pltpu.VMEM((units, part, width // 2), bf16),
             pltpu.VMEM((units, part, width // 2), bf16),
-            dma((pairs,)), dma((pairs,)),
-            dma((units, SCATTER_COPIES)), dma((units, SCATTER_COPIES)), dma((units,)),
+            dma((pairs,)), dma((pairs,)), dma((4, 2)), dma((3,)),
+            dma((units, SCATTER_COPIES)), dma((units, SCATTER_COPIES)),
             dma((DEPTH + 2,)), dma((DEPTH + 2,)),
-        ],
-        compiler_params=pltpu.CompilerParams(collective_id=1, has_side_effects=True, vmem_limit_bytes=63 << 20),
+        ] + [land for order in ORDERS for land in landing(order, part, width)],
+        compiler_params=pltpu.CompilerParams(collective_id=1, has_side_effects=True, vmem_limit_bytes=65200 << 10),
         name="attention_backward",
-    )(x, *saved, gatt, gres, vec, ints, lengths, gdn, gin, go)
+    )(
+        x, *saved, hidden_low, normed, inverse, grad_resid, gain, vec, lengths, gelu_low, slope, win, wdn, square
+    )
 
 
 def to_pairs(rows):
@@ -881,32 +1003,19 @@
     hidden_low = hidden_wide.astype(bf16)
     pre_act = affine(hidden_low, in_weight, in_bias)
     gelu_low = gelu_value(pre_act).astype(bf16)
+    slope_low = gelu_slope(pre_act).astype(bf16)
     residual_two = hidden_low.astype(f32) + affine(gelu_low, down_weight, down_bias)
     layer_wide, normed_two, inverse_two = layer_norm(residual_two, gain_two, offset_two)
     grad_out = cotangent[0].astype(f32)
     grad_resid_two, grad_gain_two, grad_offset_two = norm_back(grad_out, normed_two, inverse_two, gain_two)
-    grad_down_low = grad_resid_two.astype(bf16)
-    grad_down_weight = mul_ta(gelu_low, grad_down_low).astype(bf16)
-    grad_down_bias = column_total(grad_down_low)
-    grad_pre_low = (mul_tb(grad_down_low, down_weight) * gelu_slope(pre_act)).astype(bf16)
-    grad_in_weight = mul_ta(hidden_low, grad_pre_low).astype(bf16)
-    grad_in_bias = column_total(grad_pre_low)
-    grad_hidden = mul_tb(grad_pre_low, in_weight) + grad_resid_two
-    grad_resid_one, grad_gain_one, grad_offset_one = norm_back(grad_hidden, normed_one, inverse_one, gain_one)
-    grad_proj_low = grad_resid_one.astype(bf16)
-    grad_out_weight = mul_ta(att_rows, grad_proj_low).astype(bf16)
-    grad_out_bias = column_total(grad_proj_low)
-    grad_att_rows = mul_tb(grad_proj_low, out_weight).astype(bf16)
-    nothing = jnp.zeros((width,), f32)
-    sums = jnp.stack(
-        [
-            nothing, nothing, nothing, grad_out_bias, grad_gain_one, grad_offset_one, grad_down_bias, grad_gain_two,
-            grad_offset_two, *grad_in_bias.reshape(-1, width), nothing, nothing, nothing,
-        ]
+    grad_down_bias = column_total(grad_resid_two.astype(bf16))
+    nothing = jnp.zeros((6, width), f32)
+    sums = jnp.concatenate(
+        [nothing, jnp.stack([grad_down_bias, grad_gain_two, grad_offset_two]), nothing, nothing[0:1]], axis=0
     )
     grad_input, gq, gk, gv, go, gin, gdn, sums = attention_backward(
-        row_block, (*saved, square), to_pairs(grad_att_rows), grad_resid_one, sums, feature_ints, doc_lengths,
-        grad_down_weight, grad_in_weight, grad_out_weight,
+        row_block, saved, hidden_low, normed_one.astype(bf16), inverse_one, grad_resid_two, gain_one.astype(f32)[None],
+        sums, doc_lengths, gelu_low, slope_low, in_weight, down_weight, square,
     )
     part = b_query.shape[0]
     wide = b_in.shape[0]

time: 279 us -> 244 us (0.87)
  matrix products: 31 us -> 10 us
  Pallas kernels: 220 us -> 208 us
  local copies, waits for them, and re-layouts: 21.4 us -> 16 us
    dot_general x6 -> x0, matrix products: 23.9 us -> none  [the longest x3 14 us: mul_ta(): lax.dot_general(a, b, (((0,), (0,)), ((), ())), preferred_element_type=f32)]
    pallas_call x1, Pallas kernels: 105 us -> 89.4 us  [attention_forward(): pl.pallas_call(partial(forward_kernel, scale), out_shape=[shape((pairs, r...]
    pallas_call x1, Pallas kernels: 115 us -> 119 us  [attention_backward(): pl.pallas_call(partial(backward_kernel, scale), out_shape=[shape((rows, w...]
    dot_general x3, matrix products: 7.1 us -> 10 us  [mul(): lax.dot_general(a, b, (((1,), (0,)), ((), ())), preferred_element_type=f32)]
    unnamed x43 -> x35, local copies, waits for them, and re-layouts: 9.56 us -> 7.88 us
where the time goes in v3:
time: 244 us; the launch traced here: 243 us
  Pallas kernels  208 us (85%)
  local copies, waits for them, and re-layouts  16 us (7%)
  matrix products  10 us (4%)
  other arithmetic  7.85 us (3%)
    pallas_call x1, Pallas kernels, attention_backward(): pl.pallas_call(partial(backward_kernel, scale), out_shape=[shape((rows, w...  119 us
    pallas_call x1, Pallas kernels, attention_forward(): pl.pallas_call(partial(forward_kernel, scale), out_shape=[shape((pairs, r...  89.4 us
    dot_general x3, matrix products, mul(): lax.dot_general(a, b, (((1,), (0,)), ((), ())), preferred_element_type=f32)  10 us
    unnamed x35, local copies, waits for them, and re-layouts  7.88 us

profile of v3, /device:TPU:0, one launch (start us, length us, event | category | flops | bytes accessed | tf_op | source)
XLA Modules:
  0.0 242.7 jit_solution(5037838578161221284)
XLA Ops:
  0.7 89.4 %attention_forward.1 = (bf16[6,512,128]{2,1,0:T(8,128)(2,1)}, bf16[6,512,128]{2,1,0:T(8,128)(2,1)}, bf16[6,512,128]{2,1,0:T(8,128)(2,1)}, bf16[6,2,512,256]{3,2,...) custom-call(bf16[512,768]{1,0:T(8,128)(2,1)} %bitcast.66, ...), custom_call_target="tpu_custom_call" | custom-call | tf_op jit(solution)/shard_map/attention_forward/pallas_call | solution.py:902
  90.1 1.0 convert_reduce_fusion.3
  91.1 0.7 slice_convert_fusion
  91.8 1.4 copy.38
  93.2 1.5 slice.58
  94.7 0.9 fusion.17
  96.0 1.2 multiply_convert_fusion.1
  97.3 6.4 %fusion.4 = (bf16[512,3072]{1,0:T(8,128)(2,1)}, bf16[512,3072]{1,0:T(8,128)(2,1)S(1)}) fusion(f32[3072]{0:T(1024)S(1)} %reshape.114, bf16[512,768]{1,0:T(8,128)(2,1)S(1)} %get-tuple-element.77.hid_ref, bf16[768,3072]{1,0:T(8,128)(2,1)S(1)} %bitcast.61), kind=kOutput, calls=%fused_computation.5 | convolution fusion | flops 2436366336 | bytes 11808768 | tf_op jit(solution)/shard_map/dot_general | solution.py:50
  103.7 2.7 %fusion.18 = (f32[512]{0:T(512)S(1)}, f32[512,768]{1,0:T(8,128)S(1)}) fusion(f32[768]{0:T(1024)S(1)} %get-tuple-element.68, bf16[512,3072]{1,0:T(8,128)(2,1)S(1)} %get-tuple-element.74.gel_ref, bf16[3072,768]{1,0:T(8,128)(2,1)S(1)} %bitcast.65, bf16[512,768]{1,0:T(8,128)(2,1)S(1)} %get-tuple-element.77.hid_ref), kind=kOutput, calls=%fused_computation.53 | convolution fusion | flops 2417491456 | bytes 10228736 | tf_op jit(solution)/shard_map/dot_general | solution.py:50
  106.7 0.8 copy-done
  107.5 0.8 fusion.13
  108.4 2.1 convert_reduce_fusion.1
  110.4 0.9 copy.39.inv_ref
  111.3 1.3 slice_convert_fusion.1.gain_ref
  112.8 1.3 concatenate.3.vecin_ref
  114.0 118.6 %attention_backward.1 = (f32[512,768]{1,0:T(8,128)}, f32[48,768]{1,0:T(8,128)}, f32[48,768]{1,0:T(8,128)}, f32[48,768]{1,0:T(8,128)}, f32[48,768]{1,0:T(8,128)},...) custom-call(bf16[512,768]{1,0:T(8,128)(2,1)} %bitcast.67, ...), custom_call_target="tpu_custom_call" | custom-call | tf_op jit(solution)/shard_map/attention_backward/pallas_call | solution.py:938
  232.6 1.6 dynamic-slice_bitcast_fusion
  234.3 0.7 slice.73
  235.7 2.7 %copy.47 = f32[1,512,768]{2,1,0:T(8,128)} copy(f32[1,512,768]{2,1,0:T(8,128)} %bitcast.69) | data formatting | bytes 3145728
  239.1 0.7 copy.49
  239.8 0.7 copy.50
  240.4 0.7 copy.51
  241.1 0.8 copy.52
  241.9 0.8 copy.53
  (46 shorter events, 2.2 us)
Async XLA Ops:
  93.2 1.5 copy-start.2
  93.2 4.1 %slice-start = ((s8[4718592]{0:T(1024)(128)(4,1)}), s8[4194304]{0:T(1024)(128)(4,1)S(1)}, s32[]{:S(2)}) async-start(s8[4718592]{0:T(1024)(128)(4,1)} %bitcast.59), calls=%async_computation | async-start | bytes 8388608
  94.7 2.5 %slice-start.1 = ((s8[4718592]{0:T(1024)(128)(4,1)}), s8[524288]{0:T(1024)(128)(4,1)S(1)}, s32[]{:S(2)}) async-start(s8[4718592]{0:T(1024)(128)(4,1)} %bitcast.59), calls=%async_computation.1 | async-start | bytes 1048576
  96.0 7.7 %slice-start.2 = ((s8[4718592]{0:T(1024)(128)(4,1)}), s8[4194304]{0:T(1024)(128)(4,1)S(1)}, s32[]{:S(2)}) async-start(s8[4718592]{0:T(1024)(128)(4,1)} %bitcast.63), calls=%async_computation.2 | async-start | bytes 8388608
  97.3 6.4 %copy-start.3 = (bf16[512,768]{1,0:T(8,128)(2,1)}, bf16[512,768]{1,0:T(8,128)(2,1)S(1)}, u32[]{:S(2)}) copy-start(bf16[512,768]{1,0:T(8,128)(2,1)S(1)} %get-tuple-element.77.hid_ref) | copy-start | bytes 2359300
  97.3 6.4 %slice-start.3 = ((s8[4718592]{0:T(1024)(128)(4,1)}), s8[524288]{0:T(1024)(128)(4,1)S(1)}, s32[]{:S(2)}) async-start(s8[4718592]{0:T(1024)(128)(4,1)} %bitcast.63), calls=%async_computation.3 | async-start | bytes 1048576
  103.7 2.7 %copy-start.1 = (bf16[512,3072]{1,0:T(8,128)(2,1)}, bf16[512,3072]{1,0:T(8,128)(2,1)S(1)}, u32[]{:S(2)}) copy-start(bf16[512,3072]{1,0:T(8,128)(2,1)S(1)} %get-tuple-element.74.gel_ref) | copy-start | bytes 9437188
  106.4 1.1 copy-start
  235.7 2.8 %copy-start.9 = (f32[48,768]{1,0:T(8,128)S(1)}, f32[48,768]{1,0:T(8,128)}, u32[]{:S(2)}) copy-start(f32[48,768]{1,0:T(8,128)} %get-tuple-element.113) | copy-start | bytes 442372
  235.7 3.4 %copy-start.8 = (f32[48,768]{1,0:T(8,128)S(1)}, f32[48,768]{1,0:T(8,128)}, u32[]{:S(2)}) copy-start(f32[48,768]{1,0:T(8,128)} %get-tuple-element.115) | copy-start | bytes 442372
  235.7 4.1 %copy-start.7 = (f32[48,768]{1,0:T(8,128)S(1)}, f32[48,768]{1,0:T(8,128)}, u32[]{:S(2)}) copy-start(f32[48,768]{1,0:T(8,128)} %get-tuple-element.117) | copy-start | bytes 442372
  235.7 4.8 %copy-start.6 = (f32[48,768]{1,0:T(8,128)S(1)}, f32[48,768]{1,0:T(8,128)}, u32[]{:S(2)}) copy-start(f32[48,768]{1,0:T(8,128)} %get-tuple-element.119) | copy-start | bytes 442372
  235.7 5.4 %copy-start.5 = (f32[48,3072]{1,0:T(8,128)S(1)}, f32[48,3072]{1,0:T(8,128)}, u32[]{:S(2)}) copy-start(f32[48,3072]{1,0:T(8,128)} %get-tuple-element.123) | copy-start | bytes 1769476
  238.4 3.5 %copy-start.4 = (f32[192,768]{1,0:T(8,128)S(1)}, f32[192,768]{1,0:T(8,128)}, u32[]{:S(2)}) copy-start(f32[192,768]{1,0:T(8,128)} %get-tuple-element.125) | copy-start | bytes 1769476

commit v4 on v3

--- a/solution.py
+++ b/solution.py
@@ -436,21 +436,43 @@
     return jnp.where(here == len(pieces) + at.z, row, rows)
 
 
+HOLD = (
+    "omx", "xt", "mask", "strad", "q", "k", "v", "pq", "pk", "att", "attt", "den", "sq", "hidt", "norm", "fin", "gelt", "slope", "fdn",
+)
+LATE = ("xt", "q", "k", "v", "pq", "pk", "att", "attt", "den", "omx", "mask", "strad")
+
+
 def forward_kernel(
     scale, x_ref, wq_ref, wk_ref, wv_ref, wo_ref, win_ref, wdn_ref, bq_ref, bk_ref, bv_ref, bo_ref, g1_ref, o1_ref, bd_ref,
-    g2_ref, o2_ref, bin_ref, ints_ref, len_ref,
-    q_ref, k_ref, v_ref, pq_ref, pk_ref, att_ref, den_ref, peak_ref, state_ref, omx_ref, sq_ref, fin_ref, fdn_ref, vec_ref,
-    mask_ref, onehot_ref, strad_ref, stradrow_ref, send_ref, total_ref, land_ref,
-    ssem, rsem, gs_sem, gr_sem, gl_sem, vs_sem, vr_sem,
+    g2_ref, o2_ref, bin_ref, ints_ref, cot_ref, len_ref, layer_ref, peak_ref, state_ref, inv_ref, res_ref, vec_ref, sums_ref, *rest,
 ):
+    outs, rest = rest[: len(HOLD)], rest[len(HOLD) :]
+    hold, rest = rest[: len(HOLD)], rest[len(HOLD) :]
+    (
+        omx_ref, xt_ref, mask_ref, strad_ref, q_ref, k_ref, v_ref, pq_ref, pk_ref, att_ref, attt_ref, den_ref, sq_ref, hidt_ref,
+        norm_ref, fin_ref, gelt_ref, slope_ref, fdn_ref,
+    ) = hold
+    hid_ref, gel_ref, onehot_ref, stradrow_ref, send_ref, total_ref, land_ref = rest[:7]
+    ssem, rsem, gs_sem, gr_sem, gl_sem, vs_sem, vr_sem, out_sem = rest[7:]
     at = Place()
     pairs = q_ref.shape[0]
+    rows, width = x_ref.shape
+
+    def stash(*names):
+        return [pltpu.make_async_copy(hold[n], outs[n], out_sem.at[n]) for n in map(HOLD.index, names)]
+
+    def give(*names):
+        for copy in stash(*names):
+            copy.start()
+
     blocks = []
     specs = [(w, sq_ref.at[n], 0, 768) for n, w in enumerate((wq_ref, wk_ref, wv_ref, wo_ref))]
     specs += [(win_ref, fin_ref, 768 * h, 768) for h in range(4)]
-    specs += [(wdn_ref.at[pl.ds(48 * h, 48)], fdn_ref.at[:, :, :, pl.ds(48 * h, 48)], 0, 768) for h in range(4)]
-    for n, (own, full, base, width) in enumerate(specs):
-        blocks.append(Gather(at, own, full, base, width, gs_sem.at[n], gr_sem.at[n], gl_sem.at[n]))
+    specs += [
+        (wdn_ref.at[pl.ds(96 * r, 96)], fdn_ref.at[:, :, :, pl.ds(96 * r, 96)], 384 * h, 384) for h in range(2) for r in range(2)
+    ]
+    for n, (own, full, base, span) in enumerate(specs):
+        blocks.append(Gather(at, own, full, base, span, gs_sem.at[n], gr_sem.at[n], gl_sem.at[n]))
     peer_barrier(at.peers())
     vec = SmallSum(at, total_ref, land_ref, vs_sem, vr_sem, False)
     total_ref[0] = spread_vectors(
@@ -462,12 +484,19 @@
         b.begin()
     doc_setup(len_ref, at.y, mask_ref, onehot_ref, strad_ref, stradrow_ref)
     features_setup(ints_ref, omx_ref)
+    for j in range(pairs):
+        xt_ref[128 * j : 128 * j + 128] = x_ref[:, 128 * j : 128 * j + 128].T
+    give("omx", "xt", "mask", "strad")
+    sums_ref[...] = jnp.zeros_like(sums_ref)
+
+    def vector(n, cols=slice(None)):
+        return vec_ref[n : n + 1, cols].astype(f32)
 
     def project(n, o_ref):
         for j in range(pairs // 2):
             cols = slice(256 * j, 256 * j + 256)
             got = mul(x_ref[...], sq_ref[n, :, :, :, :, cols].reshape(768, 256))
-            got = (got + vec_ref[n : n + 1, cols].astype(f32)).astype(bf16)
+            got = (got + vector(n, cols)).astype(bf16)
             o_ref[2 * j] = got[:, 0:128]
             o_ref[2 * j + 1] = got[:, 128:256]
 
@@ -485,34 +514,114 @@
     for n, ref in enumerate((q_ref, k_ref, v_ref)):
         tick(3 + n)
         project(n, ref)
+        give("qkv"[n])
 
     def copy(p):
         return remote(send_ref.at[p], state_ref.at[p], ssem.at[p], rsem.at[p], at.across)
 
-    early = {0: 6, 2: 7, 4: 8}
-    late = {0: 9, 1: 10, 2: 11, 3: 12, 4: 13, 5: 14}
+    def ticks_at(p, plan):
+        for n, t in plan.items():
+            @pl.when(p == n)
+            def _(t=t):
+                tick(t)
 
     @pl.loop(0, pairs)
     def _(p):
         forward_states(p, scale, q_ref, k_ref, v_ref, omx_ref, onehot_ref, strad_ref, stradrow_ref, pq_ref, pk_ref, peak_ref, send_ref)
         copy(p).start()
-        for n, t in early.items():
-            @pl.when(p == n)
-            def _(t=t):
-                tick(t)
+        ticks_at(p, {0: 6, 2: 7, 4: 8})
+
+    give("pq", "pk", "sq")
 
     @pl.loop(0, pairs)
     def _(p):
         copy(p).wait()
         forward_finish(p, scale, v_ref, pq_ref, pk_ref, mask_ref, strad_ref, peak_ref, state_ref, att_ref, den_ref)
-        for n, t in late.items():
-            @pl.when(p == n)
-            def _(t=t):
-                tick(t)
+        attt_ref[p] = att_ref[p].T
+        ticks_at(p, {0: 9, 3: 10})
+
+    give("att", "attt", "den", "fin")
+
+
+    whole = jnp.concatenate([att_ref[p] for p in range(pairs)], axis=1)
+    for j in range(pairs // 2):
+        cols = slice(256 * j, 256 * j + 256)
+        got = mul(whole, sq_ref[3, :, :, :, :, cols].reshape(768, 256))
+        res_ref[:, cols] = got + vector(3, cols) + x_ref[:, cols].astype(f32)
+
+    def centred(value):
+        value = value - jnp.mean(value, axis=1, keepdims=True)
+        inverse = lax.rsqrt(jnp.mean(value * value, axis=1, keepdims=True) + 1e-06)
+        return value * inverse, inverse
+
+    def here(r):
+        return pl.ds(pl.multiple_of(128 * r, 128), 128)
+
+    @pl.loop(0, rows // 128)
+    def _(r):
+        normed, inverse = centred(res_ref[here(r)])
+        inv_ref[here(r)] = inverse
+        norm_ref[here(r)] = normed.astype(bf16)
+        hid_ref[here(r)] = (normed * vector(4) + vector(5)).astype(bf16)
+
+    for j in range(pairs):
+        hidt_ref[128 * j : 128 * j + 128] = hid_ref[:, 128 * j : 128 * j + 128].T
+    give("hidt", "norm")
+
+
+    @pl.loop(0, 4)
+    def _(b):
+        ticks_at(b, {0: 11, 2: 12})
+        for j in range(3):
+            cols = cols_at(768 * b + 256 * j, 256)
+            pre = mul(hid_ref[...], fin_ref[:, :, :, :, cols].reshape(768, 256))
+            bias = jnp.zeros((1, 256), f32)
+            for n in range(4):
+                bias = jnp.where(b == n, vector(9 + n, slice(256 * j, 256 * j + 256)), bias)
+            pre = pre + bias
+            share = 0.5 * (1.0 + lax.erf(pre * inv_root_two))
+            gel = (pre * share).astype(bf16)
+            gel_ref[:, cols] = gel
+            gelt_ref[cols] = gel.T
+            slope_ref[:, cols] = (share + pre * (jnp.exp(-0.5 * pre * pre) * inv_root_tau)).astype(bf16)
+
+    give("gelt", "slope")
+
+    def down(h):
+        cols = slice(384 * h, 384 * h + 384)
+        res_ref[:, cols] = hid_ref[:, cols].astype(f32) + vector(6, cols)
+
+        @pl.loop(0, DEPTH)
+        def _(z):
+            got = mul(gel_ref[:, cols_at(768 * z, 768)], fdn_ref[z, :, :, :, cols].reshape(768, 384))
+            res_ref[:, cols] = res_ref[:, cols] + got
+
+    down(0)
+    tick(13)
+    tick(14)
+    give("fdn")
+    down(1)
+
+
+    @pl.loop(0, rows // 128)
+    def _(r):
+        normed, inverse = centred(res_ref[here(r)])
+        layer_ref[here(r)] = (normed * vector(7) + vector(8)).astype(bf16)
+        grad = cot_ref[here(r)].astype(f32)
+        scaled = grad * vector(7)
+        centre = jnp.mean(scaled, axis=1, keepdims=True)
+        lean = jnp.mean(scaled * normed, axis=1, keepdims=True)
+        resid = inverse * (scaled - centre - normed * lean)
+        res_ref[here(r)] = resid
+        sums_ref[6:7] = sums_ref[6:7] + jnp.sum(resid.astype(bf16).astype(f32), axis=0, keepdims=True)
+        sums_ref[7:8] = sums_ref[7:8] + jnp.sum(grad * normed, axis=0, keepdims=True)
+        sums_ref[8:9] = sums_ref[8:9] + jnp.sum(grad, axis=0, keepdims=True)
 
     for b in blocks:
         b.drain()
     vec.drain()
+    for one in stash(*HOLD):
+        one.wait()
 
 
 class Scatter:
@@ -644,18 +753,20 @@
 
 
 def backward_kernel(
-    scale, x_ref, q_ref, k_ref, v_ref, pq_ref, pk_ref, att_ref, den_ref, peak_ref, state_ref, omx_ref, hid_ref, norm_ref,
-    inv_ref, res_ref, gain_ref, vecin_ref, len_ref, gel_ref, slope_ref, win_ref, wdn_ref, sq_ref,
-    gx_ref, oq_ref, ok_ref, ov_ref, oo_ref, oin_ref, odn_ref, vec_ref,
-    gstate_ref, mask_ref, onehot_ref, strad_ref, stradrow_ref, send_ref,
-    xt_ref, gq_ref, gk_ref, gv_ref, gatt_ref, low_ref, wide_ref, gelbuf_ref, slopebuf_ref,
-    gdn_ref, gin_ref, go_ref, gw_ref, total_ref, land_ref,
-    twin_ref, done_ref, donein_ref,
-    ssem, rsem, load_sem, late_sem, ws_sem, wr_sem, vs_sem, vr_sem, *land_refs,
+    scale, peak_ref, state_ref, hidt_ref, norm_ref, inv_ref, res_ref, gain_ref, vecin_ref, gel_ref, slope_ref, win_ref, wdn_ref,
+    sq_ref, *rest,
 ):
+    late_refs, rest = rest[: len(LATE)], rest[len(LATE) :]
+    gx_ref, oq_ref, ok_ref, ov_ref, oo_ref, oin_ref, odn_ref, vec_ref = rest[:8]
+    kept_refs, rest = rest[8 : 8 + len(LATE)], rest[8 + len(LATE) :]
+    xt_ref, q_ref, k_ref, v_ref, pq_ref, pk_ref, att_ref, attt_ref, den_ref, omx_ref, mask_ref, strad_ref = kept_refs
+    gstate_ref, send_ref, gq_ref, gk_ref, gv_ref, gatt_ref, low_ref, wide_ref, gelbuf_ref, slopebuf_ref = rest[:10]
+    gdn_ref, gin_ref, go_ref, gw_ref, total_ref, land_ref, twin_ref, done_ref, donein_ref = rest[10:19]
+    ssem, rsem, load_sem, late_sem, keep_sem, ws_sem, wr_sem, vs_sem, vr_sem = rest[19:28]
+    land_refs = rest[28:]
     at = Place()
     pairs = q_ref.shape[0]
-    rows, width = x_ref.shape
+    rows, width = res_ref.shape
     span = width // 2
     chunks = win_ref.shape[1] // span
     sources = [lambda c, b=b: gdn_ref.at[:, :, c, pl.ds(48 * b, 48)] for b in range(4)]
@@ -695,7 +806,7 @@
         return lax.rem(m, 2)
 
     def load_gelu(m):
-        return load(gel_ref.at[:, cols_at(span * m, span)], gelbuf_ref.at[slot(m)], load_sem.at[0, slot(m)])
+        return load(gel_ref.at[pl.ds(pl.multiple_of(span * m, 128), span)], gelbuf_ref.at[slot(m)], load_sem.at[0, slot(m)])
 
     def load_chunk(m):
         start = pl.multiple_of(span * slot(m), 128)
@@ -713,6 +824,9 @@
     for one in load_chunk(jnp.int32(0)):
         one.start()
     load_square(3, 2).start()
+    kept = [load(src, dst, keep_sem.at[n]) for n, (src, dst) in enumerate(zip(late_refs, kept_refs))]
+    for one in kept:
+        one.start()
     total_ref[0] = vecin_ref[...]
 
     @pl.loop(0, rows // 128)
@@ -730,7 +844,7 @@
         def _():
             load_gelu(m + 1).start()
 
-        turned = gelbuf_ref[slot(m)].T
+        turned = gelbuf_ref[slot(m)]
         for n in range(3):
             cols = slice(256 * n, 256 * n + 256)
             got = mul(turned, low_ref[:, cols]).astype(bf16)
@@ -738,9 +852,6 @@
 
     units[0].begin()
     units[1].begin()
-    for j in range(pairs):
-        xt_ref[128 * j : 128 * j + 128] = hid_ref[:, 128 * j : 128 * j + 128].T
-
     @pl.loop(0, chunks)
     def _(m):
         for one in load_chunk(m):
@@ -755,7 +866,7 @@
         gpre = mul_tb(low_ref[...], wide_ref[0, pl.ds(start, span)]) * slopebuf_ref[slot(m)].astype(f32)
         gpre = gpre.astype(bf16)
         total_ref[0, pl.ds(9 + lax.div(m, 2), 1), cols_at(start, span)] = jnp.sum(gpre.astype(f32), axis=0, keepdims=True)
-        got = mul(xt_ref[...], gpre).astype(bf16)
+        got = mul(hidt_ref[...], gpre).astype(bf16)
         gin_ref[:, :, :, :, cols_at(span * m, span)] = got.reshape(DEPTH, 2, 2, 48, span)
         for n in range(3):
             cols = slice(256 * n, 256 * n + 256)
@@ -777,7 +888,7 @@
         here = pl.ds(pl.multiple_of(128 * r, 128), 128)
         grad = gx_ref[here]
         normed = norm_ref[here].astype(f32)
-        scaled = grad * gain_ref[...]
+        scaled = grad * gain_ref[4:5].astype(f32)
         centre = jnp.mean(scaled, axis=1, keepdims=True)
         slope = jnp.mean(scaled * normed, axis=1, keepdims=True)
         resid = inv_ref[here] * (scaled - centre - normed * slope)
@@ -789,8 +900,10 @@
         total_ref[0, 5:6] = total_ref[0, 5:6] + jnp.sum(grad, axis=0, keepdims=True)
 
     load_square(3, 2).wait()
+    for one in kept:
+        one.wait()
     for h in range(2):
-        turned = jnp.concatenate([att_ref[3 * h + i].T for i in range(3)], axis=0)
+        turned = attt_ref[3 * h : 3 * h + 3].reshape(384, rows)
         for n in range(3):
             cols = slice(256 * n, 256 * n + 256)
             go_ref[2 * h : 2 * h + 2, :, :, :, cols] = mul(turned, low_ref[:, cols]).astype(bf16).reshape(2, 2, 2, 48, 256)
@@ -805,8 +918,6 @@
     done_steps += 1
 
 
-    doc_setup(len_ref, at.y, mask_ref, onehot_ref, strad_ref, stradrow_ref)
-
     def copy(p):
         return remote(send_ref.at[p], gstate_ref.at[p], ssem.at[p], rsem.at[p], at.across)
 
@@ -814,9 +925,6 @@
     def _(p):
         backward_states(p, scale, att_ref, den_ref, gatt_ref, pq_ref, strad_ref, peak_ref, state_ref, send_ref)
         copy(p).start()
-
-    for j in range(pairs):
-        xt_ref[128 * j : 128 * j + 128] = x_ref[:, 128 * j : 128 * j + 128].T
 
     @pl.loop(0, pairs)
     def _(p):
@@ -889,7 +997,7 @@
     return pl.BlockSpec(memory_space=pltpu.SMEM)
 
 
-def attention_forward(x, weights, vectors, ints, lengths):
+def attention_forward(x, weights, vectors, ints, cot, lengths):
     rows, width = x.shape
     heads, size, feats = ints.shape
     pairs = heads // 2
@@ -899,36 +1007,48 @@
     shape = jax.ShapeDtypeStruct
     grid = (DEPTH, 2, 2)
     dma = pltpu.SemaphoreType.DMA
-    return pl.pallas_call(
+    pair, phi, full, tall = (pairs, rows, 128), (pairs, 2, rows, feats), (rows, width), (rows, hidden)
+    held = {
+        "omx": (heads, 256, feats), "xt": (width, rows), "mask": (rows, rows), "strad": (rows, 128), "q": pair, "k": pair, "v": pair, "pq": phi, "pk": phi, "att": pair,
+        "attt": (pairs, 128, rows), "den": pair, "sq": (4, *grid, part, width), "hidt": (width, rows), "norm": full,
+        "fin": (*grid, part, hidden), "gelt": (hidden, rows), "slope": tall,
+        "fdn": (*grid, weights[5].shape[0], width),
+    }
+    kind = {name: f32 if name in ("den", "strad") else bf16 for name in HOLD}
+    layer, peak, state, inverse, resid, vec, sums, *rest = pl.pallas_call(
         partial(forward_kernel, scale),
         out_shape=[
-            shape((pairs, rows, 128), bf16), shape((pairs, rows, 128), bf16), shape((pairs, rows, 128), bf16),
-            shape((pairs, 2, rows, feats), bf16), shape((pairs, 2, rows, feats), bf16),
-            shape((pairs, rows, 128), bf16), shape((pairs, rows, 128), f32),
-            shape((pairs, 2, 1, feats), f32), shape((pairs, 128 + TAIL, feats), bf16), shape((heads, 256, feats), bf16),
-            shape((4, *grid, part, width), bf16),
-            shape((*grid, part, hidden), bf16), shape((*grid, weights[5].shape[0], width), bf16),
-            shape((16, width), bf16),
-        ],
-        in_specs=[vmem()] * 18 + [smem()],
-        out_specs=[vmem()] * 11 + [anywhere()] * 2 + [vmem()],
-        scratch_shapes=scratch_masks(rows, heads, feats)[1:] + [
+            shape(full, bf16), shape((pairs, 2, 1, feats), f32), shape((pairs, 128 + TAIL, feats), bf16),
+            shape((rows, 1), f32), shape(full, f32), shape((16, width), bf16), shape((16, width), f32),
+        ] + [shape(held[name], kind[name]) for name in HOLD],
+        in_specs=[vmem()] * 19 + [smem()],
+        out_specs=[vmem()] * 7 + [anywhere()] * len(HOLD),
+        scratch_shapes=[pltpu.VMEM(held[name], kind[name]) for name in HOLD] + [
+            pltpu.VMEM(full, bf16), pltpu.VMEM(tall, bf16),
+            pltpu.VMEM((rows, 128), f32), pltpu.VMEM((TAIL, rows), bf16),
             pltpu.VMEM((pairs, 128 + TAIL, feats), bf16),
             pltpu.VMEM((4, 16, width), bf16),
             pltpu.VMEM((DEPTH + 1, 16, width), bf16),
             dma((pairs,)), dma((pairs,)),
             dma((12, GATHER_COPIES)), dma((12, GATHER_COPIES)), dma((12,)),
-            dma((DEPTH + 1,)), dma((DEPTH + 1,)),
+            dma((DEPTH + 1,)), dma((DEPTH + 1,)), dma((len(HOLD),)),
         ],
-        compiler_params=pltpu.CompilerParams(collective_id=0, has_side_effects=True, vmem_limit_bytes=60 << 20),
+        compiler_params=pltpu.CompilerParams(collective_id=0, has_side_effects=True, vmem_limit_bytes=65200 << 10),
         name="attention_forward",
-    )(x, *weights, *vectors, ints, lengths)
-
-
-def attention_backward(x, saved, hidden_low, normed, inverse, grad_resid, gain, vec, lengths, gelu_low, slope, win, wdn, square):
-    rows, width = x.shape
-    pairs, _, _, feats = saved[3].shape
-    heads, hidden = 2 * pairs, win.shape[1]
+    )(x, *weights, *vectors, ints, cot, lengths)
+    got = dict(zip(HOLD, rest))
+    inner = (peak, state, got["hidt"], got["norm"], inverse, resid, vec, sums)
+    late = (
+        got["gelt"], got["slope"], got["fin"].reshape(width, hidden), got["fdn"].reshape(hidden, width),
+        got["sq"].reshape(4, width, width), *(got[name] for name in LATE),
+    )
+    return layer, inner, late
+
+
+def attention_backward(inner, late):
+    rows, width = inner[5].shape
+    pairs, _, _, feats = inner[0].shape
+    heads, hidden = 2 * pairs, late[0].shape[0]
     scale = (width // heads) ** (-0.25) * unit_spread
     shape = jax.ShapeDtypeStruct
     dma = pltpu.SemaphoreType.DMA
@@ -940,16 +1060,15 @@
         out_shape=[shape((rows, width), f32)]
         + [shape((part, width), f32)] * 4
         + [shape((part, hidden), f32), shape((hidden // 16, width), f32), shape((16, width), f32)],
-        in_specs=[vmem()] * 17 + [smem()] + [anywhere()] * 5,
+        in_specs=[vmem()] * 8 + [anywhere()] * (5 + len(LATE)),
         out_specs=[vmem()] * 8,
-        scratch_shapes=[pltpu.VMEM((pairs, 128 + TAIL, feats), bf16)] + scratch_masks(rows, heads, feats)[1:] + [
-            pltpu.VMEM((pairs, 128 + TAIL, feats), bf16),
-            pltpu.VMEM((width, rows), bf16),
+        scratch_shapes=[pltpu.VMEM(one.shape, one.dtype) for one in late[5:]] + [
+            pltpu.VMEM((pairs, 128 + TAIL, feats), bf16), pltpu.VMEM((pairs, 128 + TAIL, feats), bf16),
             pltpu.VMEM((pairs, rows, 128), bf16), pltpu.VMEM((pairs, rows, 128), bf16), pltpu.VMEM((pairs, rows, 128), bf16),
             pltpu.VMEM((pairs, rows, 128), bf16),
             pltpu.VMEM((rows, width), bf16),
             pltpu.VMEM((3, width, width), bf16),
-            pltpu.VMEM((2, rows, width // 2), bf16), pltpu.VMEM((2, rows, width // 2), bf16),
+            pltpu.VMEM((2, width // 2, rows), bf16), pltpu.VMEM((2, rows, width // 2), bf16),
             pltpu.VMEM((*grid, hidden // 16, width), bf16),
             pltpu.VMEM((*grid, part, hidden), bf16),
             pltpu.VMEM((*grid, part, width), bf16),
@@ -959,15 +1078,50 @@
             pltpu.VMEM((units, DEPTH, 2, part, width), bf16),
             pltpu.VMEM((units, part, width // 2), bf16),
             pltpu.VMEM((units, part, width // 2), bf16),
-            dma((pairs,)), dma((pairs,)), dma((4, 2)), dma((3,)),
+            dma((pairs,)), dma((pairs,)), dma((4, 2)), dma((3,)), dma((len(LATE),)),
             dma((units, SCATTER_COPIES)), dma((units, SCATTER_COPIES)),
             dma((DEPTH + 2,)), dma((DEPTH + 2,)),
         ] + [land for order in ORDERS for land in landing(order, part, width)],
         compiler_params=pltpu.CompilerParams(collective_id=1, has_side_effects=True, vmem_limit_bytes=65200 << 10),
         name="attention_backward",
-    )(
-        x, *saved, hidden_low, normed, inverse, grad_resid, gain, vec, lengths, gelu_low, slope, win, wdn, square
-    )
+    )(*inner, *late)
+
+
+def finish_kernel(sums_ref, *refs):
+    big = BIG
+    ins, outs, vectors, sem = refs[:big], refs[big : 2 * big], refs[2 * big : -1], refs[-1]
+    copies = [pltpu.make_async_copy(src, dst, sem.at[n]) for n, (src, dst) in enumerate(zip(ins, outs))]
+    for one in copies:
+        one.start()
+    me = lax.axis_index("fsdp")
+    part, wide = vectors[0].shape[1], vectors[9].shape[1]
+    width = sums_ref.shape[1]
+    sums = sums_ref[...]
+    turned = pltpu.roll(sums, lax.rem(width - part * me, width), 1)
+    for n in range(9):
+        vectors[n][...] = turned[n : n + 1, 0:part]
+    inner = pltpu.roll(sums, lax.rem(width - wide * lax.rem(me, 4), width), 1)
+    row = jnp.zeros((1, width), f32)
+    for n in range(DEPTH):
+        row = jnp.where(lax.div(me, 4) == n, inner[9 + n : 10 + n], row)
+    vectors[9][...] = row[:, 0:wide]
+    for one in copies:
+        one.wait()
+
+
+BIG = 8
+
+
+def finish(arrays, sums, part, wide):
+    shape = jax.ShapeDtypeStruct
+    return pl.pallas_call(
+        finish_kernel,
+        out_shape=[shape(a.shape, a.dtype) for a in arrays] + [shape((1, part), f32)] * 9 + [shape((1, wide), f32)],
+        in_specs=[vmem()] + [anywhere()] * BIG,
+        out_specs=[vmem()] * (BIG + 10),
+        scratch_shapes=[pltpu.SemaphoreType.DMA((BIG,))],
+        name="finish",
+    )(sums, *arrays)
 
 
 def to_pairs(rows):
@@ -982,49 +1136,19 @@
     tokens, doc_lengths, feature_ints, w_query, b_query, w_key, b_key, w_value, b_value, w_out, b_out,
     norm1_gain, norm1_bias, w_in, b_in, w_down, b_down, norm2_gain, norm2_bias, cotangent,
 ):
-    row_block = tokens[0]
-    width = row_block.shape[1]
-    me = lax.axis_index("fsdp")
-    *saved, square, in_weight, down_weight, vec = attention_forward(
-        row_block,
+    layer_out, inner, late = attention_forward(
+        tokens[0],
         (w_query, w_key, w_value, w_out, w_in, w_down),
         (b_query, b_key, b_value, b_out, norm1_gain, norm1_bias, b_down, norm2_gain, norm2_bias, b_in),
-        feature_ints, doc_lengths,
+        feature_ints, cotangent[0], doc_lengths,
     )
-    in_weight = in_weight.reshape(width, -1)
-    down_weight = down_weight.reshape(-1, width)
-    square = square.reshape(4, width, width)
-    out_weight = square[3]
-    _, _, _, out_bias, gain_one, offset_one, down_bias, gain_two, offset_two = (vec[i] for i in range(9))
-    in_bias = vec[9:13].reshape(-1)
-    att_rows = from_pairs(saved[5])
-    residual_one = row_block.astype(f32) + affine(att_rows, out_weight, out_bias)
-    hidden_wide, normed_one, inverse_one = layer_norm(residual_one, gain_one, offset_one)
-    hidden_low = hidden_wide.astype(bf16)
-    pre_act = affine(hidden_low, in_weight, in_bias)
-    gelu_low = gelu_value(pre_act).astype(bf16)
-    slope_low = gelu_slope(pre_act).astype(bf16)
-    residual_two = hidden_low.astype(f32) + affine(gelu_low, down_weight, down_bias)
-    layer_wide, normed_two, inverse_two = layer_norm(residual_two, gain_two, offset_two)
-    grad_out = cotangent[0].astype(f32)
-    grad_resid_two, grad_gain_two, grad_offset_two = norm_back(grad_out, normed_two, inverse_two, gain_two)
-    grad_down_bias = column_total(grad_resid_two.astype(bf16))
-    nothing = jnp.zeros((6, width), f32)
-    sums = jnp.concatenate(
-        [nothing, jnp.stack([grad_down_bias, grad_gain_two, grad_offset_two]), nothing, nothing[0:1]], axis=0
-    )
-    grad_input, gq, gk, gv, go, gin, gdn, sums = attention_backward(
-        row_block, saved, hidden_low, normed_one.astype(bf16), inverse_one, grad_resid_two, gain_one.astype(f32)[None],
-        sums, doc_lengths, gelu_low, slope_low, in_weight, down_weight, square,
-    )
-    part = b_query.shape[0]
-    wide = b_in.shape[0]
-    mine = lax.dynamic_slice(sums, (0, me * part), (9, part))
-    mine_in = lax.dynamic_slice(sums[9:13].reshape(-1), (me * wide,), (wide,))
+    *grads, sums = attention_backward(inner, late)
+    done = finish((layer_out, *grads), sums, b_query.shape[0], b_in.shape[0])
+    layer_out, grad_input, gq, gk, gv, go, gin, gdn = done[:BIG]
+    bq, bk, bv, bo, g1, o1, bd, g2, o2, bi = (one.reshape(-1) for one in done[BIG:])
     return (
-        layer_wide.astype(bf16)[None],
-        grad_input[None],
-        gq, mine[0], gk, mine[1], gv, mine[2], go, mine[3], mine[4], mine[5], gin, mine_in, gdn, mine[6], mine[7], mine[8],
+        layer_out[None], grad_input[None],
+        gq, bq, gk, bk, gv, bv, go, bo, g1, o1, gin, bi, gdn, bd, g2, o2,
     )
 
 

time: 244 us -> 217 us (0.89)
  local copies, waits for them, and re-layouts: 16 us -> 0 us
  matrix products: 10 us -> 0 us
  Pallas kernels: 208 us -> 216 us
  other arithmetic: 7.85 us -> 0 us
    dot_general x3 -> x0, matrix products: 10 us -> none  [mul(): lax.dot_general(a, b, (((1,), (0,)), ((), ())), preferred_element_type=f32)]
    unnamed x35 -> x0, local copies, waits for them, and re-layouts: 7.88 us -> none
    pallas_call x1 -> x2, Pallas kernels: 89.4 us -> 96.8 us  [the longest x1 91.7 us: attention_forward(): pl.pallas_call(partial(forward_kernel, scale), out_shape=[shape(full, bf1...]
    reduce_sum x5 -> x0, other arithmetic: 3.63 us -> none  [the longest x1 2.07 us: column_total(): return jnp.sum(values, axis=0, dtype=f32)]
    convert_element_type x3 -> x0, other arithmetic: 3.24 us -> none  [the longest x1 1.29 us: layer_norm(): norm_gain.astype(f32)]
where the time goes in v4:
time: 217 us
  Pallas kernels  216 us (100%)
    pallas_call x1, Pallas kernels, attention_backward(): pl.pallas_call(partial(backward_kernel, scale), out_shape=[shape((rows, w...  119 us
    pallas_call x1, Pallas kernels, attention_forward(): pl.pallas_call(partial(forward_kernel, scale), out_shape=[shape(full, bf1...  91.7 us
    pallas_call x1, Pallas kernels, finish(): pl.pallas_call(finish_kernel, out_shape=[shape(a.shape, a.dtype) for a in...  5.03 us

profile of v4, /device:TPU:0, one launch (start us, length us, event | category | flops | bytes accessed | tf_op | source)
XLA Modules:
  0.0 216.9 jit_solution(15042455269478205322)
XLA Ops:
  0.7 91.7 %attention_forward.1 = (bf16[512,768]{1,0:T(8,128)(2,1)}, f32[6,2,1,256]{3,2,1,0:T(1,128)}, bf16[6,144,256]{2,1,0:T(8,128)(2,1)}, f32[512,1]{1,0:T(8,128)}, f32[...) custom-call(bf16[512,768]{1,0:T(8,128)(2,1)} %bitcast.20, ...), custom_call_target="tpu_custom_call" | custom-call | tf_op jit(solution)/shard_map/attention_forward/pallas_call | solution.py:1018
  92.4 119.3 %attention_backward.1 = (f32[512,768]{1,0:T(8,128)}, f32[48,768]{1,0:T(8,128)}, f32[48,768]{1,0:T(8,128)}, f32[48,768]{1,0:T(8,128)}, f32[48,768]{1,0:T(8,128)},...) custom-call(f32[6,2,1,256]{3,2,1,0:T(1,128)} %get-tuple-element.70.peak_ref, ...), custom_call_target="tpu_custom_call" | custom-call | tf_op jit(solution)/shard_map/attention_backward/pallas_call | solution.py:1058
  211.8 5.0 %finish.1 = (bf16[512,768]{1,0:T(8,128)(2,1)}, f32[512,768]{1,0:T(8,128)}, f32[48,768]{1,0:T(8,128)}, f32[48,768]{1,0:T(8,128)}, f32[48,768]{1,0:T(8,128)}, /*in...) custom-call(f32[16,768]{1,0:T(8,128)} %get-tuple-element.95.sums_ref, ...), custom_call_target="tpu_custom_call" | custom-call | tf_op jit(solution)/shard_map/finish/pallas_call | solution.py:1117

commit v5 on v4

--- a/solution.py
+++ b/solution.py
@@ -746,10 +746,12 @@
 
 
 SCATTER_COPIES = DEPTH + 3
+GELU_SLOTS = 4
+FEED_SLOTS = 3
 FEED_STEPS = (3, 7)
 HEAD_STEPS = (0, 1, 2, 3, 4, 5)
 PACE = ((0, 2, 4, 6, 8),) * 6 + ((0, 2, 3, 4, 5),) * 3 + ((0, 1, 2, 3, 4),) * 3
-ORDERS = ("xyz", "yxz") * 6
+ORDERS = ("yxz", "xyz", "xyz") * 4
 
 
 def backward_kernel(
@@ -760,10 +762,10 @@
     gx_ref, oq_ref, ok_ref, ov_ref, oo_ref, oin_ref, odn_ref, vec_ref = rest[:8]
     kept_refs, rest = rest[8 : 8 + len(LATE)], rest[8 + len(LATE) :]
     xt_ref, q_ref, k_ref, v_ref, pq_ref, pk_ref, att_ref, attt_ref, den_ref, omx_ref, mask_ref, strad_ref = kept_refs
-    gstate_ref, send_ref, gq_ref, gk_ref, gv_ref, gatt_ref, low_ref, wide_ref, gelbuf_ref, slopebuf_ref = rest[:10]
-    gdn_ref, gin_ref, go_ref, gw_ref, total_ref, land_ref, twin_ref, done_ref, donein_ref = rest[10:19]
-    ssem, rsem, load_sem, late_sem, keep_sem, ws_sem, wr_sem, vs_sem, vr_sem = rest[19:28]
-    land_refs = rest[28:]
+    gstate_ref, send_ref, gq_ref, gk_ref, gv_ref, gatt_ref, low_ref, wide_ref, gelbuf_ref, slopebuf_ref, winbuf_ref = rest[:11]
+    gdn_ref, gin_ref, go_ref, gw_ref, total_ref, land_ref, twin_ref, done_ref, donein_ref = rest[11:20]
+    ssem, rsem, load_sem, late_sem, keep_sem, ws_sem, wr_sem, vs_sem, vr_sem = rest[20:29]
+    land_refs = rest[29:]
     at = Place()
     pairs = q_ref.shape[0]
     rows, width = res_ref.shape
@@ -802,53 +804,66 @@
     def load(src, dst, sem):
         return pltpu.make_async_copy(src, dst, sem)
 
+    def gelu_at(m):
+        return lax.rem(m, GELU_SLOTS)
+
+    def load_gelu(m):
+        return load(
+            gel_ref.at[pl.ds(pl.multiple_of(span * m, 128), span)], gelbuf_ref.at[gelu_at(m)], load_sem.at[0, gelu_at(m)]
+        )
+
     def slot(m):
-        return lax.rem(m, 2)
-
-    def load_gelu(m):
-        return load(gel_ref.at[pl.ds(pl.multiple_of(span * m, 128), span)], gelbuf_ref.at[slot(m)], load_sem.at[0, slot(m)])
+        return lax.rem(m, FEED_SLOTS)
+
+    def down_at(m):
+        n = slot(m)
+        return 2 * lax.div(n, 2), pl.ds(pl.multiple_of(span * lax.rem(n, 2), 128), span)
 
     def load_chunk(m):
-        start = pl.multiple_of(span * slot(m), 128)
         return [
             load(slope_ref.at[:, cols_at(span * m, span)], slopebuf_ref.at[slot(m)], load_sem.at[1, slot(m)]),
-            load(wdn_ref.at[pl.ds(pl.multiple_of(span * m, 128), span)], wide_ref.at[0, pl.ds(start, span)], load_sem.at[2, slot(m)]),
-            load(win_ref.at[:, cols_at(span * m, span)], wide_ref.at[1, :, pl.ds(start, span)], load_sem.at[3, slot(m)]),
+            load(wdn_ref.at[pl.ds(pl.multiple_of(span * m, 128), span)], wide_ref.at[down_at(m)], load_sem.at[2, slot(m)]),
+            load(win_ref.at[:, cols_at(span * m, span)], winbuf_ref.at[slot(m)], load_sem.at[3, slot(m)]),
         ]
 
     def load_square(n, to):
         return load(sq_ref.at[n], wide_ref.at[to], late_sem.at[to])
 
     peer_barrier(at.peers())
-    load_gelu(jnp.int32(0)).start()
-    for one in load_chunk(jnp.int32(0)):
-        one.start()
-    load_square(3, 2).start()
+    first = load(res_ref, gx_ref, late_sem.at[0])
+    first.start()
+    for m in range(GELU_SLOTS - 1):
+        load_gelu(jnp.int32(m)).start()
+    for m in range(FEED_SLOTS - 1):
+        for one in load_chunk(jnp.int32(m)):
+            one.start()
+    load_square(3, 1).start()
     kept = [load(src, dst, keep_sem.at[n]) for n, (src, dst) in enumerate(zip(late_refs, kept_refs))]
     for one in kept:
         one.start()
     total_ref[0] = vecin_ref[...]
 
+    first.wait()
+
     @pl.loop(0, rows // 128)
     def _(r):
         here = pl.ds(pl.multiple_of(128 * r, 128), 128)
-        low_ref[here] = res_ref[here].astype(bf16)
-        gx_ref[here] = res_ref[here]
+        low_ref[here] = gx_ref[here].astype(bf16)
 
 
     @pl.loop(0, chunks)
     def _(m):
         load_gelu(m).wait()
 
-        @pl.when(m < chunks - 1)
+        @pl.when(m < chunks - (GELU_SLOTS - 1))
         def _():
-            load_gelu(m + 1).start()
-
-        turned = gelbuf_ref[slot(m)]
+            load_gelu(m + GELU_SLOTS - 1).start()
+
+        turned = gelbuf_ref[gelu_at(m)]
         for n in range(3):
             cols = slice(256 * n, 256 * n + 256)
             got = mul(turned, low_ref[:, cols]).astype(bf16)
-            gdn_ref[lax.div(m, 2), slot(m), :, :, cols] = got.reshape(2, span // 2, 256)
+            gdn_ref[lax.div(m, 2), lax.rem(m, 2), :, :, cols] = got.reshape(2, span // 2, 256)
 
     units[0].begin()
     units[1].begin()
@@ -857,20 +872,20 @@
         for one in load_chunk(m):
             one.wait()
 
-        @pl.when(m < chunks - 1)
+        @pl.when(m < chunks - (FEED_SLOTS - 1))
         def _():
-            for one in load_chunk(m + 1):
+            for one in load_chunk(m + FEED_SLOTS - 1):
                 one.start()
 
-        start = pl.multiple_of(span * slot(m), 128)
-        gpre = mul_tb(low_ref[...], wide_ref[0, pl.ds(start, span)]) * slopebuf_ref[slot(m)].astype(f32)
+        start = pl.multiple_of(span * lax.rem(m, 2), 128)
+        gpre = mul_tb(low_ref[...], wide_ref[down_at(m)]) * slopebuf_ref[slot(m)].astype(f32)
         gpre = gpre.astype(bf16)
         total_ref[0, pl.ds(9 + lax.div(m, 2), 1), cols_at(start, span)] = jnp.sum(gpre.astype(f32), axis=0, keepdims=True)
         got = mul(hidt_ref[...], gpre).astype(bf16)
         gin_ref[:, :, :, :, cols_at(span * m, span)] = got.reshape(DEPTH, 2, 2, 48, span)
         for n in range(3):
             cols = slice(256 * n, 256 * n + 256)
-            gx_ref[:, cols] = gx_ref[:, cols] + mul_tb(gpre, wide_ref[1, cols, pl.ds(start, span)])
+            gx_ref[:, cols] = gx_ref[:, cols] + mul_tb(gpre, winbuf_ref[slot(m), cols])
         for n in range(8):
             @pl.when(m == n)
             def _(n=n):
@@ -899,7 +914,7 @@
         total_ref[0, 4:5] = total_ref[0, 4:5] + jnp.sum(grad * normed, axis=0, keepdims=True)
         total_ref[0, 5:6] = total_ref[0, 5:6] + jnp.sum(grad, axis=0, keepdims=True)
 
-    load_square(3, 2).wait()
+    load_square(3, 1).wait()
     for one in kept:
         one.wait()
     for h in range(2):
@@ -909,7 +924,7 @@
             go_ref[2 * h : 2 * h + 2, :, :, :, cols] = mul(turned, low_ref[:, cols]).astype(bf16).reshape(2, 2, 2, 48, 256)
     units[8].begin()
     for j in range(pairs // 2):
-        got = mul_tb(low_ref[...], wide_ref[2, 256 * j : 256 * j + 256]).astype(bf16)
+        got = mul_tb(low_ref[...], wide_ref[1, 256 * j : 256 * j + 256]).astype(bf16)
         gatt_ref[2 * j] = got[:, 0:128]
         gatt_ref[2 * j + 1] = got[:, 128:256]
     for n in range(3):
@@ -1060,7 +1075,7 @@
         out_shape=[shape((rows, width), f32)]
         + [shape((part, width), f32)] * 4
         + [shape((part, hidden), f32), shape((hidden // 16, width), f32), shape((16, width), f32)],
-        in_specs=[vmem()] * 8 + [anywhere()] * (5 + len(LATE)),
+        in_specs=[vmem()] * 5 + [anywhere()] + [vmem()] * 2 + [anywhere()] * (5 + len(LATE)),
         out_specs=[vmem()] * 8,
         scratch_shapes=[pltpu.VMEM(one.shape, one.dtype) for one in late[5:]] + [
             pltpu.VMEM((pairs, 128 + TAIL, feats), bf16), pltpu.VMEM((pairs, 128 + TAIL, feats), bf16),
@@ -1068,7 +1083,8 @@
             pltpu.VMEM((pairs, rows, 128), bf16),
             pltpu.VMEM((rows, width), bf16),
             pltpu.VMEM((3, width, width), bf16),
-            pltpu.VMEM((2, width // 2, rows), bf16), pltpu.VMEM((2, rows, width // 2), bf16),
+            pltpu.VMEM((GELU_SLOTS, width // 2, rows), bf16), pltpu.VMEM((FEED_SLOTS, rows, width // 2), bf16),
+            pltpu.VMEM((FEED_SLOTS, width, width // 2), bf16),
             pltpu.VMEM((*grid, hidden // 16, width), bf16),
             pltpu.VMEM((*grid, part, hidden), bf16),
             pltpu.VMEM((*grid, part, width), bf16),
@@ -1078,7 +1094,7 @@
             pltpu.VMEM((units, DEPTH, 2, part, width), bf16),
             pltpu.VMEM((units, part, width // 2), bf16),
             pltpu.VMEM((units, part, width // 2), bf16),
-            dma((pairs,)), dma((pairs,)), dma((4, 2)), dma((3,)), dma((len(LATE),)),
+            dma((pairs,)), dma((pairs,)), dma((4, GELU_SLOTS)), dma((3,)), dma((len(LATE),)),
             dma((units, SCATTER_COPIES)), dma((units, SCATTER_COPIES)),
             dma((DEPTH + 2,)), dma((DEPTH + 2,)),
         ] + [land for order in ORDERS for land in landing(order, part, width)],

time: 217 us -> 213 us (0.982)
  Pallas kernels: 216 us -> 212 us
    pallas_call x1, Pallas kernels: 119 us -> 115 us  [attention_backward(): pl.pallas_call(partial(backward_kernel, scale), out_shape=[shape((rows, w...]
where the time goes in v5:
time: 213 us
  Pallas kernels  212 us (100%)
    pallas_call x1, Pallas kernels, attention_backward(): pl.pallas_call(partial(backward_kernel, scale), out_shape=[shape((rows, w...  115 us
    pallas_call x1, Pallas kernels, attention_forward(): pl.pallas_call(partial(forward_kernel, scale), out_shape=[shape(full, bf1...  91.7 us
    pallas_call x1, Pallas kernels, finish(): pl.pallas_call(finish_kernel, out_shape=[shape(a.shape, a.dtype) for a in...  5.03 us

profile of v5, /device:TPU:0, one launch (start us, length us, event | category | flops | bytes accessed | tf_op | source)
XLA Modules:
  0.0 212.9 jit_solution(11463843055409088790)
XLA Ops:
  0.7 91.7 %attention_forward.1 = (bf16[512,768]{1,0:T(8,128)(2,1)}, f32[6,2,1,256]{3,2,1,0:T(1,128)}, bf16[6,144,256]{2,1,0:T(8,128)(2,1)}, f32[512,1]{1,0:T(8,128)}, f32[...) custom-call(bf16[512,768]{1,0:T(8,128)(2,1)} %bitcast.20, ...), custom_call_target="tpu_custom_call" | custom-call | tf_op jit(solution)/shard_map/attention_forward/pallas_call | solution.py:1033
  92.4 115.3 %attention_backward.1 = (f32[512,768]{1,0:T(8,128)}, f32[48,768]{1,0:T(8,128)}, f32[48,768]{1,0:T(8,128)}, f32[48,768]{1,0:T(8,128)}, f32[48,768]{1,0:T(8,128)},...) custom-call(f32[6,2,1,256]{3,2,1,0:T(1,128)} %get-tuple-element.70.peak_ref, ...), custom_call_target="tpu_custom_call" | custom-call | tf_op jit(solution)/shard_map/attention_backward/pallas_call | solution.py:1073
  207.7 5.0 %finish.1 = (bf16[512,768]{1,0:T(8,128)(2,1)}, f32[512,768]{1,0:T(8,128)}, f32[48,768]{1,0:T(8,128)}, f32[48,768]{1,0:T(8,128)}, f32[48,768]{1,0:T(8,128)}, /*in...) custom-call(f32[16,768]{1,0:T(8,128)} %get-tuple-element.95.sums_ref, ...), custom_call_target="tpu_custom_call" | custom-call | tf_op jit(solution)/shard_map/finish/pallas_call | solution.py:1133

commit v6 on v5

--- a/solution.py
+++ b/solution.py
@@ -748,9 +748,9 @@
 SCATTER_COPIES = DEPTH + 3
 GELU_SLOTS = 4
 FEED_SLOTS = 3
-FEED_STEPS = (3, 7)
+FEED_STEPS = (2, 6)
 HEAD_STEPS = (0, 1, 2, 3, 4, 5)
-PACE = ((0, 2, 4, 6, 8),) * 6 + ((0, 2, 3, 4, 5),) * 3 + ((0, 1, 2, 3, 4),) * 3
+PACE = ((0, 2, 4, 6, 8),) * 8 + ((0, 2, 3, 4, 5),) + ((0, 1, 2, 3, 4),) * 3
 ORDERS = ("yxz", "xyz", "xyz") * 4
 
 
@@ -1105,9 +1105,10 @@
 
 def finish_kernel(sums_ref, *refs):
     big = BIG
-    ins, outs, vectors, sem = refs[:big], refs[big : 2 * big], refs[2 * big : -1], refs[-1]
-    copies = [pltpu.make_async_copy(src, dst, sem.at[n]) for n, (src, dst) in enumerate(zip(ins, outs))]
-    for one in copies:
+    ins, outs, vectors, mids, sem = refs[:big], refs[big : 2 * big], refs[2 * big : -1 - big], refs[-1 - big : -1], refs[-1]
+    taken = [pltpu.make_async_copy(src, dst, sem.at[0, n]) for n, (src, dst) in enumerate(zip(ins, mids))]
+    given = [pltpu.make_async_copy(src, dst, sem.at[1, n]) for n, (src, dst) in enumerate(zip(mids, outs))]
+    for one in taken:
         one.start()
     me = lax.axis_index("fsdp")
     part, wide = vectors[0].shape[1], vectors[9].shape[1]
@@ -1121,8 +1122,11 @@
     for n in range(DEPTH):
         row = jnp.where(lax.div(me, 4) == n, inner[9 + n : 10 + n], row)
     vectors[9][...] = row[:, 0:wide]
-    for one in copies:
+    for one, two in zip(taken, given):
         one.wait()
+        two.start()
+    for two in given:
+        two.wait()
 
 
 BIG = 8
@@ -1134,8 +1138,8 @@
         finish_kernel,
         out_shape=[shape(a.shape, a.dtype) for a in arrays] + [shape((1, part), f32)] * 9 + [shape((1, wide), f32)],
         in_specs=[vmem()] + [anywhere()] * BIG,
-        out_specs=[vmem()] * (BIG + 10),
-        scratch_shapes=[pltpu.SemaphoreType.DMA((BIG,))],
+        out_specs=[anywhere()] * BIG + [vmem()] * 10,
+        scratch_shapes=[pltpu.VMEM(a.shape, a.dtype) for a in arrays] + [pltpu.SemaphoreType.DMA((2, BIG))],
         name="finish",
     )(sums, *arrays)
 

time: 213 us -> 210 us (0.986)
  Pallas kernels: 212 us -> 209 us
    pallas_call x1, Pallas kernels: 115 us -> 112 us  [attention_backward(): pl.pallas_call(partial(backward_kernel, scale), out_shape=[shape((rows, w...]
where the time goes in v6:
time: 210 us
  Pallas kernels  209 us (100%)
    pallas_call x1, Pallas kernels, attention_backward(): pl.pallas_call(partial(backward_kernel, scale), out_shape=[shape((rows, w...  112 us
    pallas_call x1, Pallas kernels, attention_forward(): pl.pallas_call(partial(forward_kernel, scale), out_shape=[shape(full, bf1...  91.7 us
    pallas_call x1, Pallas kernels, finish(): pl.pallas_call(finish_kernel, out_shape=[shape(a.shape, a.dtype) for a in...  4.93 us

profile of v6, /device:TPU:0, one launch (start us, length us, event | category | flops | bytes accessed | tf_op | source)
XLA Modules:
  0.0 209.9 jit_solution(11387745436552918615)
XLA Ops:
  0.7 91.7 %attention_forward.1 = (bf16[512,768]{1,0:T(8,128)(2,1)}, f32[6,2,1,256]{3,2,1,0:T(1,128)}, bf16[6,144,256]{2,1,0:T(8,128)(2,1)}, f32[512,1]{1,0:T(8,128)}, f32[...) custom-call(bf16[512,768]{1,0:T(8,128)(2,1)} %bitcast.20, ...), custom_call_target="tpu_custom_call" | custom-call | tf_op jit(solution)/shard_map/attention_forward/pallas_call | solution.py:1033
  92.4 112.4 %attention_backward.1 = (f32[512,768]{1,0:T(8,128)}, f32[48,768]{1,0:T(8,128)}, f32[48,768]{1,0:T(8,128)}, f32[48,768]{1,0:T(8,128)}, f32[48,768]{1,0:T(8,128)},...) custom-call(f32[6,2,1,256]{3,2,1,0:T(1,128)} %get-tuple-element.70.peak_ref, ...), custom_call_target="tpu_custom_call" | custom-call | tf_op jit(solution)/shard_map/attention_backward/pallas_call | solution.py:1073
  204.8 4.9 %finish.1 = (bf16[512,768]{1,0:T(8,128)(2,1)}, f32[512,768]{1,0:T(8,128)}, f32[48,768]{1,0:T(8,128)}, f32[48,768]{1,0:T(8,128)}, f32[48,768]{1,0:T(8,128)}, /*in...) custom-call(f32[16,768]{1,0:T(8,128)} %get-tuple-element.95.sums_ref, ...), custom_call_target="tpu_custom_call" | custom-call | tf_op jit(solution)/shard_map/finish/pallas_call | solution.py:1137

commit v7 on v6

--- a/solution.py
+++ b/solution.py
@@ -748,7 +748,7 @@
 SCATTER_COPIES = DEPTH + 3
 GELU_SLOTS = 4
 FEED_SLOTS = 3
-FEED_STEPS = (2, 6)
+FEED_STEPS = (1, 5)
 HEAD_STEPS = (0, 1, 2, 3, 4, 5)
 PACE = ((0, 2, 4, 6, 8),) * 8 + ((0, 2, 3, 4, 5),) + ((0, 1, 2, 3, 4),) * 3
 ORDERS = ("yxz", "xyz", "xyz") * 4

time: 210 us -> 210 us (level)
  no operation moved by 1% of the time
where the time goes in v7:
time: 210 us
  Pallas kernels  209 us (100%)
    pallas_call x1, Pallas kernels, attention_backward(): pl.pallas_call(partial(backward_kernel, scale), out_shape=[shape((rows, w...  112 us
    pallas_call x1, Pallas kernels, attention_forward(): pl.pallas_call(partial(forward_kernel, scale), out_shape=[shape(full, bf1...  91.7 us
    pallas_call x1, Pallas kernels, finish(): pl.pallas_call(finish_kernel, out_shape=[shape(a.shape, a.dtype) for a in...  4.93 us

profile of v7, /device:TPU:0, one launch (start us, length us, event | category | flops | bytes accessed | tf_op | source)
XLA Modules:
  0.0 209.7 jit_solution(1608941906224047034)
XLA Ops:
  0.7 91.7 %attention_forward.1 = (bf16[512,768]{1,0:T(8,128)(2,1)}, f32[6,2,1,256]{3,2,1,0:T(1,128)}, bf16[6,144,256]{2,1,0:T(8,128)(2,1)}, f32[512,1]{1,0:T(8,128)}, f32[...) custom-call(bf16[512,768]{1,0:T(8,128)(2,1)} %bitcast.20, ...), custom_call_target="tpu_custom_call" | custom-call | tf_op jit(solution)/shard_map/attention_forward/pallas_call | solution.py:1033
  92.4 112.2 %attention_backward.1 = (f32[512,768]{1,0:T(8,128)}, f32[48,768]{1,0:T(8,128)}, f32[48,768]{1,0:T(8,128)}, f32[48,768]{1,0:T(8,128)}, f32[48,768]{1,0:T(8,128)},...) custom-call(f32[6,2,1,256]{3,2,1,0:T(1,128)} %get-tuple-element.70.peak_ref, ...), custom_call_target="tpu_custom_call" | custom-call | tf_op jit(solution)/shard_map/attention_backward/pallas_call | solution.py:1073
  204.7 4.9 %finish.1 = (bf16[512,768]{1,0:T(8,128)(2,1)}, f32[512,768]{1,0:T(8,128)}, f32[48,768]{1,0:T(8,128)}, f32[48,768]{1,0:T(8,128)}, f32[48,768]{1,0:T(8,128)}, /*in...) custom-call(f32[16,768]{1,0:T(8,128)} %get-tuple-element.95.sums_ref, ...), custom_call_target="tpu_custom_call" | custom-call | tf_op jit(solution)/shard_map/finish/pallas_call | solution.py:1137
